TPU v7x, 32 devices: a whole 2x2x4 slice. The times are simulated.
32 devices in a mesh: groups: 2 (over y), tile: 16 (over z, x, core).
Axes of the slice: x: 2, y: 2, z: 4, core: 2. Of those that a mesh axis runs over, the one named last changes fastest.
Arguments:
- level_map: int32 [16], replicated, may hold values from 0 to 7, as said below
- loc_lat: bfloat16 [256, 256], replicated, may hold values from -0.1875 to 0.1875
- loc_lon: bfloat16 [256, 256], replicated, may hold values from -0.1875 to 0.1875
- ens_perts: bfloat16 [32, 256, 256], P(('groups', 'tile')), parts along dimension 0, may hold values from -4 to 4
- ens_control: float32 [32, 256, 256], P(('groups', 'tile')), parts along dimension 0, may hold values from -6 to 6
- static_control: float32 [16, 256, 256], P('groups', 'tile'), parts along dimension 0, may hold values from -6 to 6
- static_scale: float32 [16, 256, 256], P('groups', 'tile'), parts along dimension 0, may hold values from 0.3 to 1.5
- coefs: float32 [4, 16, 256, 256], P(None, 'groups', 'tile'), parts along dimension 1, may hold values from 0.02 to 0.24
- obs_weight: float32 [3, 16, 256, 256], P(None, 'groups', 'tile'), parts along dimension 1, may hold values from 0.05 to 0.5
- innovation: float32 [3, 16, 256, 256], P(None, 'groups', 'tile'), parts along dimension 1, may hold values from -6 to 6
Outputs:
- ens_final: float32 [32, 256, 256], P(('groups', 'tile')), parts along dimension 0
- static_final: float32 [16, 256, 256], P('groups', 'tile'), parts along dimension 0
There are 2 independent parts, one for each index of `groups`. A program takes and returns all parts, laid end to end along the dimension named above; an argument that names none is the same for every part. Nothing has to cross between parts.
Inputs may be any that keep to these rules, and one draw needn't show every extreme that they name: `level_map`: each of the 8 levels is named by exactly 2 entries.
All inputs are finite; a program needn't handle non-finite values.
Results may differ from a plain program's by a relative error of at most 0.0003.
Values sent between devices are 32-bit elements; how exact they have to be, the bound alone decides.
No kernel may reach another device: no remote copies, remote signals or barrier semaphores. Data moves between devices by JAX's collectives and lax.ppermute only.
A program may use at most 64 MiB of HBM per device.

v0:
```python
import jax
import jax.numpy as jnp
from jax import lax
from jax.sharding import PartitionSpec as P

STEPS = 3


step_size = 0.15


def extended(block, sides, width):
    for axis, dim in sides:
        count = lax.axis_size(axis)
        forward = [(i, i + 1) for i in range(count - 1)]
        backward = [(target, source) for source, target in forward]
        low = lax.ppermute(
            lax.slice_in_dim(block, block.shape[dim] - width, None, axis=dim), axis, forward
        )
        high = lax.ppermute(lax.slice_in_dim(block, 0, width, axis=dim), axis, backward)
        block = jnp.concatenate([low, block, high], axis=dim)
    return block


def forward_step(state, coeffs):
    padded = extended(state, (("tile", 1),), 1)
    north_rows = padded[:, 2:]
    south_rows = padded[:, :-2]
    east_cells = jnp.roll(state, -1, 2)
    west_cells = jnp.roll(state, 1, 2)
    return (
        state
        + coeffs[0] * (north_rows - state)
        + coeffs[1] * (south_rows - state)
        + coeffs[2] * (east_cells - state)
        + coeffs[3] * (west_cells - state)
    )


def adjoint_step(adjoint, coeffs):
    coef_sum = coeffs[0] + coeffs[1] + coeffs[2] + coeffs[3]
    fluxes = jnp.stack([coeffs[0] * adjoint, coeffs[1] * adjoint])
    padded = extended(fluxes, (("tile", 2),), 1)
    north_flux = padded[0][:, :-2]
    south_flux = padded[1][:, 2:]
    return (
        (1.0 - coef_sum) * adjoint
        + north_flux
        + south_flux
        + jnp.roll(coeffs[2] * adjoint, 1, 2)
        + jnp.roll(coeffs[3] * adjoint, -1, 2)
    )


def window_gradient(total_incr, coefs, obs_weight, innovation):
    state = total_incr
    weighted = []
    for section in range(STEPS):
        state = forward_step(state, coefs)
        weighted.append(obs_weight[section] * (state - innovation[section]))
    adjoint = weighted[STEPS - 1]
    for section in range(STEPS - 2, -1, -1):
        adjoint = adjoint_step(adjoint, coefs) + weighted[section]
    return adjoint_step(adjoint, coefs)


def local(
    level_map,
    loc_lat,
    loc_lon,
    ens_perts,
    ens_control,
    static_control,
    static_scale,
    coefs,
    obs_weight,
    innovation,
):
    tile_count = lax.axis_size("tile")
    my_level = level_map[lax.axis_index("tile")]
    levels = static_control.shape[0]
    level_ids = jnp.arange(levels, dtype=jnp.int32)
    level_onehot = (level_map[:, None] == level_ids[None, :]).astype(jnp.float32)
    control = ens_control
    lat_smoothed = jnp.einsum(
        "ij,bjk->bik", loc_lat, control.astype(jnp.bfloat16), preferred_element_type=jnp.float32
    ).astype(jnp.bfloat16)
    member_field = jnp.einsum(
        "bij,kj->bik", lat_smoothed, loc_lon, preferred_element_type=jnp.float32
    )
    partial_value = jnp.sum(ens_perts.astype(jnp.float32) * member_field, axis=0)
    pieces = partial_value.reshape(tile_count, -1, partial_value.shape[1])
    received = lax.all_to_all(pieces, "tile", split_axis=0, concat_axis=0, tiled=True)
    ens_incr = jnp.einsum("dl,dij->lij", level_onehot, received, precision=lax.Precision.HIGHEST)
    total_incr = static_scale * static_control + ens_incr
    gradient = window_gradient(total_incr, coefs, obs_weight, innovation)
    static_control = static_control - step_size * (static_control + static_scale * gradient)
    gathered = lax.all_gather(gradient, "tile", axis=1, tiled=True)
    grad_field = lax.dynamic_index_in_dim(gathered, my_level, 0, keepdims=False)
    weighted_grad = (ens_perts.astype(jnp.float32) * grad_field[None]).astype(jnp.bfloat16)
    adjoint_lat = jnp.einsum(
        "ji,bjk->bik", loc_lat, weighted_grad, preferred_element_type=jnp.float32
    ).astype(jnp.bfloat16)
    member_grad = jnp.einsum(
        "bij,jk->bik", adjoint_lat, loc_lon, preferred_element_type=jnp.float32
    )
    control = control - step_size * (control + member_grad)
    return (control, static_control)


def solution(mesh):
    in_specs = (
        P(),
        P(),
        P(),
        P(("groups", "tile"), None, None),
        P(("groups", "tile"), None, None),
        P("groups", "tile", None),
        P("groups", "tile", None),
        P(None, "groups", "tile", None),
        P(None, "groups", "tile", None),
        P(None, "groups", "tile", None),
    )
    out_specs = (P(("groups", "tile"), None, None), P("groups", "tile", None))
    return jax.shard_map(local, mesh=mesh, in_specs=in_specs, out_specs=out_specs, check_vma=False)
```

profile of v0, /device:TPU:1, one launch (start us, length us, event | category | flops | bytes accessed | tf_op | source)
XLA Modules:
  0.0 129.0 jit_solution(13692890221290343578)
XLA Ops:
  7.2 0.0 all-gather.2.cloned.1.call-start
  7.2 0.8 copy-done
  8.1 1.5 %fusion = f32[1,256,256]{2,1,0:T(8,128)S(1)} fusion(bf16[256,256]{1,0:T(8,128)(2,1)S(1)} %copy-done, bf16[256,256]{1,0:T(8,128)(2,1)} %param.11, bf16[1,256,256]{2,1,0:T(8,128)(2,1)} %param.13, f32[1,256,256]{2,1,0:T(8,128)} %param.14), kind=kOutput, calls=%fused_computation.2 | convolution fusion | flops 67371008 | bytes 917504 | tf_op jit(solution)/shard_map/bij,kj->bik/dot_general | solution.py:88
  9.6 16.6 %all_to_all.5 = f32[16,16,256]{2,1,0:T(8,128)S(1)} all-to-all(f32[16,16,256]{2,1,0:T(8,128)S(1)} %bitcast.156), channel_id=1, replica_groups=mesh['groups'=2,'tile'=16] {'tile'}, dimensions={0} | all-to-all | bytes 524288 | tf_op jit(solution)/shard_map/all_to_all | solution.py:93
  26.2 1.0 fusion.7
  27.2 1.0 copy_add_fusion
  28.3 0.1 fusion.82
  28.4 2.5 %collective-permute-start = (f32[8,1,256]{2,1,0:T(1,128)S(1)}, f32[8,1,256]{2,1,0:T(1,128)S(1)}, u32[]{:S(2)}, u32[]{:S(2)}) collective-permute-start(f32[8,1,256]{2,1,0:T(1,128)S(1)} %get-tuple-element.48), channel_id=1, source_target_pairs={{1,0},{2,1},{3,2},{4,3},{5,4},{6,5},{7,6},{8,7},{9,8},{10,9},{11,1... | collective-permute-start | bytes 24584 | tf_op jit(solution)/shard_map/ppermute | solution.py:20
  30.9 3.2 %collective-permute-start.1 = (f32[8,1,256]{2,1,0:T(1,128)S(1)}, f32[8,1,256]{2,1,0:T(1,128)S(1)}, u32[]{:S(2)}, u32[]{:S(2)}) collective-permute-start(f32[8,1,256]{2,1,0:T(1,128)S(1)} %get-tuple-element.49), channel_id=1, source_target_pairs={{0,1},{1,2},{2,3},{3,4},{4,5},{5,6},{6,7},{7,8},{8,9},{9,10},{10,1... | collective-permute-start | bytes 24584 | tf_op jit(solution)/shard_map/ppermute | solution.py:17
  34.1 0.1 fusion.81
  34.2 0.7 collective-permute-done.1
  34.9 0.1 fusion.42
  35.1 0.1 fusion.79
  35.2 1.9 %collective-permute-start.2 = (f32[8,1,256]{2,1,0:T(1,128)S(1)}, f32[8,1,256]{2,1,0:T(1,128)S(1)}, u32[]{:S(2)}, u32[]{:S(2)}) collective-permute-start(f32[8,1,256]{2,1,0:T(1,128)S(1)} %get-tuple-element.42), channel_id=1, source_target_pairs={{1,0},{2,1},{3,2},{4,3},{5,4},{6,5},{7,6},{8,7},{9,8},{10,9},{11,1... | collective-permute-start | bytes 24584 | tf_op jit(solution)/shard_map/ppermute | solution.py:20
  37.1 4.2 %collective-permute-start.3 = (f32[8,1,256]{2,1,0:T(1,128)S(1)}, f32[8,1,256]{2,1,0:T(1,128)S(1)}, u32[]{:S(2)}, u32[]{:S(2)}) collective-permute-start(f32[8,1,256]{2,1,0:T(1,128)S(1)} %get-tuple-element.43), channel_id=1, source_target_pairs={{0,1},{1,2},{2,3},{3,4},{4,5},{5,6},{6,7},{7,8},{8,9},{9,10},{10,1... | collective-permute-start | bytes 24584 | tf_op jit(solution)/shard_map/ppermute | solution.py:17
  41.3 0.1 fusion.78
  41.4 0.7 collective-permute-done.3
  42.1 0.1 fusion.34
  42.2 0.1 fusion.76
  42.3 1.9 %collective-permute-start.4 = (f32[8,1,256]{2,1,0:T(1,128)S(1)}, f32[8,1,256]{2,1,0:T(1,128)S(1)}, u32[]{:S(2)}, u32[]{:S(2)}) collective-permute-start(f32[8,1,256]{2,1,0:T(1,128)S(1)} %get-tuple-element.32), channel_id=1, source_target_pairs={{1,0},{2,1},{3,2},{4,3},{5,4},{6,5},{7,6},{8,7},{9,8},{10,9},{11,1... | collective-permute-start | bytes 24584 | tf_op jit(solution)/shard_map/ppermute | solution.py:20
  44.2 4.2 %collective-permute-start.5 = (f32[8,1,256]{2,1,0:T(1,128)S(1)}, f32[8,1,256]{2,1,0:T(1,128)S(1)}, u32[]{:S(2)}, u32[]{:S(2)}) collective-permute-start(f32[8,1,256]{2,1,0:T(1,128)S(1)} %get-tuple-element.33), channel_id=1, source_target_pairs={{0,1},{1,2},{2,3},{3,4},{4,5},{5,6},{6,7},{7,8},{8,9},{9,10},{10,1... | collective-permute-start | bytes 24584 | tf_op jit(solution)/shard_map/ppermute | solution.py:17
  48.4 0.1 fusion.77
  48.5 0.7 collective-permute-done.5
  49.2 0.1 bitcast_multiply_fusion.2
  49.4 4.2 %collective-permute-start.6 = (f32[2,8,1,256]{3,2,1,0:T(1,128)S(1)}, f32[2,8,1,256]{3,2,1,0:T(1,128)S(1)}, u32[]{:S(2)}, u32[]{:S(2)}) collective-permute-start(f32[2,8,1,256]{3,2,1,0:T(1,128)S(1)} %get-tuple-element.30), channel_id=1, source_target_pairs={{0,1},{1,2},{2,3},{3,4},{4,5},{5,6},{6,7},{7,8},{8,9},{9,10},{10,1... | collective-permute-start | bytes 49160 | tf_op jit(solution)/shard_map/ppermute | solution.py:17
  53.7 1.9 %collective-permute-start.7 = (f32[2,8,1,256]{3,2,1,0:T(1,128)S(1)}, f32[2,8,1,256]{3,2,1,0:T(1,128)S(1)}, u32[]{:S(2)}, u32[]{:S(2)}) collective-permute-start(f32[2,8,1,256]{3,2,1,0:T(1,128)S(1)} %get-tuple-element.31), channel_id=1, source_target_pairs={{1,0},{2,1},{3,2},{4,3},{5,4},{6,5},{7,6},{8,7},{9,8},{10,9},{11,1... | collective-permute-start | bytes 49160 | tf_op jit(solution)/shard_map/ppermute | solution.py:20
  55.6 0.1 slice.322
  55.7 0.1 slice.320
  55.8 2.9 %collective-permute-done.7 = f32[2,8,1,256]{3,2,1,0:T(1,128)S(1)} collective-permute-done((f32[2,8,1,256]{3,2,1,0:T(1,128)S(1)}, f32[2,8,1,256]{3,2,1,0:T(1,128)S(1)}, u32[]{:S(2)}, u32[]{:S(2)}) %collective-permute-start.7) | collective-permute-done | bytes 16416 | tf_op jit(solution)/shard_map/ppermute | solution.py:20
  58.7 0.1 pad_maximum_fusion
  58.8 0.2 bitcast_multiply_fusion.1
  59.1 3.7 %collective-permute-start.8 = (f32[2,8,1,256]{3,2,1,0:T(1,128)S(1)}, f32[2,8,1,256]{3,2,1,0:T(1,128)S(1)}, u32[]{:S(2)}, u32[]{:S(2)}) collective-permute-start(f32[2,8,1,256]{3,2,1,0:T(1,128)S(1)} %get-tuple-element.28), channel_id=1, source_target_pairs={{0,1},{1,2},{2,3},{3,4},{4,5},{5,6},{6,7},{7,8},{8,9},{9,10},{10,1... | collective-permute-start | bytes 49160 | tf_op jit(solution)/shard_map/ppermute | solution.py:17
  62.8 1.9 %collective-permute-start.9 = (f32[2,8,1,256]{3,2,1,0:T(1,128)S(1)}, f32[2,8,1,256]{3,2,1,0:T(1,128)S(1)}, u32[]{:S(2)}, u32[]{:S(2)}) collective-permute-start(f32[2,8,1,256]{3,2,1,0:T(1,128)S(1)} %get-tuple-element.29), channel_id=1, source_target_pairs={{1,0},{2,1},{3,2},{4,3},{5,4},{6,5},{7,6},{8,7},{9,8},{10,9},{11,1... | collective-permute-start | bytes 49160 | tf_op jit(solution)/shard_map/ppermute | solution.py:20
  64.8 0.1 slice.330
  64.9 0.1 slice.328
  65.0 4.6 %collective-permute-done.9 = f32[2,8,1,256]{3,2,1,0:T(1,128)S(1)} collective-permute-done((f32[2,8,1,256]{3,2,1,0:T(1,128)S(1)}, f32[2,8,1,256]{3,2,1,0:T(1,128)S(1)}, u32[]{:S(2)}, u32[]{:S(2)}) %collective-permute-start.9) | collective-permute-done | bytes 16416 | tf_op jit(solution)/shard_map/ppermute | solution.py:20
  69.5 0.1 pad_maximum_fusion.1
  69.7 0.2 bitcast_multiply_fusion
  69.9 2.1 %collective-permute-start.10 = (f32[2,8,1,256]{3,2,1,0:T(1,128)S(1)}, f32[2,8,1,256]{3,2,1,0:T(1,128)S(1)}, u32[]{:S(2)}, u32[]{:S(2)}) collective-permute-start(f32[2,8,1,256]{3,2,1,0:T(1,128)S(1)} %get-tuple-element.26), channel_id=1, source_target_pairs={{0,1},{1,2},{2,3},{3,4},{4,5},{5,6},{6,7},{7,8},{8,9},{9,10},{10,1... | collective-permute-start | bytes 49160 | tf_op jit(solution)/shard_map/ppermute | solution.py:17
  72.0 2.4 %collective-permute-start.11 = (f32[2,8,1,256]{3,2,1,0:T(1,128)S(1)}, f32[2,8,1,256]{3,2,1,0:T(1,128)S(1)}, u32[]{:S(2)}, u32[]{:S(2)}) collective-permute-start(f32[2,8,1,256]{3,2,1,0:T(1,128)S(1)} %get-tuple-element.27), channel_id=1, source_target_pairs={{1,0},{2,1},{3,2},{4,3},{5,4},{6,5},{7,6},{8,7},{9,8},{10,9},{11,1... | collective-permute-start | bytes 49160 | tf_op jit(solution)/shard_map/ppermute | solution.py:20
  74.4 0.1 slice.338
  74.5 0.1 slice.336
  74.6 3.4 %collective-permute-done.11 = f32[2,8,1,256]{3,2,1,0:T(1,128)S(1)} collective-permute-done((f32[2,8,1,256]{3,2,1,0:T(1,128)S(1)}, f32[2,8,1,256]{3,2,1,0:T(1,128)S(1)}, u32[]{:S(2)}, u32[]{:S(2)}) %collective-permute-start.11) | collective-permute-done | bytes 16416 | tf_op jit(solution)/shard_map/ppermute | solution.py:20
  78.0 0.1 pad_maximum_fusion.2
  78.1 0.8 multiply_subtract_fusion
  79.0 0.6 dynamic_slice.7
  81.4 38.7 %all-gather.2.cloned.1.call-done = f32[8,256,256]{2,1,0:T(8,128)} async-done(((f32[8,16,256]{2,1,0:T(8,128)}), f32[8,256,256]{2,1,0:T(8,128)}) %all-gather.2.cloned.1.call-update) | async-done | bytes 2097168 | tf_op jit(solution)/shard_map/all_gather | solution.py:98
  120.1 2.1 %fusion.3 = f32[1,256,256]{2,1,0:T(8,128)} fusion(f32[1,256,256]{2,1,0:T(8,128)S(1)} %copy-done.2, bf16[256,256]{1,0:T(8,128)(2,1)S(1)} %copy-done, bf16[256,256]{1,0:T(8,128)(2,1)S(1)} %copy-done.3, f32[8,256,256]{2,1,0:T(8,128)} %all-gather.2.cloned.1.call-done, s32[]{:T(128)S(6)} %select_n.8, bf16[1,256,256]{2,1,0:T(8,128)(2,1)S(1)} %copy-done.4), kind=kOutput, calls=%fused_computation.5 | convolution fusion | flops 67567616 | bytes 1179652 | tf_op jit(solution)/shard_map/bij,jk->bik/dot_general | solution.py:104
  (41 shorter events, 0.4 us)
Async XLA Ops:
  7.2 0.9 copy-start
  7.2 27.7 %copy-start.1 = (f32[4,8,16,256]{3,2,1,0:T(8,128)S(1)}, f32[4,8,16,256]{3,2,1,0:T(8,128)}, u32[]{:S(2)}) copy-start(f32[4,8,16,256]{3,2,1,0:T(8,128)} %param.17) | copy-start | bytes 1572868
  7.2 112.9 %all-gather.2.cloned.1.call-start = ((), (), s32[]{:S(2)}) async-start(), calls=%async_computation.1 | async-start | bytes 2228224 | tf_op jit(solution)/shard_map/all_gather | solution.py:98
  28.4 5.8 %collective-permute-start = (f32[8,1,256]{2,1,0:T(1,128)S(1)}, f32[8,1,256]{2,1,0:T(1,128)S(1)}, u32[]{:S(2)}, u32[]{:S(2)}) collective-permute-start(f32[8,1,256]{2,1,0:T(1,128)S(1)} %get-tuple-element.48), channel_id=1, source_target_pairs={{1,0},{2,1},{3,2},{4,3},{5,4},{6,5},{7,6},{8,7},{9,8},{10,9},{11,1... | collective-permute-start | bytes 24584 | tf_op jit(solution)/shard_map/ppermute | solution.py:20
  30.9 18.3 %copy-start.7 = (f32[3,8,16,256]{3,2,1,0:T(8,128)S(1)}, f32[3,8,16,256]{3,2,1,0:T(8,128)}, u32[]{:S(2)}) copy-start(f32[3,8,16,256]{3,2,1,0:T(8,128)} %param.19) | copy-start | bytes 1179652
  30.9 18.3 %copy-start.8 = (f32[3,8,16,256]{3,2,1,0:T(8,128)S(1)}, f32[3,8,16,256]{3,2,1,0:T(8,128)}, u32[]{:S(2)}) copy-start(f32[3,8,16,256]{3,2,1,0:T(8,128)} %param.18) | copy-start | bytes 1179652
  30.9 4.0 %collective-permute-start.1 = (f32[8,1,256]{2,1,0:T(1,128)S(1)}, f32[8,1,256]{2,1,0:T(1,128)S(1)}, u32[]{:S(2)}, u32[]{:S(2)}) collective-permute-start(f32[8,1,256]{2,1,0:T(1,128)S(1)} %get-tuple-element.49), channel_id=1, source_target_pairs={{0,1},{1,2},{2,3},{3,4},{4,5},{5,6},{6,7},{7,8},{8,9},{9,10},{10,1... | collective-permute-start | bytes 24584 | tf_op jit(solution)/shard_map/ppermute | solution.py:17
  35.2 6.2 %collective-permute-start.2 = (f32[8,1,256]{2,1,0:T(1,128)S(1)}, f32[8,1,256]{2,1,0:T(1,128)S(1)}, u32[]{:S(2)}, u32[]{:S(2)}) collective-permute-start(f32[8,1,256]{2,1,0:T(1,128)S(1)} %get-tuple-element.42), channel_id=1, source_target_pairs={{1,0},{2,1},{3,2},{4,3},{5,4},{6,5},{7,6},{8,7},{9,8},{10,9},{11,1... | collective-permute-start | bytes 24584 | tf_op jit(solution)/shard_map/ppermute | solution.py:20
  37.1 5.0 %collective-permute-start.3 = (f32[8,1,256]{2,1,0:T(1,128)S(1)}, f32[8,1,256]{2,1,0:T(1,128)S(1)}, u32[]{:S(2)}, u32[]{:S(2)}) collective-permute-start(f32[8,1,256]{2,1,0:T(1,128)S(1)} %get-tuple-element.43), channel_id=1, source_target_pairs={{0,1},{1,2},{2,3},{3,4},{4,5},{5,6},{6,7},{7,8},{8,9},{9,10},{10,1... | collective-permute-start | bytes 24584 | tf_op jit(solution)/shard_map/ppermute | solution.py:17
  42.3 6.2 %collective-permute-start.4 = (f32[8,1,256]{2,1,0:T(1,128)S(1)}, f32[8,1,256]{2,1,0:T(1,128)S(1)}, u32[]{:S(2)}, u32[]{:S(2)}) collective-permute-start(f32[8,1,256]{2,1,0:T(1,128)S(1)} %get-tuple-element.32), channel_id=1, source_target_pairs={{1,0},{2,1},{3,2},{4,3},{5,4},{6,5},{7,6},{8,7},{9,8},{10,9},{11,1... | collective-permute-start | bytes 24584 | tf_op jit(solution)/shard_map/ppermute | solution.py:20
  44.2 5.0 %collective-permute-start.5 = (f32[8,1,256]{2,1,0:T(1,128)S(1)}, f32[8,1,256]{2,1,0:T(1,128)S(1)}, u32[]{:S(2)}, u32[]{:S(2)}) collective-permute-start(f32[8,1,256]{2,1,0:T(1,128)S(1)} %get-tuple-element.33), channel_id=1, source_target_pairs={{0,1},{1,2},{2,3},{3,4},{4,5},{5,6},{6,7},{7,8},{8,9},{9,10},{10,1... | collective-permute-start | bytes 24584 | tf_op jit(solution)/shard_map/ppermute | solution.py:17
  49.4 6.4 %collective-permute-start.6 = (f32[2,8,1,256]{3,2,1,0:T(1,128)S(1)}, f32[2,8,1,256]{3,2,1,0:T(1,128)S(1)}, u32[]{:S(2)}, u32[]{:S(2)}) collective-permute-start(f32[2,8,1,256]{3,2,1,0:T(1,128)S(1)} %get-tuple-element.30), channel_id=1, source_target_pairs={{0,1},{1,2},{2,3},{3,4},{4,5},{5,6},{6,7},{7,8},{8,9},{9,10},{10,1... | collective-permute-start | bytes 49160 | tf_op jit(solution)/shard_map/ppermute | solution.py:17
  53.7 5.1 %collective-permute-start.7 = (f32[2,8,1,256]{3,2,1,0:T(1,128)S(1)}, f32[2,8,1,256]{3,2,1,0:T(1,128)S(1)}, u32[]{:S(2)}, u32[]{:S(2)}) collective-permute-start(f32[2,8,1,256]{3,2,1,0:T(1,128)S(1)} %get-tuple-element.31), channel_id=1, source_target_pairs={{1,0},{2,1},{3,2},{4,3},{5,4},{6,5},{7,6},{8,7},{9,8},{10,9},{11,1... | collective-permute-start | bytes 49160 | tf_op jit(solution)/shard_map/ppermute | solution.py:20
  59.1 5.9 %collective-permute-start.8 = (f32[2,8,1,256]{3,2,1,0:T(1,128)S(1)}, f32[2,8,1,256]{3,2,1,0:T(1,128)S(1)}, u32[]{:S(2)}, u32[]{:S(2)}) collective-permute-start(f32[2,8,1,256]{3,2,1,0:T(1,128)S(1)} %get-tuple-element.28), channel_id=1, source_target_pairs={{0,1},{1,2},{2,3},{3,4},{4,5},{5,6},{6,7},{7,8},{8,9},{9,10},{10,1... | collective-permute-start | bytes 49160 | tf_op jit(solution)/shard_map/ppermute | solution.py:17
  62.8 6.7 %collective-permute-start.9 = (f32[2,8,1,256]{3,2,1,0:T(1,128)S(1)}, f32[2,8,1,256]{3,2,1,0:T(1,128)S(1)}, u32[]{:S(2)}, u32[]{:S(2)}) collective-permute-start(f32[2,8,1,256]{3,2,1,0:T(1,128)S(1)} %get-tuple-element.29), channel_id=1, source_target_pairs={{1,0},{2,1},{3,2},{4,3},{5,4},{6,5},{7,6},{8,7},{9,8},{10,9},{11,1... | collective-permute-start | bytes 49160 | tf_op jit(solution)/shard_map/ppermute | solution.py:20
  69.6 8.4 %copy-start.5 = (f32[8,16,256]{2,1,0:T(8,128)S(1)}, f32[8,16,256]{2,1,0:T(8,128)}, u32[]{:S(2)}) copy-start(f32[8,16,256]{2,1,0:T(8,128)} %param.15) | copy-start | bytes 393220
  69.6 8.4 %copy-start.6 = (f32[8,16,256]{2,1,0:T(8,128)S(1)}, f32[8,16,256]{2,1,0:T(8,128)}, u32[]{:S(2)}) copy-start(f32[8,16,256]{2,1,0:T(8,128)} %param.16) | copy-start | bytes 393220
  69.9 9.1 %copy-start.9 = (s32[16]{0:T(128)S(1)}, s32[16]{0:T(128)}, u32[]{:S(2)}) copy-start(s32[16]{0:T(128)} %param.10) | copy-start | bytes 196
  69.9 50.2 %copy-start.2 = (f32[1,256,256]{2,1,0:T(8,128)S(1)}, f32[1,256,256]{2,1,0:T(8,128)}, u32[]{:S(2)}) copy-start(f32[1,256,256]{2,1,0:T(8,128)} %param.14) | copy-start | bytes 786436
  69.9 50.2 %copy-start.3 = (bf16[256,256]{1,0:T(8,128)(2,1)S(1)}, bf16[256,256]{1,0:T(8,128)(2,1)}, u32[]{:S(2)}) copy-start(bf16[256,256]{1,0:T(8,128)(2,1)} %param.11) | copy-start | bytes 393220
  69.9 50.2 %copy-start.4 = (bf16[1,256,256]{2,1,0:T(8,128)(2,1)S(1)}, bf16[1,256,256]{2,1,0:T(8,128)(2,1)}, u32[]{:S(2)}) copy-start(bf16[1,256,256]{2,1,0:T(8,128)(2,1)} %param.13) | copy-start | bytes 393220
  69.9 4.7 %collective-permute-start.10 = (f32[2,8,1,256]{3,2,1,0:T(1,128)S(1)}, f32[2,8,1,256]{3,2,1,0:T(1,128)S(1)}, u32[]{:S(2)}, u32[]{:S(2)}) collective-permute-start(f32[2,8,1,256]{3,2,1,0:T(1,128)S(1)} %get-tuple-element.26), channel_id=1, source_target_pairs={{0,1},{1,2},{2,3},{3,4},{4,5},{5,6},{6,7},{7,8},{8,9},{9,10},{10,1... | collective-permute-start | bytes 49160 | tf_op jit(solution)/shard_map/ppermute | solution.py:17
  72.0 6.0 %collective-permute-start.11 = (f32[2,8,1,256]{3,2,1,0:T(1,128)S(1)}, f32[2,8,1,256]{3,2,1,0:T(1,128)S(1)}, u32[]{:S(2)}, u32[]{:S(2)}) collective-permute-start(f32[2,8,1,256]{3,2,1,0:T(1,128)S(1)} %get-tuple-element.27), channel_id=1, source_target_pairs={{1,0},{2,1},{3,2},{4,3},{5,4},{6,5},{7,6},{8,7},{9,8},{10,9},{11,1... | collective-permute-start | bytes 49160 | tf_op jit(solution)/shard_map/ppermute | solution.py:20
Sparse Core Ops, SparseCore 0:
  79.1 40.9 all-gather.1
where the time goes:
time: 130 us; the launch traced here: 129 us
  waiting for transfers between devices  51.6 us (40%)
  starting transfers between devices  34.2 us (26%)
  blocking collectives  16.6 us (13%)
  between operations  16.3 us (13%)
  matrix products  4.64 us (4%)
  other arithmetic  2.97 us (2%)
  local copies, waits for them, and re-layouts  2.66 us (2%)
    all_gather x1, waiting for transfers between devices, local(): gathered = lax.all_gather(gradient, 'tile', axis=1, tiled=True)  38.7 us
    ppermute x6, starting transfers between devices, extended(): lax.ppermute(lax.slice_in_dim(block, block.shape[dim] - width, None, axis...  21.6 us
    all_to_all x1, blocking collectives, local(): lax.all_to_all(pieces, 'tile', split_axis=0, concat_axis=0, tiled=True)  16.6 us
    ppermute x6, starting transfers between devices, extended(): lax.ppermute(lax.slice_in_dim(block, 0, width, axis=dim), axis, backward)  12.6 us
    ppermute x6, waiting for transfers between devices, extended(): lax.ppermute(lax.slice_in_dim(block, 0, width, axis=dim), axis, backward)  10.9 us
  transfers between devices with their start and end apart: 13, of which 7 were waited for; matrix products, arithmetic and copies ran while one was open for 1% of the time, Pallas kernels for 0%

commit v1 on v0

--- a/solution.py
+++ b/solution.py
@@ -77,7 +77,6 @@
     innovation,
 ):
     tile_count = lax.axis_size("tile")
-    my_level = level_map[lax.axis_index("tile")]
     levels = static_control.shape[0]
     level_ids = jnp.arange(levels, dtype=jnp.int32)
     level_onehot = (level_map[:, None] == level_ids[None, :]).astype(jnp.float32)
@@ -95,8 +94,9 @@
     total_incr = static_scale * static_control + ens_incr
     gradient = window_gradient(total_incr, coefs, obs_weight, innovation)
     static_control = static_control - step_size * (static_control + static_scale * gradient)
-    gathered = lax.all_gather(gradient, "tile", axis=1, tiled=True)
-    grad_field = lax.dynamic_index_in_dim(gathered, my_level, 0, keepdims=False)
+    outgoing = jnp.take(gradient, level_map, axis=0)
+    incoming = lax.all_to_all(outgoing, "tile", split_axis=0, concat_axis=0, tiled=True)
+    grad_field = incoming.reshape(-1, incoming.shape[2])
     weighted_grad = (ens_perts.astype(jnp.float32) * grad_field[None]).astype(jnp.bfloat16)
     adjoint_lat = jnp.einsum(
         "ji,bjk->bik", loc_lat, weighted_grad, preferred_element_type=jnp.float32

time: 130 us -> 91.1 us (0.70)
  waiting for transfers between devices: 51.6 us -> 30 us
  blocking collectives: 16.6 us -> 0 us
  between operations: 16.3 us -> 1.08 us
  starting transfers between devices: 34.2 us -> 45.5 us
  local copies, waits for them, and re-layouts: 2.66 us -> 5.43 us
    all_gather x1 -> x0, waiting for transfers between devices: 38.7 us -> none  [local(): gathered = lax.all_gather(gradient, 'tile', axis=1, tiled=True)]
    all_to_all x0 -> x2, waiting for transfers between devices: none -> 17.1 us  [the longest x1 8.81 us: local(): lax.all_to_all(outgoing, 'tile', split_axis=0, concat_axis=0, tiled=True)]
    all_to_all x1 -> x0, blocking collectives: 16.6 us -> none  [local(): lax.all_to_all(pieces, 'tile', split_axis=0, concat_axis=0, tiled=True)]
    all_to_all x0 -> x2, starting transfers between devices: none -> 11.6 us  [the longest x1 7.31 us: local(): lax.all_to_all(pieces, 'tile', split_axis=0, concat_axis=0, tiled=True)]
    unnamed x20 -> x21, local copies, waits for them, and re-layouts: 0.9 us -> 3.62 us
  transfers between devices with their start and end apart: 13 -> 14, of which waited for: 7 -> 8; matrix products, arithmetic and copies ran while one was open for 1% -> 2% of each run, Pallas kernels for 0% -> 0%
where the time goes in v1:
time: 91.1 us; the launch traced here: 89.8 us
  starting transfers between devices  45.5 us (50%)
  waiting for transfers between devices  30 us (33%)
  local copies, waits for them, and re-layouts  5.43 us (6%)
  other arithmetic  3.97 us (4%)
  matrix products  3.82 us (4%)
  between operations  1.08 us (1%)
    ppermute x6, starting transfers between devices, extended(): lax.ppermute(lax.slice_in_dim(block, block.shape[dim] - width, None, axis...  21.3 us
    ppermute x6, starting transfers between devices, extended(): lax.ppermute(lax.slice_in_dim(block, 0, width, axis=dim), axis, backward)  12.6 us
    ppermute x6, waiting for transfers between devices, extended(): lax.ppermute(lax.slice_in_dim(block, 0, width, axis=dim), axis, backward)  10.8 us
    all_to_all x1, waiting for transfers between devices, local(): lax.all_to_all(outgoing, 'tile', split_axis=0, concat_axis=0, tiled=True)  8.81 us
    all_to_all x1, waiting for transfers between devices, local(): lax.all_to_all(pieces, 'tile', split_axis=0, concat_axis=0, tiled=True)  8.33 us
    all_to_all x1, starting transfers between devices, local(): lax.all_to_all(pieces, 'tile', split_axis=0, concat_axis=0, tiled=True)  7.31 us
    all_to_all x1, starting transfers between devices, local(): lax.all_to_all(outgoing, 'tile', split_axis=0, concat_axis=0, tiled=True)  4.3 us
    unnamed x21, local copies, waits for them, and re-layouts  3.62 us
  transfers between devices with their start and end apart: 14, of which 8 were waited for; matrix products, arithmetic and copies ran while one was open for 2% of the time, Pallas kernels for 0%

profile of v1, /device:TPU:1, one launch (start us, length us, event | category | flops | bytes accessed | tf_op | source)
XLA Modules:
  0.0 89.8 jit_solution(6414663107753779918)
XLA Ops:
  0.7 0.9 copy-done
  1.5 2.2 %fusion = f32[1,256,256]{2,1,0:T(8,128)} fusion(bf16[256,256]{1,0:T(8,128)(2,1)S(1)} %copy-done, bf16[256,256]{1,0:T(8,128)(2,1)} %param.11, bf16[1,256,256]{2,1,0:T(8,128)(2,1)} %param.13, f32[1,256,256]{2,1,0:T(8,128)} %param.14), kind=kOutput, calls=%fused_computation.3 | convolution fusion | flops 67371008 | bytes 917504 | tf_op jit(solution)/shard_map/bij,kj->bik/dot_general | solution.py:87
  3.8 7.3 %all-to-all-start = ((f32[16,16,256]{2,1,0:T(8,128)}), f32[16,16,256]{2,1,0:T(8,128)S(1)}, u32[]{:S(2)}, u32[]{:S(2)}) async-start(f32[16,16,256]{2,1,0:T(8,128)} %bitcast.11), calls=%async_computation | async-start | bytes 524288 | tf_op jit(solution)/shard_map/all_to_all | solution.py:92
  11.1 0.9 %copy-done.7 = f32[3,8,16,256]{3,2,1,0:T(8,128)S(1)} copy-done((f32[3,8,16,256]{3,2,1,0:T(8,128)S(1)}, f32[3,8,16,256]{3,2,1,0:T(8,128)}, u32[]{:S(2)}) %copy-start.7) | copy-done | bytes 393240
  12.1 0.1 copy-done.8
  12.3 8.3 %all-to-all-done = f32[16,16,256]{2,1,0:T(8,128)S(1)} async-done(((f32[16,16,256]{2,1,0:T(8,128)}), f32[16,16,256]{2,1,0:T(8,128)S(1)}, u32[]{:S(2)}, u32[]{:S(2)}) %all-to-all-start) | async-done | bytes 262176 | tf_op jit(solution)/shard_map/all_to_all | solution.py:92
  20.6 0.4 convolution_add_fusion
  21.0 0.1 fusion.80
  21.1 2.5 %collective-permute-start = (f32[8,1,256]{2,0,1:T(8,128)S(1)}, f32[8,1,256]{2,0,1:T(8,128)S(1)}, u32[]{:S(2)}, u32[]{:S(2)}) collective-permute-start(f32[8,1,256]{2,0,1:T(8,128)S(1)} %get-tuple-element.64), channel_id=1, source_target_pairs={{1,0},{2,1},{3,2},{4,3},{5,4},{6,5},{7,6},{8,7},{9,8},{10,9},{11,1... | collective-permute-start | bytes 24584 | tf_op jit(solution)/shard_map/ppermute | solution.py:20
  23.7 3.1 %collective-permute-start.1 = (f32[8,1,256]{2,0,1:T(8,128)S(1)}, f32[8,1,256]{2,0,1:T(8,128)S(1)}, u32[]{:S(2)}, u32[]{:S(2)}) collective-permute-start(f32[8,1,256]{2,0,1:T(8,128)S(1)} %get-tuple-element.65), channel_id=1, source_target_pairs={{0,1},{1,2},{2,3},{3,4},{4,5},{5,6},{6,7},{7,8},{8,9},{9,10},{10,1... | collective-permute-start | bytes 24584 | tf_op jit(solution)/shard_map/ppermute | solution.py:17
  26.7 0.1 fusion.79
  26.8 0.7 collective-permute-done.1
  27.5 0.4 fusion.39
  27.9 0.1 fusion.77
  28.0 1.9 %collective-permute-start.2 = (f32[8,1,256]{2,0,1:T(8,128)S(1)}, f32[8,1,256]{2,0,1:T(8,128)S(1)}, u32[]{:S(2)}, u32[]{:S(2)}) collective-permute-start(f32[8,1,256]{2,0,1:T(8,128)S(1)} %get-tuple-element.58), channel_id=1, source_target_pairs={{1,0},{2,1},{3,2},{4,3},{5,4},{6,5},{7,6},{8,7},{9,8},{10,9},{11,1... | collective-permute-start | bytes 24584 | tf_op jit(solution)/shard_map/ppermute | solution.py:20
  29.9 4.2 %collective-permute-start.3 = (f32[8,1,256]{2,0,1:T(8,128)S(1)}, f32[8,1,256]{2,0,1:T(8,128)S(1)}, u32[]{:S(2)}, u32[]{:S(2)}) collective-permute-start(f32[8,1,256]{2,0,1:T(8,128)S(1)} %get-tuple-element.59), channel_id=1, source_target_pairs={{0,1},{1,2},{2,3},{3,4},{4,5},{5,6},{6,7},{7,8},{8,9},{9,10},{10,1... | collective-permute-start | bytes 24584 | tf_op jit(solution)/shard_map/ppermute | solution.py:17
  34.2 0.7 collective-permute-done.3
  34.9 0.4 fusion.31
  35.2 0.1 fusion.74
  35.4 1.9 %collective-permute-start.4 = (f32[8,1,256]{2,0,1:T(8,128)S(1)}, f32[8,1,256]{2,0,1:T(8,128)S(1)}, u32[]{:S(2)}, u32[]{:S(2)}) collective-permute-start(f32[8,1,256]{2,0,1:T(8,128)S(1)} %get-tuple-element.48), channel_id=1, source_target_pairs={{1,0},{2,1},{3,2},{4,3},{5,4},{6,5},{7,6},{8,7},{9,8},{10,9},{11,1... | collective-permute-start | bytes 24584 | tf_op jit(solution)/shard_map/ppermute | solution.py:20
  37.3 4.2 %collective-permute-start.5 = (f32[8,1,256]{2,0,1:T(8,128)S(1)}, f32[8,1,256]{2,0,1:T(8,128)S(1)}, u32[]{:S(2)}, u32[]{:S(2)}) collective-permute-start(f32[8,1,256]{2,0,1:T(8,128)S(1)} %get-tuple-element.49), channel_id=1, source_target_pairs={{0,1},{1,2},{2,3},{3,4},{4,5},{5,6},{6,7},{7,8},{8,9},{9,10},{10,1... | collective-permute-start | bytes 24584 | tf_op jit(solution)/shard_map/ppermute | solution.py:17
  41.6 0.7 collective-permute-done.5
  42.3 0.5 fusion.62
  42.8 0.2 multiply_bitcast_fusion.5
  43.1 4.2 %collective-permute-start.6 = (f32[2,8,1,256]{3,1,2,0:T(8,128)S(1)}, f32[2,8,1,256]{3,1,2,0:T(8,128)S(1)}, u32[]{:S(2)}, u32[]{:S(2)}) collective-permute-start(f32[2,8,1,256]{3,1,2,0:T(8,128)S(1)} %get-tuple-element.37), channel_id=1, source_target_pairs={{0,1},{1,2},{2,3},{3,4},{4,5},{5,6},{6,7},{7,8},{8,9},{9,10},{10,1... | collective-permute-start | bytes 49160 | tf_op jit(solution)/shard_map/ppermute | solution.py:17
  47.3 1.9 %collective-permute-start.7 = (f32[2,8,1,256]{3,1,2,0:T(8,128)S(1)}, f32[2,8,1,256]{3,1,2,0:T(8,128)S(1)}, u32[]{:S(2)}, u32[]{:S(2)}) collective-permute-start(f32[2,8,1,256]{3,1,2,0:T(8,128)S(1)} %get-tuple-element.38), channel_id=1, source_target_pairs={{1,0},{2,1},{3,2},{4,3},{5,4},{6,5},{7,6},{8,7},{9,8},{10,9},{11,1... | collective-permute-start | bytes 49160 | tf_op jit(solution)/shard_map/ppermute | solution.py:20
  49.2 0.1 slice.324
  49.4 2.9 %collective-permute-done.7 = f32[2,8,1,256]{3,1,2,0:T(8,128)S(1)} collective-permute-done((f32[2,8,1,256]{3,1,2,0:T(8,128)S(1)}, f32[2,8,1,256]{3,1,2,0:T(8,128)S(1)}, u32[]{:S(2)}, u32[]{:S(2)}) %collective-permute-start.7) | collective-permute-done | bytes 16416 | tf_op jit(solution)/shard_map/ppermute | solution.py:20
  52.4 0.5 fusion.61
  53.0 0.2 multiply_bitcast_fusion.3
  53.2 3.7 %collective-permute-start.8 = (f32[2,8,1,256]{3,1,2,0:T(8,128)S(1)}, f32[2,8,1,256]{3,1,2,0:T(8,128)S(1)}, u32[]{:S(2)}, u32[]{:S(2)}) collective-permute-start(f32[2,8,1,256]{3,1,2,0:T(8,128)S(1)} %get-tuple-element.35), channel_id=1, source_target_pairs={{0,1},{1,2},{2,3},{3,4},{4,5},{5,6},{6,7},{7,8},{8,9},{9,10},{10,1... | collective-permute-start | bytes 49160 | tf_op jit(solution)/shard_map/ppermute | solution.py:17
  56.9 1.9 %collective-permute-start.9 = (f32[2,8,1,256]{3,1,2,0:T(8,128)S(1)}, f32[2,8,1,256]{3,1,2,0:T(8,128)S(1)}, u32[]{:S(2)}, u32[]{:S(2)}) collective-permute-start(f32[2,8,1,256]{3,1,2,0:T(8,128)S(1)} %get-tuple-element.36), channel_id=1, source_target_pairs={{1,0},{2,1},{3,2},{4,3},{5,4},{6,5},{7,6},{8,7},{9,8},{10,9},{11,1... | collective-permute-start | bytes 49160 | tf_op jit(solution)/shard_map/ppermute | solution.py:20
  58.9 0.1 slice.332
  59.1 4.6 %collective-permute-done.9 = f32[2,8,1,256]{3,1,2,0:T(8,128)S(1)} collective-permute-done((f32[2,8,1,256]{3,1,2,0:T(8,128)S(1)}, f32[2,8,1,256]{3,1,2,0:T(8,128)S(1)}, u32[]{:S(2)}, u32[]{:S(2)}) %collective-permute-start.9) | collective-permute-done | bytes 16416 | tf_op jit(solution)/shard_map/ppermute | solution.py:20
  63.7 0.3 fusion.60
  64.0 0.2 multiply_bitcast_fusion.1
  64.3 1.9 %collective-permute-start.10 = (f32[2,8,1,256]{3,1,2,0:T(8,128)S(1)}, f32[2,8,1,256]{3,1,2,0:T(8,128)S(1)}, u32[]{:S(2)}, u32[]{:S(2)}) collective-permute-start(f32[2,8,1,256]{3,1,2,0:T(8,128)S(1)} %get-tuple-element.33), channel_id=1, source_target_pairs={{0,1},{1,2},{2,3},{3,4},{4,5},{5,6},{6,7},{7,8},{8,9},{9,10},{10,1... | collective-permute-start | bytes 49160 | tf_op jit(solution)/shard_map/ppermute | solution.py:17
  66.2 2.4 %collective-permute-start.11 = (f32[2,8,1,256]{3,1,2,0:T(8,128)S(1)}, f32[2,8,1,256]{3,1,2,0:T(8,128)S(1)}, u32[]{:S(2)}, u32[]{:S(2)}) collective-permute-start(f32[2,8,1,256]{3,1,2,0:T(8,128)S(1)} %get-tuple-element.34), channel_id=1, source_target_pairs={{1,0},{2,1},{3,2},{4,3},{5,4},{6,5},{7,6},{8,7},{9,8},{10,9},{11,1... | collective-permute-start | bytes 49160 | tf_op jit(solution)/shard_map/ppermute | solution.py:20
  68.6 0.1 slice.340
  68.8 3.3 %collective-permute-done.11 = f32[2,8,1,256]{3,1,2,0:T(8,128)S(1)} collective-permute-done((f32[2,8,1,256]{3,1,2,0:T(8,128)S(1)}, f32[2,8,1,256]{3,1,2,0:T(8,128)S(1)}, u32[]{:S(2)}, u32[]{:S(2)}) %collective-permute-start.11) | collective-permute-done | bytes 16416 | tf_op jit(solution)/shard_map/ppermute | solution.py:20
  72.2 0.2 multiply_subtract_fusion
  72.5 0.6 gather_fusion
  73.1 0.8 broadcast_select_fusion
  73.9 4.3 %all-to-all-start.1 = ((f32[16,16,256]{2,1,0:T(8,128)}), f32[16,16,256]{2,1,0:T(8,128)S(1)}, u32[]{:S(2)}, u32[]{:S(2)}) async-start(f32[16,16,256]{2,1,0:T(8,128)} %broadcast_select_fusion), calls=%async_computation.1 | async-start | bytes 524288 | tf_op jit(solution)/shard_map/all_to_all | solution.py:98
  78.2 0.7 copy.65
  78.9 8.8 %all-to-all-done.1 = f32[16,16,256]{2,1,0:T(8,128)S(1)} async-done(((f32[16,16,256]{2,1,0:T(8,128)}), f32[16,16,256]{2,1,0:T(8,128)S(1)}, u32[]{:S(2)}, u32[]{:S(2)}) %all-to-all-start.1) | async-done | bytes 262176 | tf_op jit(solution)/shard_map/all_to_all | solution.py:98
  87.7 0.9 %copy-done.1 = f32[1,256,256]{2,1,0:T(8,128)S(1)} copy-done((f32[1,256,256]{2,1,0:T(8,128)S(1)}, f32[1,256,256]{2,1,0:T(8,128)}, u32[]{:S(2)}) %copy-start.1) | copy-done | bytes 262168
  88.7 1.2 %fusion.3 = f32[1,256,256]{2,1,0:T(8,128)} fusion(f32[1,256,256]{2,1,0:T(8,128)S(1)} %copy-done.1, bf16[256,256]{1,0:T(8,128)(2,1)S(1)} %copy-done, bf16[256,256]{1,0:T(8,128)(2,1)S(1)} %fusion.8, bf16[256,256]{1,0:T(8,128)(2,1)S(1)} %copy-done.2), kind=kOutput, calls=%fused_computation.6 | convolution fusion | flops 67371008 | bytes 917504 | tf_op jit(solution)/shard_map/bij,jk->bik/dot_general | solution.py:104
  (49 shorter events, 0.8 us)
Async XLA Ops:
  0.6 0.9 %copy-start = (bf16[256,256]{1,0:T(8,128)(2,1)S(1)}, bf16[256,256]{1,0:T(8,128)(2,1)}, u32[]{:S(2)}) copy-start(bf16[256,256]{1,0:T(8,128)(2,1)} %param.12) | copy-start | bytes 393220
  0.6 10.4 %copy-start.3 = (f32[4,8,16,256]{3,2,1,0:T(8,128)S(1)}, f32[4,8,16,256]{3,2,1,0:T(8,128)}, u32[]{:S(2)}) copy-start(f32[4,8,16,256]{3,2,1,0:T(8,128)} %param.17) | copy-start | bytes 1572868
  3.8 16.8 %all-to-all-start = ((f32[16,16,256]{2,1,0:T(8,128)}), f32[16,16,256]{2,1,0:T(8,128)S(1)}, u32[]{:S(2)}, u32[]{:S(2)}) async-start(f32[16,16,256]{2,1,0:T(8,128)} %bitcast.11), calls=%async_computation | async-start | bytes 524288 | tf_op jit(solution)/shard_map/all_to_all | solution.py:92
  11.1 1.0 %copy-start.7 = (f32[3,8,16,256]{3,2,1,0:T(8,128)S(1)}, f32[3,8,16,256]{3,2,1,0:T(8,128)}, u32[]{:S(2)}) copy-start(f32[3,8,16,256]{3,2,1,0:T(8,128)} %param.18) | copy-start | bytes 1179652
  11.1 1.1 %copy-start.8 = (f32[3,8,16,256]{3,2,1,0:T(8,128)S(1)}, f32[3,8,16,256]{3,2,1,0:T(8,128)}, u32[]{:S(2)}) copy-start(f32[3,8,16,256]{3,2,1,0:T(8,128)} %param.19) | copy-start | bytes 1179652
  12.2 8.4 %copy-start.5 = (f32[8,16,256]{2,1,0:T(8,128)S(1)}, f32[8,16,256]{2,1,0:T(8,128)}, u32[]{:S(2)}) copy-start(f32[8,16,256]{2,1,0:T(8,128)} %param.15) | copy-start | bytes 393220
  12.2 8.4 %copy-start.6 = (f32[8,16,256]{2,1,0:T(8,128)S(1)}, f32[8,16,256]{2,1,0:T(8,128)}, u32[]{:S(2)}) copy-start(f32[8,16,256]{2,1,0:T(8,128)} %param.16) | copy-start | bytes 393220
  12.2 8.4 %copy-start.9 = (s32[16]{0:T(128)S(1)}, s32[16]{0:T(128)}, u32[]{:S(2)}) copy-start(s32[16]{0:T(128)} %param.10) | copy-start | bytes 196
  21.1 5.7 %collective-permute-start = (f32[8,1,256]{2,0,1:T(8,128)S(1)}, f32[8,1,256]{2,0,1:T(8,128)S(1)}, u32[]{:S(2)}, u32[]{:S(2)}) collective-permute-start(f32[8,1,256]{2,0,1:T(8,128)S(1)} %get-tuple-element.64), channel_id=1, source_target_pairs={{1,0},{2,1},{3,2},{4,3},{5,4},{6,5},{7,6},{8,7},{9,8},{10,9},{11,1... | collective-permute-start | bytes 24584 | tf_op jit(solution)/shard_map/ppermute | solution.py:20
  23.7 3.8 %collective-permute-start.1 = (f32[8,1,256]{2,0,1:T(8,128)S(1)}, f32[8,1,256]{2,0,1:T(8,128)S(1)}, u32[]{:S(2)}, u32[]{:S(2)}) collective-permute-start(f32[8,1,256]{2,0,1:T(8,128)S(1)} %get-tuple-element.65), channel_id=1, source_target_pairs={{0,1},{1,2},{2,3},{3,4},{4,5},{5,6},{6,7},{7,8},{8,9},{9,10},{10,1... | collective-permute-start | bytes 24584 | tf_op jit(solution)/shard_map/ppermute | solution.py:17
  28.0 6.2 %collective-permute-start.2 = (f32[8,1,256]{2,0,1:T(8,128)S(1)}, f32[8,1,256]{2,0,1:T(8,128)S(1)}, u32[]{:S(2)}, u32[]{:S(2)}) collective-permute-start(f32[8,1,256]{2,0,1:T(8,128)S(1)} %get-tuple-element.58), channel_id=1, source_target_pairs={{1,0},{2,1},{3,2},{4,3},{5,4},{6,5},{7,6},{8,7},{9,8},{10,9},{11,1... | collective-permute-start | bytes 24584 | tf_op jit(solution)/shard_map/ppermute | solution.py:20
  29.9 5.0 %collective-permute-start.3 = (f32[8,1,256]{2,0,1:T(8,128)S(1)}, f32[8,1,256]{2,0,1:T(8,128)S(1)}, u32[]{:S(2)}, u32[]{:S(2)}) collective-permute-start(f32[8,1,256]{2,0,1:T(8,128)S(1)} %get-tuple-element.59), channel_id=1, source_target_pairs={{0,1},{1,2},{2,3},{3,4},{4,5},{5,6},{6,7},{7,8},{8,9},{9,10},{10,1... | collective-permute-start | bytes 24584 | tf_op jit(solution)/shard_map/ppermute | solution.py:17
  35.4 6.2 %collective-permute-start.4 = (f32[8,1,256]{2,0,1:T(8,128)S(1)}, f32[8,1,256]{2,0,1:T(8,128)S(1)}, u32[]{:S(2)}, u32[]{:S(2)}) collective-permute-start(f32[8,1,256]{2,0,1:T(8,128)S(1)} %get-tuple-element.48), channel_id=1, source_target_pairs={{1,0},{2,1},{3,2},{4,3},{5,4},{6,5},{7,6},{8,7},{9,8},{10,9},{11,1... | collective-permute-start | bytes 24584 | tf_op jit(solution)/shard_map/ppermute | solution.py:20
  37.3 5.0 %collective-permute-start.5 = (f32[8,1,256]{2,0,1:T(8,128)S(1)}, f32[8,1,256]{2,0,1:T(8,128)S(1)}, u32[]{:S(2)}, u32[]{:S(2)}) collective-permute-start(f32[8,1,256]{2,0,1:T(8,128)S(1)} %get-tuple-element.49), channel_id=1, source_target_pairs={{0,1},{1,2},{2,3},{3,4},{4,5},{5,6},{6,7},{7,8},{8,9},{9,10},{10,1... | collective-permute-start | bytes 24584 | tf_op jit(solution)/shard_map/ppermute | solution.py:17
  43.1 6.4 %collective-permute-start.6 = (f32[2,8,1,256]{3,1,2,0:T(8,128)S(1)}, f32[2,8,1,256]{3,1,2,0:T(8,128)S(1)}, u32[]{:S(2)}, u32[]{:S(2)}) collective-permute-start(f32[2,8,1,256]{3,1,2,0:T(8,128)S(1)} %get-tuple-element.37), channel_id=1, source_target_pairs={{0,1},{1,2},{2,3},{3,4},{4,5},{5,6},{6,7},{7,8},{8,9},{9,10},{10,1... | collective-permute-start | bytes 49160 | tf_op jit(solution)/shard_map/ppermute | solution.py:17
  47.3 5.1 %collective-permute-start.7 = (f32[2,8,1,256]{3,1,2,0:T(8,128)S(1)}, f32[2,8,1,256]{3,1,2,0:T(8,128)S(1)}, u32[]{:S(2)}, u32[]{:S(2)}) collective-permute-start(f32[2,8,1,256]{3,1,2,0:T(8,128)S(1)} %get-tuple-element.38), channel_id=1, source_target_pairs={{1,0},{2,1},{3,2},{4,3},{5,4},{6,5},{7,6},{8,7},{9,8},{10,9},{11,1... | collective-permute-start | bytes 49160 | tf_op jit(solution)/shard_map/ppermute | solution.py:20
  53.2 5.9 %collective-permute-start.8 = (f32[2,8,1,256]{3,1,2,0:T(8,128)S(1)}, f32[2,8,1,256]{3,1,2,0:T(8,128)S(1)}, u32[]{:S(2)}, u32[]{:S(2)}) collective-permute-start(f32[2,8,1,256]{3,1,2,0:T(8,128)S(1)} %get-tuple-element.35), channel_id=1, source_target_pairs={{0,1},{1,2},{2,3},{3,4},{4,5},{5,6},{6,7},{7,8},{8,9},{9,10},{10,1... | collective-permute-start | bytes 49160 | tf_op jit(solution)/shard_map/ppermute | solution.py:17
  56.9 6.7 %collective-permute-start.9 = (f32[2,8,1,256]{3,1,2,0:T(8,128)S(1)}, f32[2,8,1,256]{3,1,2,0:T(8,128)S(1)}, u32[]{:S(2)}, u32[]{:S(2)}) collective-permute-start(f32[2,8,1,256]{3,1,2,0:T(8,128)S(1)} %get-tuple-element.36), channel_id=1, source_target_pairs={{1,0},{2,1},{3,2},{4,3},{5,4},{6,5},{7,6},{8,7},{9,8},{10,9},{11,1... | collective-permute-start | bytes 49160 | tf_op jit(solution)/shard_map/ppermute | solution.py:20
  64.3 4.5 %collective-permute-start.10 = (f32[2,8,1,256]{3,1,2,0:T(8,128)S(1)}, f32[2,8,1,256]{3,1,2,0:T(8,128)S(1)}, u32[]{:S(2)}, u32[]{:S(2)}) collective-permute-start(f32[2,8,1,256]{3,1,2,0:T(8,128)S(1)} %get-tuple-element.33), channel_id=1, source_target_pairs={{0,1},{1,2},{2,3},{3,4},{4,5},{5,6},{6,7},{7,8},{8,9},{9,10},{10,1... | collective-permute-start | bytes 49160 | tf_op jit(solution)/shard_map/ppermute | solution.py:17
  66.2 6.0 %collective-permute-start.11 = (f32[2,8,1,256]{3,1,2,0:T(8,128)S(1)}, f32[2,8,1,256]{3,1,2,0:T(8,128)S(1)}, u32[]{:S(2)}, u32[]{:S(2)}) collective-permute-start(f32[2,8,1,256]{3,1,2,0:T(8,128)S(1)} %get-tuple-element.34), channel_id=1, source_target_pairs={{1,0},{2,1},{3,2},{4,3},{5,4},{6,5},{7,6},{8,7},{9,8},{10,9},{11,1... | collective-permute-start | bytes 49160 | tf_op jit(solution)/shard_map/ppermute | solution.py:20
  73.9 13.8 %all-to-all-start.1 = ((f32[16,16,256]{2,1,0:T(8,128)}), f32[16,16,256]{2,1,0:T(8,128)S(1)}, u32[]{:S(2)}, u32[]{:S(2)}) async-start(f32[16,16,256]{2,1,0:T(8,128)} %broadcast_select_fusion), calls=%async_computation.1 | async-start | bytes 524288 | tf_op jit(solution)/shard_map/all_to_all | solution.py:98
  78.2 9.5 %copy-start.4 = (bf16[1,256,256]{2,1,0:T(8,128)(2,1)S(1)}, bf16[1,256,256]{2,1,0:T(8,128)(2,1)}, u32[]{:S(2)}) copy-start(bf16[1,256,256]{2,1,0:T(8,128)(2,1)} %param.13) | copy-start | bytes 393220
  87.7 1.0 %copy-start.1 = (f32[1,256,256]{2,1,0:T(8,128)S(1)}, f32[1,256,256]{2,1,0:T(8,128)}, u32[]{:S(2)}) copy-start(f32[1,256,256]{2,1,0:T(8,128)} %param.14) | copy-start | bytes 786436
  87.7 1.0 %copy-start.2 = (bf16[256,256]{1,0:T(8,128)(2,1)S(1)}, bf16[256,256]{1,0:T(8,128)(2,1)}, u32[]{:S(2)}) copy-start(bf16[256,256]{1,0:T(8,128)(2,1)} %param.11) | copy-start | bytes 393220

commit v2 on v1

v2 whole, which is shorter than its diff:
```python
import jax
import jax.numpy as jnp
from jax import lax
from jax.experimental import pallas as pl
from jax.experimental.pallas import tpu as pltpu
from jax.sharding import PartitionSpec as P

STEPS = 3
LANES = 128
SUB = 8
STEP_SIZE = 0.15

HALO = 2 * STEPS
COEF_ROWS = HALO - 1


def weight_rows(section):
    return section + 1


def packed_fields():
    fields = [("coefs", k, COEF_ROWS) for k in range(4)]
    for section in range(STEPS):
        fields.append(("obs_weight", section, weight_rows(section)))
        fields.append(("innovation", section, weight_rows(section)))
    return fields


PACKED_ROWS = sum(rows for _, _, rows in packed_fields())
HALO_ROWS = -(-(SUB + PACKED_ROWS) // SUB) * SUB


def vmem(count):
    return [pl.BlockSpec(memory_space=pltpu.VMEM)] * count


def member_sum_kernel(tiles, lat_ref, lon_ref, perts_ref, control_ref, out_ref, padded_ref):
    blocks, nlat, nlon = control_ref.shape
    rows = nlat // tiles
    tall = rows + 2 * HALO
    total = None
    for b in range(blocks):
        smoothed = jnp.dot(
            lat_ref[...], control_ref[b].astype(jnp.bfloat16), preferred_element_type=jnp.float32
        ).astype(jnp.bfloat16)
        field = lax.dot_general(
            smoothed, lon_ref[...], (((1,), (1,)), ((), ())), preferred_element_type=jnp.float32
        )
        term = perts_ref[b].astype(jnp.float32) * field
        total = term if total is None else total + term
    edge = jnp.zeros((SUB, nlon), jnp.float32)
    padded_ref[0:SUB, :] = edge
    padded_ref[SUB + nlat : 2 * SUB + nlat, :] = edge
    padded_ref[SUB : SUB + nlat, :] = total
    for e in range(tiles):
        start = SUB + e * rows - HALO
        for h in range(nlon // LANES):
            out_ref[e, h * tall : (h + 1) * tall, :] = padded_ref[
                start : start + tall, h * LANES : (h + 1) * LANES
            ]


def pack_kernel(control_ref, scale_ref, coefs_ref, weight_ref, innov_ref, up_ref, down_ref):
    refs = {"coefs": coefs_ref, "obs_weight": weight_ref, "innovation": innov_ref}
    rows = control_ref.shape[1]

    def level(l, carry):
        scale, control = scale_ref.at[l], control_ref.at[l]
        last, first = slice(rows - SUB, rows), slice(0, SUB)
        up_ref[l, 0:SUB, :] = scale[last, :] * control[last, :]
        down_ref[l, HALO_ROWS - SUB : HALO_ROWS, :] = scale[first, :] * control[first, :]
        up_at, down_at = SUB, 0
        for name, k, count in packed_fields():
            field = refs[name].at[k, l]
            up_ref[l, up_at : up_at + count, :] = field[rows - count : rows, :]
            down_ref[l, down_at : down_at + count, :] = field[0:count, :]
            up_at, down_at = up_at + count, down_at + count
        return carry

    lax.fori_loop(0, control_ref.shape[0], level, 0)


def window_kernel(
    level_ref,
    received_ref,
    low_ref,
    high_ref,
    control_ref,
    scale_ref,
    coefs_ref,
    weight_ref,
    innov_ref,
    send_ref,
    grad_ref,
    sums_ref,
):
    tiles = received_ref.shape[0]
    levels, rows, nlon = control_ref.shape
    tall = rows + 2 * HALO
    ext = rows + 2 * SUB
    halves = nlon // LANES
    packed = halves * tall
    refs = {"coefs": coefs_ref, "obs_weight": weight_ref, "innovation": innov_ref}

    sums_ref[...] = jnp.zeros_like(sums_ref)
    for d in range(tiles):
        at = level_ref[d]
        sums_ref[at, SUB : SUB + packed, :] += received_ref[d]

    def level(l, carry):
        parts = []
        for h in range(halves):
            start = SUB + h * tall - (SUB - HALO)
            parts.append(sums_ref[l, start : start + ext, :])
        ens = jnp.concatenate(parts, axis=1)
        static = jnp.concatenate(
            [
                low_ref[l, 0:SUB, :],
                scale_ref[l] * control_ref[l],
                high_ref[l, HALO_ROWS - SUB : HALO_ROWS, :],
            ],
            axis=0,
        )
        state = static + ens
        fields = {}
        low_at, high_at = SUB, 0
        for name, k, count in packed_fields():
            low_at += count
            fields[name, k] = jnp.concatenate(
                [
                    low_ref[l, low_at - SUB : low_at, :],
                    refs[name][k, l],
                    high_ref[l, high_at : high_at + SUB, :],
                ],
                axis=0,
            )
            high_at += count
        c0, c1, c2, c3 = (fields["coefs", k] for k in range(4))
        rest = 1.0 - (c0 + c1 + c2 + c3)
        weighted = []
        for section in range(STEPS):
            state = (
                rest * state
                + c0 * pltpu.roll(state, ext - 1, 0)
                + c1 * pltpu.roll(state, 1, 0)
                + c2 * pltpu.roll(state, nlon - 1, 1)
                + c3 * pltpu.roll(state, 1, 1)
            )
            weighted.append(
                fields["obs_weight", section] * (state - fields["innovation", section])
            )
        adjoint = weighted[STEPS - 1]
        for section in range(STEPS - 2, -2, -1):
            adjoint = (
                rest * adjoint
                + pltpu.roll(c0 * adjoint, 1, 0)
                + pltpu.roll(c1 * adjoint, ext - 1, 0)
                + pltpu.roll(c2 * adjoint, 1, 1)
                + pltpu.roll(c3 * adjoint, nlon - 1, 1)
            )
            if section >= 0:
                adjoint = adjoint + weighted[section]
        grad_ref[l] = adjoint[SUB : SUB + rows, :]
        return carry

    lax.fori_loop(0, levels, level, 0)
    for e in range(tiles):
        send_ref[e] = grad_ref[level_ref[e]]


def member_update_kernel(lat_ref, lon_ref, perts_ref, grad_ref, control_ref, out_ref):
    for b in range(control_ref.shape[0]):
        weighted = (perts_ref[b].astype(jnp.float32) * grad_ref[...]).astype(jnp.bfloat16)
        adjoint_lat = lax.dot_general(
            lat_ref[...], weighted, (((0,), (0,)), ((), ())), preferred_element_type=jnp.float32
        ).astype(jnp.bfloat16)
        member_grad = jnp.dot(adjoint_lat, lon_ref[...], preferred_element_type=jnp.float32)
        control = control_ref[b]
        out_ref[b] = control - STEP_SIZE * (control + member_grad)


def tall_local(
    level_map, loc_lat, loc_lon, ens_perts, ens_control,
    static_control, static_scale, coefs, obs_weight, innovation,
):
    tiles = lax.axis_size("tile")
    levels, rows, nlon = static_control.shape
    nlat = ens_control.shape[1]
    tall = rows + 2 * HALO
    packed = tall * (nlon // LANES)
    pieces = pl.pallas_call(
        lambda *refs: member_sum_kernel(tiles, *refs),
        out_shape=jax.ShapeDtypeStruct((tiles, packed, LANES), jnp.float32),
        in_specs=vmem(4),
        out_specs=pl.BlockSpec(memory_space=pltpu.VMEM),
        scratch_shapes=[pltpu.VMEM((nlat + 2 * SUB, nlon), jnp.float32)],
        name="member_sum",
    )(loc_lat, loc_lon, ens_perts, ens_control)
    received = lax.all_to_all(pieces, "tile", split_axis=0, concat_axis=0, tiled=True)

    halo = jax.ShapeDtypeStruct((levels, HALO_ROWS, nlon), jnp.float32)
    up, down = pl.pallas_call(
        pack_kernel,
        out_shape=(halo, halo),
        in_specs=vmem(5),
        out_specs=tuple(vmem(2)),
        name="pack",
    )(static_control, static_scale, coefs, obs_weight, innovation)
    forward = [(i, i + 1) for i in range(tiles - 1)]
    backward = [(target, source) for source, target in forward]
    low = lax.ppermute(up, "tile", forward)
    high = lax.ppermute(down, "tile", backward)

    send, gradient = pl.pallas_call(
        window_kernel,
        out_shape=(
            jax.ShapeDtypeStruct((tiles, rows, nlon), jnp.float32),
            jax.ShapeDtypeStruct((levels, rows, nlon), jnp.float32),
        ),
        in_specs=[pl.BlockSpec(memory_space=pltpu.SMEM)] + vmem(8),
        out_specs=tuple(vmem(2)),
        scratch_shapes=[pltpu.VMEM((levels, packed + 2 * SUB, LANES), jnp.float32)],
        name="window",
    )(level_map, received, low, high, static_control, static_scale, coefs, obs_weight, innovation)
    incoming = lax.all_to_all(send, "tile", split_axis=0, concat_axis=0, tiled=True)
    static_final = static_control - STEP_SIZE * (static_control + static_scale * gradient)

    ens_final = pl.pallas_call(
        member_update_kernel,
        out_shape=jax.ShapeDtypeStruct(ens_control.shape, jnp.float32),
        in_specs=vmem(5),
        out_specs=pl.BlockSpec(memory_space=pltpu.VMEM),
        name="member_update",
    )(loc_lat, loc_lon, ens_perts, incoming.reshape(nlat, nlon), ens_control)
    return ens_final, static_final


def exchanged(block, axis):
    count = lax.axis_size("tile")
    forward = [(i, i + 1) for i in range(count - 1)]
    backward = [(target, source) for source, target in forward]
    last = block.shape[axis] - 1
    low = lax.ppermute(lax.slice_in_dim(block, last, last + 1, axis=axis), "tile", forward)
    high = lax.ppermute(lax.slice_in_dim(block, 0, 1, axis=axis), "tile", backward)
    return jnp.concatenate([low, block, high], axis=axis)


def forward_step(state, coeffs):
    padded = exchanged(state, 1)
    return (
        state
        + coeffs[0] * (padded[:, 2:] - state)
        + coeffs[1] * (padded[:, :-2] - state)
        + coeffs[2] * (jnp.roll(state, -1, 2) - state)
        + coeffs[3] * (jnp.roll(state, 1, 2) - state)
    )


def adjoint_step(adjoint, coeffs):
    coef_sum = coeffs[0] + coeffs[1] + coeffs[2] + coeffs[3]
    padded = exchanged(jnp.stack([coeffs[0] * adjoint, coeffs[1] * adjoint]), 2)
    return (
        (1.0 - coef_sum) * adjoint
        + padded[0][:, :-2]
        + padded[1][:, 2:]
        + jnp.roll(coeffs[2] * adjoint, 1, 2)
        + jnp.roll(coeffs[3] * adjoint, -1, 2)
    )


def any_local(
    level_map, loc_lat, loc_lon, ens_perts, ens_control,
    static_control, static_scale, coefs, obs_weight, innovation,
):
    tiles = lax.axis_size("tile")
    level_ids = jnp.arange(static_control.shape[0], dtype=jnp.int32)
    level_onehot = (level_map[:, None] == level_ids[None, :]).astype(jnp.float32)
    lat_smoothed = jnp.einsum(
        "ij,bjk->bik", loc_lat, ens_control.astype(jnp.bfloat16),
        preferred_element_type=jnp.float32,
    ).astype(jnp.bfloat16)
    member_field = jnp.einsum(
        "bij,kj->bik", lat_smoothed, loc_lon, preferred_element_type=jnp.float32
    )
    partial_value = jnp.sum(ens_perts.astype(jnp.float32) * member_field, axis=0)
    pieces = partial_value.reshape(tiles, -1, partial_value.shape[1])
    received = lax.all_to_all(pieces, "tile", split_axis=0, concat_axis=0, tiled=True)
    ens_incr = jnp.einsum("dl,dij->lij", level_onehot, received, precision=lax.Precision.HIGHEST)
    state = static_scale * static_control + ens_incr
    weighted = []
    for section in range(STEPS):
        state = forward_step(state, coefs)
        weighted.append(obs_weight[section] * (state - innovation[section]))
    adjoint = weighted[STEPS - 1]
    for section in range(STEPS - 2, -1, -1):
        adjoint = adjoint_step(adjoint, coefs) + weighted[section]
    gradient = adjoint_step(adjoint, coefs)
    static_final = static_control - STEP_SIZE * (static_control + static_scale * gradient)
    outgoing = jnp.take(gradient, level_map, axis=0)
    incoming = lax.all_to_all(outgoing, "tile", split_axis=0, concat_axis=0, tiled=True)
    grad_field = incoming.reshape(-1, incoming.shape[2])
    weighted_grad = (ens_perts.astype(jnp.float32) * grad_field[None]).astype(jnp.bfloat16)
    adjoint_lat = jnp.einsum(
        "ji,bjk->bik", loc_lat, weighted_grad, preferred_element_type=jnp.float32
    ).astype(jnp.bfloat16)
    member_grad = jnp.einsum("bij,jk->bik", adjoint_lat, loc_lon, preferred_element_type=jnp.float32)
    return ens_control - STEP_SIZE * (ens_control + member_grad), static_final


def local(*args):
    _, rows, nlon = args[5].shape
    whole_tiles = rows % SUB == 0 and nlon % LANES == 0
    return (tall_local if whole_tiles else any_local)(*args)


def solution(mesh):
    in_specs = (
        P(),
        P(),
        P(),
        P(("groups", "tile"), None, None),
        P(("groups", "tile"), None, None),
        P("groups", "tile", None),
        P("groups", "tile", None),
        P(None, "groups", "tile", None),
        P(None, "groups", "tile", None),
        P(None, "groups", "tile", None),
    )
    out_specs = (P(("groups", "tile"), None, None), P("groups", "tile", None))
    return jax.shard_map(local, mesh=mesh, in_specs=in_specs, out_specs=out_specs, check_vma=False)
```

time: 91.1 us -> 54.2 us (0.59)
  starting transfers between devices: 45.5 us -> 19.9 us
  waiting for transfers between devices: 30 us -> 16.4 us
  Pallas kernels: 0 us -> 13.3 us
  matrix products: 3.82 us -> 0 us
  other arithmetic: 3.97 us -> 0.69 us
  local copies, waits for them, and re-layouts: 5.43 us -> 2.22 us
    ppermute x12 -> x2, starting transfers between devices: 33.9 us -> 5.45 us  [the longest x1 3.53 us: tall_local(): low = lax.ppermute(up, 'tile', forward)]
    pallas_call x0 -> x4, Pallas kernels: none -> 13.3 us  [the longest x1 6.33 us: tall_local(): pl.pallas_call(window_kernel, out_shape=(jax.ShapeDtypeStruct((tiles, row...]
    all_to_all x2, waiting for transfers between devices: 17.1 us -> 8.81 us  [the longest x1 8.8 us: tall_local(): lax.all_to_all(send, 'tile', split_axis=0, concat_axis=0, tiled=True)]
    ppermute x12 -> x2, waiting for transfers between devices: 12.9 us -> 7.59 us  [the longest x1 4.11 us: tall_local(): high = lax.ppermute(down, 'tile', backward)]
    dot_general x3 -> x0, matrix products: 3.82 us -> none  [the longest x1 2.22 us: local(): jnp.einsum('bij,kj->bik', lat_smoothed, loc_lon, preferred_element_type=j...]
    all_to_all x2, starting transfers between devices: 11.6 us -> 14.4 us  [the longest x1 7.31 us: tall_local(): lax.all_to_all(pieces, 'tile', split_axis=0, concat_axis=0, tiled=True)]
    unnamed x21 -> x14, local copies, waits for them, and re-layouts: 3.62 us -> 2.22 us
    mul x3 -> x0, other arithmetic: 1.39 us -> none  [adjoint_step(): coeffs[3] * adjoint]
  transfers between devices with their start and end apart: 14 -> 4, of which waited for: 8 -> 3; matrix products, arithmetic and copies ran while one was open for 2% -> 1% of each run, Pallas kernels for 0% -> 5%
where the time goes in v2:
time: 54.2 us; the launch traced here: 53.2 us
  starting transfers between devices  19.9 us (37%)
  waiting for transfers between devices  16.4 us (30%)
  Pallas kernels  13.3 us (25%)
  local copies, waits for them, and re-layouts  2.22 us (4%)
  other arithmetic  0.69 us (1%)
  between operations  0.69 us (1%)
    all_to_all x1, waiting for transfers between devices, tall_local(): lax.all_to_all(send, 'tile', split_axis=0, concat_axis=0, tiled=True)  8.8 us
    all_to_all x1, starting transfers between devices, tall_local(): lax.all_to_all(pieces, 'tile', split_axis=0, concat_axis=0, tiled=True)  7.31 us
    all_to_all x1, starting transfers between devices, tall_local(): lax.all_to_all(send, 'tile', split_axis=0, concat_axis=0, tiled=True)  7.12 us
    pallas_call x1, Pallas kernels, tall_local(): pl.pallas_call(window_kernel, out_shape=(jax.ShapeDtypeStruct((tiles, row...  6.33 us
    ppermute x1, waiting for transfers between devices, tall_local(): high = lax.ppermute(down, 'tile', backward)  4.11 us
    ppermute x1, starting transfers between devices, tall_local(): low = lax.ppermute(up, 'tile', forward)  3.53 us
    ppermute x1, waiting for transfers between devices, tall_local(): low = lax.ppermute(up, 'tile', forward)  3.49 us
    pallas_call x1, Pallas kernels, tall_local(): pl.pallas_call(pack_kernel, out_shape=(halo, halo), in_specs=vmem(5), out...  2.4 us
  transfers between devices with their start and end apart: 4, of which 3 were waited for; matrix products, arithmetic and copies ran while one was open for 1% of the time, Pallas kernels for 5%

profile of v2, /device:TPU:1, one launch (start us, length us, event | category | flops | bytes accessed | tf_op | source)
XLA Modules:
  0.0 53.2 jit_solution(8507135140308480578)
XLA Ops:
  0.6 2.3 %member_sum.1 = f32[16,56,128]{2,1,0:T(8,128)} custom-call(bf16[256,256]{1,0:T(8,128)(2,1)} %lat_ref.1, bf16[256,256]{1,0:T(8,128)(2,1)} %lon_ref.1, bf16[1,256,256]{2,1,0:T(8,128)(2,1)} %perts_ref.1, f32[1,256,256]{2,1,0:T(8,128)} %control_ref.5), custom_call_target="tpu_custom_call" | custom-call | tf_op jit(solution)/shard_map/member_sum/pallas_call | solution.py:191
  2.9 7.3 %all-to-all-start = ((f32[16,56,128]{2,1,0:T(8,128)}), f32[16,56,128]{2,1,0:T(8,128)S(1)}, u32[]{:S(2)}, u32[]{:S(2)}) async-start(f32[16,56,128]{2,1,0:T(8,128)} %member_sum.1), calls=%async_computation | async-start | bytes 917504 | tf_op jit(solution)/shard_map/all_to_all | solution.py:199
  10.2 2.4 %pack.1 = (f32[8,40,256]{2,1,0:T(8,128)}, f32[8,40,256]{2,1,0:T(8,128)}) custom-call(f32[8,16,256]{2,1,0:T(8,128)} %control_ref.4, f32[8,16,256]{2,1,0:T(8,128)} %scale_ref.3, f32[4,8,16,256]{3,2,1,0:T(8,128)} %coefs_ref.3, f32[3,8,16,256]{3,2,1,0:T(8,128)} %weight_ref.3, f32[3,8,16,256]{3,2,1,0:T(8,128)} %innov_ref.3), custom_call_target="tpu_custom_call" | custom-call | tf_op jit(solution)/shard_map/pack/pallas_call | solution.py:202
  12.6 3.5 %collective-permute-start = (f32[8,40,256]{2,1,0:T(8,128)}, f32[8,40,256]{2,1,0:T(8,128)S(1)}, u32[]{:S(2)}, u32[]{:S(2)}) collective-permute-start(f32[8,40,256]{2,1,0:T(8,128)} %get-tuple-element.6), channel_id=1, source_target_pairs={{0,1},{1,2},{2,3},{3,4},{4,5},{5,6},{6,7},{7,8},{8,9},{9,10},{10,1... | collective-permute-start | bytes 983048 | tf_op jit(solution)/shard_map/ppermute | solution.py:211
  16.2 1.9 %collective-permute-start.1 = (f32[8,40,256]{2,1,0:T(8,128)}, f32[8,40,256]{2,1,0:T(8,128)S(1)}, u32[]{:S(2)}, u32[]{:S(2)}) collective-permute-start(f32[8,40,256]{2,1,0:T(8,128)} %get-tuple-element.7), channel_id=1, source_target_pairs={{1,0},{2,1},{3,2},{4,3},{5,4},{6,5},{7,6},{8,7},{9,8},{10,9},{11,1... | collective-permute-start | bytes 983048 | tf_op jit(solution)/shard_map/ppermute | solution.py:212
  18.1 3.5 %collective-permute-done.low_ref = f32[8,40,256]{2,1,0:T(8,128)S(1)} collective-permute-done((f32[8,40,256]{2,1,0:T(8,128)}, f32[8,40,256]{2,1,0:T(8,128)S(1)}, u32[]{:S(2)}, u32[]{:S(2)}) %collective-permute-start) | collective-permute-done | bytes 327712 | tf_op jit(solution)/shard_map/ppermute | solution.py:211
  21.6 0.0 copy-start.4
  21.6 4.1 %collective-permute-done.1.high_ref = f32[8,40,256]{2,1,0:T(8,128)S(1)} collective-permute-done((f32[8,40,256]{2,1,0:T(8,128)}, f32[8,40,256]{2,1,0:T(8,128)S(1)}, u32[]{:S(2)}, u32[]{:S(2)}) %collective-permute-start.1) | collective-permute-done | bytes 327712 | tf_op jit(solution)/shard_map/ppermute | solution.py:212
  25.7 0.0 copy-start.5
  25.7 0.0 all-to-all-done.received_ref
  25.7 0.0 copy-done.4
  25.7 0.7 %copy-done.5 = f32[8,40,256]{2,1,0:T(8,128)} copy-done((f32[8,40,256]{2,1,0:T(8,128)}, f32[8,40,256]{2,1,0:T(8,128)S(1)}, u32[]{:S(2)}) %copy-start.5) | copy-done | bytes 327704
  26.4 0.0 copy-start
  26.4 0.8 %copy-done = f32[16,56,128]{2,1,0:T(8,128)} copy-done((f32[16,56,128]{2,1,0:T(8,128)}, f32[16,56,128]{2,1,0:T(8,128)S(1)}, u32[]{:S(2)}) %copy-start) | copy-done | bytes 458776
  27.2 6.3 %window.1 = (f32[16,16,256]{2,1,0:T(8,128)}, f32[8,16,256]{2,1,0:T(8,128)}) custom-call(s32[16]{0:T(128)} %level_ref.1, f32[16,56,128]{2,1,0:T(8,128)} %copy-done, f32[8,40,256]{2,1,0:T(8,128)} %copy-done.4, f32[8,40,256]{2,1,0:T(8,128)} %copy-done.5, f32[8,16,256]{2,1,0:T(8,128)} %control_ref.4, f32[8,16,256]{2,1,0:T(8,128)} %scale_ref.3, ...), custom_call_target="tpu_custom_call" | custom-call | tf_op jit(solution)/shard_map/window/pallas_call | solution.py:214
  33.5 0.0 copy-start.1
  33.5 0.0 copy-start.2
  33.5 0.0 copy-start.6
  33.6 7.1 %all-to-all-start.1 = ((f32[16,16,256]{2,1,0:T(8,128)}), f32[16,16,256]{2,1,0:T(8,128)S(1)}, u32[]{:S(2)}, u32[]{:S(2)}) async-start(f32[16,16,256]{2,1,0:T(8,128)} %get-tuple-element.8), calls=%async_computation.1 | async-start | bytes 524288 | tf_op jit(solution)/shard_map/all_to_all | solution.py:225
  40.7 0.0 copy-done.1
  40.7 0.0 copy-done.2
  40.7 0.0 copy-done.6
  40.7 0.7 %multiply_subtract_fusion = f32[8,16,256]{2,1,0:T(8,128)} fusion(f32[8,16,256]{2,1,0:T(8,128)S(1)} %copy-done.1, f32[8,16,256]{2,1,0:T(8,128)S(1)} %copy-done.2, f32[8,16,256]{2,1,0:T(8,128)S(1)} %copy-done.6), kind=kLoop, calls=%fused_computation | loop fusion | flops 131072 | bytes 524288 | tf_op jit(solution)/shard_map/sub | solution.py:226
  41.4 8.8 %all-to-all-done.1 = f32[16,16,256]{2,1,0:T(8,128)S(1)} async-done(((f32[16,16,256]{2,1,0:T(8,128)}), f32[16,16,256]{2,1,0:T(8,128)S(1)}, u32[]{:S(2)}, u32[]{:S(2)}) %all-to-all-start.1) | async-done | bytes 262176 | tf_op jit(solution)/shard_map/all_to_all | solution.py:225
  50.2 0.0 copy-start.3
  50.2 0.7 %copy-done.3 = f32[16,16,256]{2,1,0:T(8,128)} copy-done((f32[16,16,256]{2,1,0:T(8,128)}, f32[16,16,256]{2,1,0:T(8,128)S(1)}, u32[]{:S(2)}) %copy-start.3) | copy-done | bytes 262168
  50.9 2.3 %member_update.1 = f32[1,256,256]{2,1,0:T(8,128)} custom-call(bf16[256,256]{1,0:T(8,128)(2,1)} %lat_ref.1, bf16[256,256]{1,0:T(8,128)(2,1)} %lon_ref.1, bf16[1,256,256]{2,1,0:T(8,128)(2,1)} %perts_ref.1, f32[256,256]{1,0:T(8,128)} %bitcast.1, f32[1,256,256]{2,1,0:T(8,128)} %control_ref.5), custom_call_target="tpu_custom_call" | custom-call | tf_op jit(solution)/shard_map/member_update/pallas_call | solution.py:228
Async XLA Ops:
  2.9 22.8 %all-to-all-start = ((f32[16,56,128]{2,1,0:T(8,128)}), f32[16,56,128]{2,1,0:T(8,128)S(1)}, u32[]{:S(2)}, u32[]{:S(2)}) async-start(f32[16,56,128]{2,1,0:T(8,128)} %member_sum.1), calls=%async_computation | async-start | bytes 917504 | tf_op jit(solution)/shard_map/all_to_all | solution.py:199
  12.6 9.0 %collective-permute-start = (f32[8,40,256]{2,1,0:T(8,128)}, f32[8,40,256]{2,1,0:T(8,128)S(1)}, u32[]{:S(2)}, u32[]{:S(2)}) collective-permute-start(f32[8,40,256]{2,1,0:T(8,128)} %get-tuple-element.6), channel_id=1, source_target_pairs={{0,1},{1,2},{2,3},{3,4},{4,5},{5,6},{6,7},{7,8},{8,9},{9,10},{10,1... | collective-permute-start | bytes 983048 | tf_op jit(solution)/shard_map/ppermute | solution.py:211
  16.2 9.5 %collective-permute-start.1 = (f32[8,40,256]{2,1,0:T(8,128)}, f32[8,40,256]{2,1,0:T(8,128)S(1)}, u32[]{:S(2)}, u32[]{:S(2)}) collective-permute-start(f32[8,40,256]{2,1,0:T(8,128)} %get-tuple-element.7), channel_id=1, source_target_pairs={{1,0},{2,1},{3,2},{4,3},{5,4},{6,5},{7,6},{8,7},{9,8},{10,9},{11,1... | collective-permute-start | bytes 983048 | tf_op jit(solution)/shard_map/ppermute | solution.py:212
  21.6 4.1 %copy-start.4 = (f32[8,40,256]{2,1,0:T(8,128)}, f32[8,40,256]{2,1,0:T(8,128)S(1)}, u32[]{:S(2)}) copy-start(f32[8,40,256]{2,1,0:T(8,128)S(1)} %collective-permute-done.low_ref) | copy-start | bytes 983044
  25.7 0.7 %copy-start.5 = (f32[8,40,256]{2,1,0:T(8,128)}, f32[8,40,256]{2,1,0:T(8,128)S(1)}, u32[]{:S(2)}) copy-start(f32[8,40,256]{2,1,0:T(8,128)S(1)} %collective-permute-done.1.high_ref) | copy-start | bytes 983044
  26.4 0.8 %copy-start = (f32[16,56,128]{2,1,0:T(8,128)}, f32[16,56,128]{2,1,0:T(8,128)S(1)}, u32[]{:S(2)}) copy-start(f32[16,56,128]{2,1,0:T(8,128)S(1)} %all-to-all-done.received_ref) | copy-start | bytes 1376260
  33.5 7.1 %copy-start.1 = (f32[8,16,256]{2,1,0:T(8,128)S(1)}, f32[8,16,256]{2,1,0:T(8,128)}, u32[]{:S(2)}) copy-start(f32[8,16,256]{2,1,0:T(8,128)} %control_ref.4) | copy-start | bytes 393220
  33.5 7.1 %copy-start.2 = (f32[8,16,256]{2,1,0:T(8,128)S(1)}, f32[8,16,256]{2,1,0:T(8,128)}, u32[]{:S(2)}) copy-start(f32[8,16,256]{2,1,0:T(8,128)} %scale_ref.3) | copy-start | bytes 393220
  33.5 7.1 %copy-start.6 = (f32[8,16,256]{2,1,0:T(8,128)S(1)}, f32[8,16,256]{2,1,0:T(8,128)}, u32[]{:S(2)}) copy-start(f32[8,16,256]{2,1,0:T(8,128)} %get-tuple-element.9) | copy-start | bytes 393220
  33.6 16.6 %all-to-all-start.1 = ((f32[16,16,256]{2,1,0:T(8,128)}), f32[16,16,256]{2,1,0:T(8,128)S(1)}, u32[]{:S(2)}, u32[]{:S(2)}) async-start(f32[16,16,256]{2,1,0:T(8,128)} %get-tuple-element.8), calls=%async_computation.1 | async-start | bytes 524288 | tf_op jit(solution)/shard_map/all_to_all | solution.py:225
  50.2 0.7 %copy-start.3 = (f32[16,16,256]{2,1,0:T(8,128)}, f32[16,16,256]{2,1,0:T(8,128)S(1)}, u32[]{:S(2)}) copy-start(f32[16,16,256]{2,1,0:T(8,128)S(1)} %all-to-all-done.1) | copy-start | bytes 786436

commit v3 on v2

v3 whole, which is shorter than its diff:
```python
import jax
import jax.numpy as jnp
from jax import lax
from jax.experimental import pallas as pl
from jax.experimental.pallas import tpu as pltpu
from jax.sharding import PartitionSpec as P

STEPS = 3
LANES = 128
SUB = 8
STEP_SIZE = 0.15
GROUP = 4

SPILL = 2
HALO = 2 * STEPS - SPILL


def packed_fields():
    fields = [("static", 0, HALO)]
    fields += [("coefs", k, HALO - 1) for k in range(4)]
    for section in range(SPILL, STEPS):
        fields += [(name, section, section + 1 - SPILL) for name in ("obs_weight", "innovation")]
    return fields


LEVEL_ROWS = sum(rows for _, _, rows in packed_fields())
PACKED = GROUP * LEVEL_ROWS


def vmem(count):
    return [pl.BlockSpec(memory_space=pltpu.VMEM)] * count


def params(mebibytes):
    return pltpu.CompilerParams(vmem_limit_bytes=mebibytes << 20)


def sublane(shape):
    return lax.broadcasted_iota(jnp.int32, shape, 0)


def member_sum_kernel(tiles, lat_ref, lon_ref, perts_ref, control_ref, out_ref):
    blocks, nlat, nlon = control_ref.shape
    rows = nlat // tiles
    halves = nlon // LANES
    total = None
    for b in range(blocks):
        smoothed = jnp.dot(
            lat_ref[...], control_ref[b].astype(jnp.bfloat16), preferred_element_type=jnp.float32
        ).astype(jnp.bfloat16)
        field = lax.dot_general(
            smoothed, lon_ref[...], (((1,), (1,)), ((), ())), preferred_element_type=jnp.float32
        )
        term = perts_ref[b].astype(jnp.float32) * field
        total = term if total is None else total + term
    first = sublane((SUB, LANES)) < HALO
    edge = jnp.zeros((SUB, LANES), jnp.float32)
    for e in range(tiles):
        for h in range(halves):
            lanes = slice(h * LANES, (h + 1) * LANES)
            start, end = e * rows, (e + 1) * rows
            above = total[end : end + SUB, lanes] if end < nlat else edge
            below = total[start - SUB : start, lanes] if start > 0 else edge
            out_ref[e, h * rows : (h + 1) * rows, :] = total[start:end, lanes]
            at = halves * rows + h * SUB
            out_ref[e, at : at + SUB, :] = jnp.where(first, above, below)


def pack_kernel(control_ref, scale_ref, coefs_ref, weight_ref, innov_ref, up_ref, down_ref):
    refs = {"coefs": coefs_ref, "obs_weight": weight_ref, "innovation": innov_ref}
    levels, rows, _ = control_ref.shape
    for l in range(levels):
        at = l % GROUP * LEVEL_ROWS
        for name, k, count in packed_fields():
            last, first = slice(rows - count, rows), slice(0, count)
            if name == "static":
                high = scale_ref[l, last, :] * control_ref[l, last, :]
                low = scale_ref[l, first, :] * control_ref[l, first, :]
            else:
                high, low = refs[name][k, l, last, :], refs[name][k, l, first, :]
            up_ref[l // GROUP, at : at + count, :] = high
            down_ref[l // GROUP, at : at + count, :] = low
            at += count


def window_kernel(
    level_ref,
    received_ref,
    low_ref,
    high_ref,
    control_ref,
    scale_ref,
    coefs_ref,
    weight_ref,
    innov_ref,
    send_ref,
    grad_ref,
    up_ref,
    down_ref,
    sums_ref,
):
    tiles = received_ref.shape[0]
    levels, rows, nlon = control_ref.shape
    ext = rows + 2 * SUB
    halves = nlon // LANES
    refs = {"coefs": coefs_ref, "obs_weight": weight_ref, "innovation": innov_ref}
    own = slice(SUB, SUB + rows)

    sums_ref[...] = jnp.zeros_like(sums_ref)
    for d in range(tiles):
        sums_ref[level_ref[d]] += received_ref[d]

    row = sublane((SUB, nlon))
    mine = (sublane((ext, nlon)) >= SUB) & (sublane((ext, nlon)) < SUB + rows)

    def low_rows(g, at, count):
        start = max(at + count - SUB, 0)
        block = low_ref[g, start : start + SUB, :]
        shift = SUB - (at + count - start)
        return pltpu.roll(block, shift, 0) if shift else block

    def high_rows(g, at):
        start = min(at, PACKED - SUB)
        block = high_ref[g, start : start + SUB, :]
        return pltpu.roll(block, SUB - (at - start), 0) if at > start else block

    def level(g, i):
        l = g * GROUP + i
        fields = {}
        at = i * LEVEL_ROWS
        for name, k, count in packed_fields():
            centre = scale_ref[l] * control_ref[l] if name == "static" else refs[name][k, l]
            fields[name, k] = jnp.concatenate(
                [low_rows(g, at, count), centre, high_rows(g, at)], axis=0
            )
            at += count
        c0, c1, c2, c3 = (fields["coefs", k] for k in range(4))
        rest = 1.0 - (c0 + c1 + c2 + c3)

        sums = []
        for h in range(halves):
            edge = sums_ref[l, halves * rows + h * SUB : halves * rows + (h + 1) * SUB, :]
            sums.append(
                jnp.concatenate([edge, sums_ref[l, h * rows : (h + 1) * rows, :], edge], axis=0)
            )
        state = fields["static", 0] + jnp.concatenate(sums, axis=1)
        weighted = []
        for section in range(STEPS):
            state = (
                rest * state
                + c0 * pltpu.roll(state, ext - 1, 0)
                + c1 * pltpu.roll(state, 1, 0)
                + c2 * pltpu.roll(state, nlon - 1, 1)
                + c3 * pltpu.roll(state, 1, 1)
            )
            if section < SPILL:
                value = weight_ref[section, l] * (state[own] - innov_ref[section, l])
                edge = jnp.zeros((SUB, nlon), jnp.float32)
                value = jnp.concatenate([edge, value, edge], axis=0)
            else:
                value = fields["obs_weight", section] * (state - fields["innovation", section])
            weighted.append(value)
        adjoint = weighted[STEPS - 1]
        for left in range(STEPS - 1, -1, -1):
            if left + 1 == SPILL:
                adjoint = jnp.where(mine, adjoint, 0.0)
            adjoint = (
                rest * adjoint
                + pltpu.roll(c0 * adjoint, 1, 0)
                + pltpu.roll(c1 * adjoint, ext - 1, 0)
                + pltpu.roll(c2 * adjoint, 1, 1)
                + pltpu.roll(c3 * adjoint, nlon - 1, 1)
            )
            if left > 0:
                adjoint = adjoint + weighted[left - 1]
        grad_ref[l, 0:rows, :] = adjoint[own]
        spilled = jnp.where(row < SPILL, adjoint[SUB + rows :], adjoint[:SUB])
        grad_ref[l, rows : rows + SUB, :] = spilled
        up_ref[g, i * SPILL : (i + 1) * SPILL, :] = spilled[0:SPILL]
        down_ref[g, i * SPILL : (i + 1) * SPILL, :] = spilled[SUB - SPILL :]

    def group(g, carry):
        for i in range(GROUP):
            level(g, i)
        return carry

    lax.fori_loop(0, levels // GROUP, group, 0)
    half_row = sublane((SUB, LANES))
    for e in range(tiles):
        at = level_ref[e]
        spilled = None
        for h in range(halves):
            lanes = slice(h * LANES, (h + 1) * LANES)
            send_ref[e, h * rows : (h + 1) * rows, :] = grad_ref[at, 0:rows, lanes]
            block = grad_ref[at, rows : rows + SUB, lanes]
            if h % 2 == 0:
                spilled = block
            if h % 2 == 1 or h == halves - 1:
                if h % 2 == 1:
                    spilled = jnp.where(half_row < SPILL, spilled, jnp.where(
                        half_row >= SUB - SPILL, spilled, jnp.where(
                            half_row < 2 * SPILL, pltpu.roll(block, SPILL, 0),
                            pltpu.roll(block, SUB - SPILL, 0))))
                start = halves * rows + h // 2 * SUB
                send_ref[e, start : start + SUB, :] = spilled


def member_update_kernel(
    lat_ref,
    lon_ref,
    perts_ref,
    incoming_ref,
    control_ref,
    low_ref,
    high_ref,
    tile_grad_ref,
    static_ref,
    scale_ref,
    out_ref,
    static_out_ref,
    field_ref,
):
    tiles = incoming_ref.shape[0]
    blocks, nlat, nlon = control_ref.shape
    rows = nlat // tiles
    halves = nlon // LANES
    half_row = sublane((SUB, LANES))
    for h in range(halves):
        lanes = slice(h * LANES, (h + 1) * LANES)
        start = halves * rows + h // 2 * SUB
        place = h % 2 * SPILL

        def spill(s, above):
            block = incoming_ref[s, start : start + SUB, :]
            if place:
                block = pltpu.roll(block, SUB - place if above else place, 0)
            keep = half_row < SPILL if above else half_row >= SUB - SPILL
            return jnp.where(keep, block, 0.0)

        for s in range(tiles):
            piece = incoming_ref[s, h * rows : (h + 1) * rows, :]
            parts = [piece[t * SUB : (t + 1) * SUB] for t in range(rows // SUB)]
            if s > 0:
                parts[0] = parts[0] + spill(s - 1, True)
            if s < tiles - 1:
                parts[-1] = parts[-1] + spill(s + 1, False)
            field_ref[s * rows : (s + 1) * rows, lanes] = jnp.concatenate(parts, axis=0)
    for b in range(blocks):
        weighted = (perts_ref[b].astype(jnp.float32) * field_ref[...]).astype(jnp.bfloat16)
        adjoint_lat = lax.dot_general(
            lat_ref[...], weighted, (((0,), (0,)), ((), ())), preferred_element_type=jnp.float32
        ).astype(jnp.bfloat16)
        member_grad = jnp.dot(adjoint_lat, lon_ref[...], preferred_element_type=jnp.float32)
        control = control_ref[b]
        out_ref[b] = control - STEP_SIZE * (control + member_grad)

    row = sublane((SUB, nlon))
    for l in range(static_ref.shape[0]):
        at = l % GROUP * SPILL
        block = low_ref[l // GROUP, 0:SUB, :]
        above = jnp.where(row < SPILL, pltpu.roll(block, SUB - at, 0) if at else block, 0.0)
        block = high_ref[l // GROUP, 0:SUB, :]
        shift = (SUB - SPILL - at) % SUB
        below = jnp.where(
            row >= SUB - SPILL, pltpu.roll(block, shift, 0) if shift else block, 0.0
        )
        parts = [tile_grad_ref[l, t * SUB : (t + 1) * SUB, :] for t in range(rows // SUB)]
        parts[0] = parts[0] + above
        parts[-1] = parts[-1] + below
        gradient = jnp.concatenate(parts, axis=0)
        static = static_ref[l]
        static_out_ref[l] = static - STEP_SIZE * (static + scale_ref[l] * gradient)


def whole_local(
    level_map, loc_lat, loc_lon, ens_perts, ens_control,
    static_control, static_scale, coefs, obs_weight, innovation,
):
    tiles = lax.axis_size("tile")
    levels, rows, nlon = static_control.shape
    halves = nlon // LANES
    forward = [(i, i + 1) for i in range(tiles - 1)]
    backward = [(target, source) for source, target in forward]

    def array(*shape):
        return jax.ShapeDtypeStruct(shape, jnp.float32)

    first_shape = (tiles, halves * (rows + SUB), LANES)
    pieces = pl.pallas_call(
        lambda *refs: member_sum_kernel(tiles, *refs),
        out_shape=array(*first_shape),
        in_specs=vmem(4),
        out_specs=vmem(1)[0],
        name="member_sum",
    )(loc_lat, loc_lon, ens_perts, ens_control)
    received = lax.all_to_all(pieces, "tile", split_axis=0, concat_axis=0, tiled=True)

    packed = array(levels // GROUP, PACKED, nlon)
    up, down = pl.pallas_call(
        pack_kernel,
        out_shape=(packed, packed),
        in_specs=vmem(5),
        out_specs=tuple(vmem(2)),
        compiler_params=params(8),
        name="pack",
    )(static_control, static_scale, coefs, obs_weight, innovation)
    low = lax.ppermute(up, "tile", forward)
    high = lax.ppermute(down, "tile", backward)

    spilled = array(levels // GROUP, GROUP * SPILL, nlon)
    send, tile_grad, up, down = pl.pallas_call(
        window_kernel,
        out_shape=(
            array(tiles, halves * rows + -(-halves // 2) * SUB, LANES),
            array(levels, rows + SUB, nlon),
            spilled,
            spilled,
        ),
        in_specs=[pl.BlockSpec(memory_space=pltpu.SMEM)] + vmem(8),
        out_specs=tuple(vmem(4)),
        scratch_shapes=[pltpu.VMEM((levels,) + first_shape[1:], jnp.float32)],
        compiler_params=params(8),
        name="window",
    )(level_map, received, low, high, static_control, static_scale, coefs, obs_weight, innovation)
    incoming = lax.all_to_all(send, "tile", split_axis=0, concat_axis=0, tiled=True)
    low = lax.ppermute(up, "tile", forward)
    high = lax.ppermute(down, "tile", backward)

    return pl.pallas_call(
        member_update_kernel,
        out_shape=(array(*ens_control.shape), array(*static_control.shape)),
        in_specs=vmem(10),
        out_specs=tuple(vmem(2)),
        scratch_shapes=[pltpu.VMEM(ens_control.shape[1:], jnp.float32)],
        compiler_params=params(8),
        name="member_update",
    )(
        loc_lat, loc_lon, ens_perts, incoming, ens_control,
        low, high, tile_grad, static_control, static_scale,
    )


def exchanged(block, axis):
    count = lax.axis_size("tile")
    forward = [(i, i + 1) for i in range(count - 1)]
    backward = [(target, source) for source, target in forward]
    last = block.shape[axis] - 1
    low = lax.ppermute(lax.slice_in_dim(block, last, last + 1, axis=axis), "tile", forward)
    high = lax.ppermute(lax.slice_in_dim(block, 0, 1, axis=axis), "tile", backward)
    return jnp.concatenate([low, block, high], axis=axis)


def forward_step(state, coeffs):
    padded = exchanged(state, 1)
    return (
        state
        + coeffs[0] * (padded[:, 2:] - state)
        + coeffs[1] * (padded[:, :-2] - state)
        + coeffs[2] * (jnp.roll(state, -1, 2) - state)
        + coeffs[3] * (jnp.roll(state, 1, 2) - state)
    )


def adjoint_step(adjoint, coeffs):
    coef_sum = coeffs[0] + coeffs[1] + coeffs[2] + coeffs[3]
    padded = exchanged(jnp.stack([coeffs[0] * adjoint, coeffs[1] * adjoint]), 2)
    return (
        (1.0 - coef_sum) * adjoint
        + padded[0][:, :-2]
        + padded[1][:, 2:]
        + jnp.roll(coeffs[2] * adjoint, 1, 2)
        + jnp.roll(coeffs[3] * adjoint, -1, 2)
    )


def any_local(
    level_map, loc_lat, loc_lon, ens_perts, ens_control,
    static_control, static_scale, coefs, obs_weight, innovation,
):
    tiles = lax.axis_size("tile")
    level_ids = jnp.arange(static_control.shape[0], dtype=jnp.int32)
    level_onehot = (level_map[:, None] == level_ids[None, :]).astype(jnp.float32)
    lat_smoothed = jnp.einsum(
        "ij,bjk->bik", loc_lat, ens_control.astype(jnp.bfloat16),
        preferred_element_type=jnp.float32,
    ).astype(jnp.bfloat16)
    member_field = jnp.einsum(
        "bij,kj->bik", lat_smoothed, loc_lon, preferred_element_type=jnp.float32
    )
    partial_value = jnp.sum(ens_perts.astype(jnp.float32) * member_field, axis=0)
    pieces = partial_value.reshape(tiles, -1, partial_value.shape[1])
    received = lax.all_to_all(pieces, "tile", split_axis=0, concat_axis=0, tiled=True)
    ens_incr = jnp.einsum("dl,dij->lij", level_onehot, received, precision=lax.Precision.HIGHEST)
    state = static_scale * static_control + ens_incr
    weighted = []
    for section in range(STEPS):
        state = forward_step(state, coefs)
        weighted.append(obs_weight[section] * (state - innovation[section]))
    adjoint = weighted[STEPS - 1]
    for section in range(STEPS - 2, -1, -1):
        adjoint = adjoint_step(adjoint, coefs) + weighted[section]
    gradient = adjoint_step(adjoint, coefs)
    static_final = static_control - STEP_SIZE * (static_control + static_scale * gradient)
    outgoing = jnp.take(gradient, level_map, axis=0)
    incoming = lax.all_to_all(outgoing, "tile", split_axis=0, concat_axis=0, tiled=True)
    grad_field = incoming.reshape(-1, incoming.shape[2])
    weighted_grad = (ens_perts.astype(jnp.float32) * grad_field[None]).astype(jnp.bfloat16)
    adjoint_lat = jnp.einsum(
        "ji,bjk->bik", loc_lat, weighted_grad, preferred_element_type=jnp.float32
    ).astype(jnp.bfloat16)
    member_grad = jnp.einsum("bij,jk->bik", adjoint_lat, loc_lon, preferred_element_type=jnp.float32)
    return ens_control - STEP_SIZE * (ens_control + member_grad), static_final


def local(*args):
    levels, rows, nlon = args[5].shape
    whole = rows % SUB == 0 and nlon % LANES == 0 and levels % GROUP == 0
    return (whole_local if whole else any_local)(*args)


def solution(mesh):
    in_specs = (
        P(),
        P(),
        P(),
        P(("groups", "tile"), None, None),
        P(("groups", "tile"), None, None),
        P("groups", "tile", None),
        P("groups", "tile", None),
        P(None, "groups", "tile", None),
        P(None, "groups", "tile", None),
        P(None, "groups", "tile", None),
    )
    out_specs = (P(("groups", "tile"), None, None), P("groups", "tile", None))
    return jax.shard_map(local, mesh=mesh, in_specs=in_specs, out_specs=out_specs, check_vma=False)
```

time: 54.2 us -> 43 us (0.79)
  Pallas kernels: 13.3 us -> 6.31 us
  waiting for transfers between devices: 16.4 us -> 11.5 us
  starting transfers between devices: 19.9 us -> 23.6 us
  local copies, waits for them, and re-layouts: 2.22 us -> 0.04 us
  other arithmetic: 0.69 us -> 0 us
    pallas_call x4, Pallas kernels: 13.3 us -> 6.31 us  [the longest x1 2.84 us: whole_local(): pl.pallas_call(window_kernel, out_shape=(array(tiles, halves * rows + -(-...]
    ppermute x2 -> x4, starting transfers between devices: 5.45 us -> 10.9 us  [the longest x2 7.07 us: whole_local(): low = lax.ppermute(up, 'tile', forward)]
    all_to_all x2, waiting for transfers between devices: 8.81 us -> 3.35 us  [the longest x1 2.17 us: whole_local(): lax.all_to_all(send, 'tile', split_axis=0, concat_axis=0, tiled=True)]
    unnamed x14 -> x20, local copies, waits for them, and re-layouts: 2.22 us -> 0.04 us
    all_to_all x2, starting transfers between devices: 14.4 us -> 12.7 us  [the longest x1 7.45 us: whole_local(): lax.all_to_all(pieces, 'tile', split_axis=0, concat_axis=0, tiled=True)]
    sub x1 -> x0, other arithmetic: 0.69 us -> none  [tall_local(): static_control - STEP_SIZE * (static_control + static_scale * gradient)]
    ppermute x2 -> x4, waiting for transfers between devices: 7.59 us -> 8.17 us  [the longest x2 6.71 us: whole_local(): high = lax.ppermute(down, 'tile', backward)]
  transfers between devices with their start and end apart: 4 -> 6, of which waited for: 3 -> 5; matrix products, arithmetic and copies ran while one was open for 1% -> 0% of each run, Pallas kernels for 5% -> 0%
where the time goes in v3:
time: 43 us; the launch traced here: 42.2 us
  starting transfers between devices  23.6 us (55%)
  waiting for transfers between devices  11.5 us (27%)
  Pallas kernels  6.31 us (15%)
  between operations  0.76 us (2%)
    all_to_all x1, starting transfers between devices, whole_local(): lax.all_to_all(pieces, 'tile', split_axis=0, concat_axis=0, tiled=True)  7.45 us
    ppermute x2, starting transfers between devices, whole_local(): low = lax.ppermute(up, 'tile', forward)  7.07 us
    ppermute x2, waiting for transfers between devices, whole_local(): high = lax.ppermute(down, 'tile', backward)  6.71 us
    all_to_all x1, starting transfers between devices, whole_local(): lax.all_to_all(send, 'tile', split_axis=0, concat_axis=0, tiled=True)  5.24 us
    ppermute x2, starting transfers between devices, whole_local(): high = lax.ppermute(down, 'tile', backward)  3.84 us
    pallas_call x1, Pallas kernels, whole_local(): pl.pallas_call(window_kernel, out_shape=(array(tiles, halves * rows + -(-...  2.84 us
    pallas_call x1, Pallas kernels, whole_local(): pl.pallas_call(lambda *refs: member_sum_kernel(tiles, *refs), out_shape=a...  2.29 us
    all_to_all x1, waiting for transfers between devices, whole_local(): lax.all_to_all(send, 'tile', split_axis=0, concat_axis=0, tiled=True)  2.17 us
  transfers between devices with their start and end apart: 6, of which 5 were waited for; matrix products, arithmetic and copies ran while one was open for 0% of the time, Pallas kernels for 0%

profile of v3, /device:TPU:1, one launch (start us, length us, event | category | flops | bytes accessed | tf_op | source)
XLA Modules:
  0.0 42.2 jit_solution(9517842377628419994)
XLA Ops:
  0.6 0.0 copy-start.1
  0.6 0.0 copy-start.2
  0.6 2.3 %member_sum.1 = f32[16,48,128]{2,1,0:T(8,128)} custom-call(bf16[256,256]{1,0:T(8,128)(2,1)} %lat_ref.1, bf16[256,256]{1,0:T(8,128)(2,1)} %lon_ref.1, bf16[1,256,256]{2,1,0:T(8,128)(2,1)} %perts_ref.1, f32[1,256,256]{2,1,0:T(8,128)} %control_ref.5), custom_call_target="tpu_custom_call" | custom-call | tf_op jit(solution)/shard_map/member_sum/pallas_call | solution.py:289
  2.9 0.0 copy-start
  2.9 0.0 copy-start.3
  2.9 0.0 copy-start.4
  3.0 7.4 %all-to-all-start = ((f32[16,48,128]{2,1,0:T(8,128)}), f32[16,48,128]{2,1,0:T(8,128)S(1)}, u32[]{:S(2)}, u32[]{:S(2)}) async-start(f32[16,48,128]{2,1,0:T(8,128)} %member_sum.1), calls=%async_computation | async-start | bytes 786432 | tf_op jit(solution)/shard_map/all_to_all | solution.py:296
  10.4 0.0 copy-done.1
  10.4 0.0 copy-done.2
  10.4 0.0 copy-done
  10.4 0.0 copy-done.3
  10.4 0.0 copy-done.4
  10.4 0.1 pack.1
  10.6 0.0 copy-start.9
  10.6 3.5 %collective-permute-start = (f32[2,72,256]{2,1,0:T(8,128)S(1)}, f32[2,72,256]{2,1,0:T(8,128)S(1)}, u32[]{:S(2)}, u32[]{:S(2)}) collective-permute-start(f32[2,72,256]{2,1,0:T(8,128)S(1)} %get-tuple-element.8), channel_id=1, source_target_pairs={{0,1},{1,2},{2,3},{3,4},{4,5},{5,6},{6,7},{7,8},{8,9},{9,10},{10,1... | collective-permute-start | bytes 442376 | tf_op jit(solution)/shard_map/ppermute | solution.py:307
  14.1 1.9 %collective-permute-start.1 = (f32[2,72,256]{2,1,0:T(8,128)S(1)}, f32[2,72,256]{2,1,0:T(8,128)S(1)}, u32[]{:S(2)}, u32[]{:S(2)}) collective-permute-start(f32[2,72,256]{2,1,0:T(8,128)S(1)} %get-tuple-element.9), channel_id=1, source_target_pairs={{1,0},{2,1},{3,2},{4,3},{5,4},{6,5},{7,6},{8,7},{9,8},{10,9},{11,1... | collective-permute-start | bytes 442376 | tf_op jit(solution)/shard_map/ppermute | solution.py:308
  16.0 1.5 %collective-permute-done.low_ref = f32[2,72,256]{2,1,0:T(8,128)S(1)} collective-permute-done((f32[2,72,256]{2,1,0:T(8,128)S(1)}, f32[2,72,256]{2,1,0:T(8,128)S(1)}, u32[]{:S(2)}, u32[]{:S(2)}) %collective-permute-start) | collective-permute-done | bytes 147488 | tf_op jit(solution)/shard_map/ppermute | solution.py:307
  17.5 3.6 %collective-permute-done.1.high_ref = f32[2,72,256]{2,1,0:T(8,128)S(1)} collective-permute-done((f32[2,72,256]{2,1,0:T(8,128)S(1)}, f32[2,72,256]{2,1,0:T(8,128)S(1)}, u32[]{:S(2)}, u32[]{:S(2)}) %collective-permute-start.1) | collective-permute-done | bytes 147488 | tf_op jit(solution)/shard_map/ppermute | solution.py:308
  21.1 1.2 %all-to-all-done.received_ref = f32[16,48,128]{2,1,0:T(8,128)S(1)} async-done(((f32[16,48,128]{2,1,0:T(8,128)}), f32[16,48,128]{2,1,0:T(8,128)S(1)}, u32[]{:S(2)}, u32[]{:S(2)}) %all-to-all-start) | async-done | bytes 393248 | tf_op jit(solution)/shard_map/all_to_all | solution.py:296
  22.3 0.0 copy-done.9
  22.3 2.8 %window.1 = (f32[16,40,128]{2,1,0:T(8,128)}, f32[8,24,256]{2,1,0:T(8,128)S(1)}, f32[2,8,256]{2,1,0:T(8,128)S(1)}, f32[2,8,256]{2,1,0:T(8,128)S(1)}) custom-call(s32[16]{0:T(128)S(1)} %copy-done.9, f32[16,48,128]{2,1,0:T(8,128)S(1)} %all-to-all-done.received_ref, f32[2,72,256]{2,1,0:T(8,128)S(1)} %collective-permute-done.low_ref, ...), custom_call_target="tpu_custom_call" | custom-call | tf_op jit(solution)/shard_map/window/pallas_call | solution.py:311
  25.1 0.0 copy-start.5
  25.1 0.0 copy-start.6
  25.1 0.0 copy-start.7
  25.1 0.0 copy-start.8
  25.1 5.2 %all-to-all-start.1 = ((f32[16,40,128]{2,1,0:T(8,128)}), f32[16,40,128]{2,1,0:T(8,128)S(1)}, u32[]{:S(2)}, u32[]{:S(2)}) async-start(f32[16,40,128]{2,1,0:T(8,128)} %get-tuple-element.10), calls=%async_computation.1 | async-start | bytes 655360 | tf_op jit(solution)/shard_map/all_to_all | solution.py:325
  30.4 3.5 %collective-permute-start.2 = (f32[2,8,256]{2,1,0:T(8,128)S(1)}, f32[2,8,256]{2,1,0:T(8,128)S(1)}, u32[]{:S(2)}, u32[]{:S(2)}) collective-permute-start(f32[2,8,256]{2,1,0:T(8,128)S(1)} %get-tuple-element.11), channel_id=1, source_target_pairs={{0,1},{1,2},{2,3},{3,4},{4,5},{5,6},{6,7},{7,8},{8,9},{9,10},{10,1... | collective-permute-start | bytes 49160 | tf_op jit(solution)/shard_map/ppermute | solution.py:326
  33.9 1.9 %collective-permute-start.3 = (f32[2,8,256]{2,1,0:T(8,128)S(1)}, f32[2,8,256]{2,1,0:T(8,128)S(1)}, u32[]{:S(2)}, u32[]{:S(2)}) collective-permute-start(f32[2,8,256]{2,1,0:T(8,128)S(1)} %get-tuple-element.12), channel_id=1, source_target_pairs={{1,0},{2,1},{3,2},{4,3},{5,4},{6,5},{7,6},{8,7},{9,8},{10,9},{11,1... | collective-permute-start | bytes 49160 | tf_op jit(solution)/shard_map/ppermute | solution.py:327
  35.8 0.0 collective-permute-done.2.low_ref
  35.8 3.1 %collective-permute-done.3.high_ref = f32[2,8,256]{2,1,0:T(8,128)S(1)} collective-permute-done((f32[2,8,256]{2,1,0:T(8,128)S(1)}, f32[2,8,256]{2,1,0:T(8,128)S(1)}, u32[]{:S(2)}, u32[]{:S(2)}) %collective-permute-start.3) | collective-permute-done | bytes 16416 | tf_op jit(solution)/shard_map/ppermute | solution.py:327
  39.0 2.2 %all-to-all-done.1.incoming_ref = f32[16,40,128]{2,1,0:T(8,128)S(1)} async-done(((f32[16,40,128]{2,1,0:T(8,128)}), f32[16,40,128]{2,1,0:T(8,128)S(1)}, u32[]{:S(2)}, u32[]{:S(2)}) %all-to-all-start.1) | async-done | bytes 327712 | tf_op jit(solution)/shard_map/all_to_all | solution.py:325
  41.1 0.0 copy-done.5
  41.1 0.0 copy-done.6
  41.1 0.0 copy-done.7
  41.1 0.0 copy-done.8
  41.1 1.1 %member_update.1 = (f32[1,256,256]{2,1,0:T(8,128)}, f32[8,16,256]{2,1,0:T(8,128)}) custom-call(bf16[256,256]{1,0:T(8,128)(2,1)S(1)} %copy-done.6, bf16[256,256]{1,0:T(8,128)(2,1)S(1)} %copy-done.7, bf16[1,256,256]{2,1,0:T(8,128)(2,1)S(1)} %copy-done.8, f32[16,40,128]{2,1,0:T(8,128)S(1)} %all-to-all-done.1.incoming_ref, f32[1,256,256]{2,1,0:T(8,128)S(1)} %copy-done.5, ...), custom_call_target="tpu_custom_call" | custom-call | tf_op jit(solution)/shard_map/member_update/pallas_call | solution.py:329
Async XLA Ops:
  0.6 9.8 %copy-start.1 = (f32[3,8,16,256]{3,2,1,0:T(8,128)S(1)}, f32[3,8,16,256]{3,2,1,0:T(8,128)}, u32[]{:S(2)}) copy-start(f32[3,8,16,256]{3,2,1,0:T(8,128)} %weight_ref.3) | copy-start | bytes 1179652
  0.6 9.8 %copy-start.2 = (f32[3,8,16,256]{3,2,1,0:T(8,128)S(1)}, f32[3,8,16,256]{3,2,1,0:T(8,128)}, u32[]{:S(2)}) copy-start(f32[3,8,16,256]{3,2,1,0:T(8,128)} %innov_ref.3) | copy-start | bytes 1179652
  2.9 7.5 %copy-start = (f32[4,8,16,256]{3,2,1,0:T(8,128)S(1)}, f32[4,8,16,256]{3,2,1,0:T(8,128)}, u32[]{:S(2)}) copy-start(f32[4,8,16,256]{3,2,1,0:T(8,128)} %coefs_ref.3) | copy-start | bytes 1572868
  2.9 7.5 %copy-start.3 = (f32[8,16,256]{2,1,0:T(8,128)S(1)}, f32[8,16,256]{2,1,0:T(8,128)}, u32[]{:S(2)}) copy-start(f32[8,16,256]{2,1,0:T(8,128)} %static_ref.1) | copy-start | bytes 393220
  2.9 7.5 %copy-start.4 = (f32[8,16,256]{2,1,0:T(8,128)S(1)}, f32[8,16,256]{2,1,0:T(8,128)}, u32[]{:S(2)}) copy-start(f32[8,16,256]{2,1,0:T(8,128)} %scale_ref.5) | copy-start | bytes 393220
  3.0 19.3 %all-to-all-start = ((f32[16,48,128]{2,1,0:T(8,128)}), f32[16,48,128]{2,1,0:T(8,128)S(1)}, u32[]{:S(2)}, u32[]{:S(2)}) async-start(f32[16,48,128]{2,1,0:T(8,128)} %member_sum.1), calls=%async_computation | async-start | bytes 786432 | tf_op jit(solution)/shard_map/all_to_all | solution.py:296
  10.6 11.7 %copy-start.9 = (s32[16]{0:T(128)S(1)}, s32[16]{0:T(128)}, u32[]{:S(2)}) copy-start(s32[16]{0:T(128)} %level_ref.1) | copy-start | bytes 196
  10.6 6.9 %collective-permute-start = (f32[2,72,256]{2,1,0:T(8,128)S(1)}, f32[2,72,256]{2,1,0:T(8,128)S(1)}, u32[]{:S(2)}, u32[]{:S(2)}) collective-permute-start(f32[2,72,256]{2,1,0:T(8,128)S(1)} %get-tuple-element.8), channel_id=1, source_target_pairs={{0,1},{1,2},{2,3},{3,4},{4,5},{5,6},{6,7},{7,8},{8,9},{9,10},{10,1... | collective-permute-start | bytes 442376 | tf_op jit(solution)/shard_map/ppermute | solution.py:307
  14.1 7.0 %collective-permute-start.1 = (f32[2,72,256]{2,1,0:T(8,128)S(1)}, f32[2,72,256]{2,1,0:T(8,128)S(1)}, u32[]{:S(2)}, u32[]{:S(2)}) collective-permute-start(f32[2,72,256]{2,1,0:T(8,128)S(1)} %get-tuple-element.9), channel_id=1, source_target_pairs={{1,0},{2,1},{3,2},{4,3},{5,4},{6,5},{7,6},{8,7},{9,8},{10,9},{11,1... | collective-permute-start | bytes 442376 | tf_op jit(solution)/shard_map/ppermute | solution.py:308
  25.1 16.0 %copy-start.5 = (f32[1,256,256]{2,1,0:T(8,128)S(1)}, f32[1,256,256]{2,1,0:T(8,128)}, u32[]{:S(2)}) copy-start(f32[1,256,256]{2,1,0:T(8,128)} %control_ref.5) | copy-start | bytes 786436
  25.1 16.0 %copy-start.6 = (bf16[256,256]{1,0:T(8,128)(2,1)S(1)}, bf16[256,256]{1,0:T(8,128)(2,1)}, u32[]{:S(2)}) copy-start(bf16[256,256]{1,0:T(8,128)(2,1)} %lat_ref.1) | copy-start | bytes 393220
  25.1 16.0 %copy-start.7 = (bf16[256,256]{1,0:T(8,128)(2,1)S(1)}, bf16[256,256]{1,0:T(8,128)(2,1)}, u32[]{:S(2)}) copy-start(bf16[256,256]{1,0:T(8,128)(2,1)} %lon_ref.1) | copy-start | bytes 393220
  25.1 16.0 %copy-start.8 = (bf16[1,256,256]{2,1,0:T(8,128)(2,1)S(1)}, bf16[1,256,256]{2,1,0:T(8,128)(2,1)}, u32[]{:S(2)}) copy-start(bf16[1,256,256]{2,1,0:T(8,128)(2,1)} %perts_ref.1) | copy-start | bytes 393220
  25.1 16.0 %all-to-all-start.1 = ((f32[16,40,128]{2,1,0:T(8,128)}), f32[16,40,128]{2,1,0:T(8,128)S(1)}, u32[]{:S(2)}, u32[]{:S(2)}) async-start(f32[16,40,128]{2,1,0:T(8,128)} %get-tuple-element.10), calls=%async_computation.1 | async-start | bytes 655360 | tf_op jit(solution)/shard_map/all_to_all | solution.py:325
  30.4 5.5 %collective-permute-start.2 = (f32[2,8,256]{2,1,0:T(8,128)S(1)}, f32[2,8,256]{2,1,0:T(8,128)S(1)}, u32[]{:S(2)}, u32[]{:S(2)}) collective-permute-start(f32[2,8,256]{2,1,0:T(8,128)S(1)} %get-tuple-element.11), channel_id=1, source_target_pairs={{0,1},{1,2},{2,3},{3,4},{4,5},{5,6},{6,7},{7,8},{8,9},{9,10},{10,1... | collective-permute-start | bytes 49160 | tf_op jit(solution)/shard_map/ppermute | solution.py:326
  33.9 5.1 %collective-permute-start.3 = (f32[2,8,256]{2,1,0:T(8,128)S(1)}, f32[2,8,256]{2,1,0:T(8,128)S(1)}, u32[]{:S(2)}, u32[]{:S(2)}) collective-permute-start(f32[2,8,256]{2,1,0:T(8,128)S(1)} %get-tuple-element.12), channel_id=1, source_target_pairs={{1,0},{2,1},{3,2},{4,3},{5,4},{6,5},{7,6},{8,7},{9,8},{10,9},{11,1... | collective-permute-start | bytes 49160 | tf_op jit(solution)/shard_map/ppermute | solution.py:327

commit v4 on v3

--- a/solution.py
+++ b/solution.py
@@ -33,6 +33,10 @@
 
 def params(mebibytes):
     return pltpu.CompilerParams(vmem_limit_bytes=mebibytes << 20)
+
+
+def order(tiles):
+    return [(2 * tiles // 3 + 1 - position) % tiles for position in range(tiles)]
 
 
 def sublane(shape):
@@ -55,10 +59,11 @@
         total = term if total is None else total + term
     first = sublane((SUB, LANES)) < HALO
     edge = jnp.zeros((SUB, LANES), jnp.float32)
-    for e in range(tiles):
+    for e, tile in enumerate(order(tiles)):
+        start = tile * rows
+        end = start + rows
         for h in range(halves):
             lanes = slice(h * LANES, (h + 1) * LANES)
-            start, end = e * rows, (e + 1) * rows
             above = total[end : end + SUB, lanes] if end < nlat else edge
             below = total[start - SUB : start, lanes] if start > 0 else edge
             out_ref[e, h * rows : (h + 1) * rows, :] = total[start:end, lanes]
@@ -101,17 +106,15 @@
 ):
     tiles = received_ref.shape[0]
     levels, rows, nlon = control_ref.shape
-    ext = rows + 2 * SUB
+    ring = rows + SUB
     halves = nlon // LANES
     refs = {"coefs": coefs_ref, "obs_weight": weight_ref, "innovation": innov_ref}
-    own = slice(SUB, SUB + rows)
 
     sums_ref[...] = jnp.zeros_like(sums_ref)
-    for d in range(tiles):
-        sums_ref[level_ref[d]] += received_ref[d]
-
-    row = sublane((SUB, nlon))
-    mine = (sublane((ext, nlon)) >= SUB) & (sublane((ext, nlon)) < SUB + rows)
+    for d, tile in enumerate(order(tiles)):
+        sums_ref[level_ref[tile]] += received_ref[d]
+
+    above = sublane((SUB, nlon)) < HALO
 
     def low_rows(g, at, count):
         start = max(at + count - SUB, 0)
@@ -129,55 +132,60 @@
         fields = {}
         at = i * LEVEL_ROWS
         for name, k, count in packed_fields():
-            centre = scale_ref[l] * control_ref[l] if name == "static" else refs[name][k, l]
-            fields[name, k] = jnp.concatenate(
-                [low_rows(g, at, count), centre, high_rows(g, at)], axis=0
-            )
+            inner = scale_ref[l] * control_ref[l] if name == "static" else refs[name][k, l]
+            edge = jnp.where(above, high_rows(g, at), low_rows(g, at, count))
+            fields[name, k] = jnp.concatenate([inner, edge], axis=0)
             at += count
         c0, c1, c2, c3 = (fields["coefs", k] for k in range(4))
         rest = 1.0 - (c0 + c1 + c2 + c3)
 
         sums = []
         for h in range(halves):
-            edge = sums_ref[l, halves * rows + h * SUB : halves * rows + (h + 1) * SUB, :]
+            edge = halves * rows + h * SUB
             sums.append(
-                jnp.concatenate([edge, sums_ref[l, h * rows : (h + 1) * rows, :], edge], axis=0)
+                jnp.concatenate(
+                    [sums_ref[l, h * rows : (h + 1) * rows, :], sums_ref[l, edge : edge + SUB, :]],
+                    axis=0,
+                )
             )
         state = fields["static", 0] + jnp.concatenate(sums, axis=1)
         weighted = []
         for section in range(STEPS):
             state = (
                 rest * state
-                + c0 * pltpu.roll(state, ext - 1, 0)
+                + c0 * pltpu.roll(state, ring - 1, 0)
                 + c1 * pltpu.roll(state, 1, 0)
                 + c2 * pltpu.roll(state, nlon - 1, 1)
                 + c3 * pltpu.roll(state, 1, 1)
             )
             if section < SPILL:
-                value = weight_ref[section, l] * (state[own] - innov_ref[section, l])
-                edge = jnp.zeros((SUB, nlon), jnp.float32)
-                value = jnp.concatenate([edge, value, edge], axis=0)
+                weighted.append(weight_ref[section, l] * (state[:rows] - innov_ref[section, l]))
             else:
-                value = fields["obs_weight", section] * (state - fields["innovation", section])
-            weighted.append(value)
+                weighted.append(
+                    fields["obs_weight", section] * (state - fields["innovation", section])
+                )
         adjoint = weighted[STEPS - 1]
         for left in range(STEPS - 1, -1, -1):
             if left + 1 == SPILL:
-                adjoint = jnp.where(mine, adjoint, 0.0)
+                adjoint = jnp.concatenate(
+                    [adjoint[:rows], jnp.zeros((SUB, nlon), jnp.float32)], axis=0
+                )
             adjoint = (
                 rest * adjoint
                 + pltpu.roll(c0 * adjoint, 1, 0)
-                + pltpu.roll(c1 * adjoint, ext - 1, 0)
+                + pltpu.roll(c1 * adjoint, ring - 1, 0)
                 + pltpu.roll(c2 * adjoint, 1, 1)
                 + pltpu.roll(c3 * adjoint, nlon - 1, 1)
             )
-            if left > 0:
+            if left > SPILL:
                 adjoint = adjoint + weighted[left - 1]
-        grad_ref[l, 0:rows, :] = adjoint[own]
-        spilled = jnp.where(row < SPILL, adjoint[SUB + rows :], adjoint[:SUB])
-        grad_ref[l, rows : rows + SUB, :] = spilled
-        up_ref[g, i * SPILL : (i + 1) * SPILL, :] = spilled[0:SPILL]
-        down_ref[g, i * SPILL : (i + 1) * SPILL, :] = spilled[SUB - SPILL :]
+            elif left > 0:
+                adjoint = jnp.concatenate(
+                    [adjoint[:rows] + weighted[left - 1], adjoint[rows:]], axis=0
+                )
+        grad_ref[l] = adjoint
+        up_ref[g, i * SPILL : (i + 1) * SPILL, :] = adjoint[rows : rows + SPILL]
+        down_ref[g, i * SPILL : (i + 1) * SPILL, :] = adjoint[ring - SPILL :]
 
     def group(g, carry):
         for i in range(GROUP):
@@ -185,24 +193,23 @@
         return carry
 
     lax.fori_loop(0, levels // GROUP, group, 0)
-    half_row = sublane((SUB, LANES))
-    for e in range(tiles):
-        at = level_ref[e]
-        spilled = None
+    row = sublane((SUB, LANES))
+    for e, tile in enumerate(order(tiles)):
+        at = level_ref[tile]
+        for h in range(0, halves, 2):
+            spilled = grad_ref[at, rows:ring, h * LANES : (h + 1) * LANES]
+            if h + 1 < halves:
+                block = grad_ref[at, rows:ring, (h + 1) * LANES : (h + 2) * LANES]
+                middle = jnp.where(
+                    row < 2 * SPILL, pltpu.roll(block, SPILL, 0), pltpu.roll(block, SUB - SPILL, 0)
+                )
+                outer = (row < SPILL) | (row >= SUB - SPILL)
+                spilled = jnp.where(outer, spilled, middle)
+            start = halves * rows + h // 2 * SUB
+            send_ref[e, start : start + SUB, :] = spilled
         for h in range(halves):
             lanes = slice(h * LANES, (h + 1) * LANES)
             send_ref[e, h * rows : (h + 1) * rows, :] = grad_ref[at, 0:rows, lanes]
-            block = grad_ref[at, rows : rows + SUB, lanes]
-            if h % 2 == 0:
-                spilled = block
-            if h % 2 == 1 or h == halves - 1:
-                if h % 2 == 1:
-                    spilled = jnp.where(half_row < SPILL, spilled, jnp.where(
-                        half_row >= SUB - SPILL, spilled, jnp.where(
-                            half_row < 2 * SPILL, pltpu.roll(block, SPILL, 0),
-                            pltpu.roll(block, SUB - SPILL, 0))))
-                start = halves * rows + h // 2 * SUB
-                send_ref[e, start : start + SUB, :] = spilled
 
 
 def member_update_kernel(
@@ -225,20 +232,21 @@
     rows = nlat // tiles
     halves = nlon // LANES
     half_row = sublane((SUB, LANES))
+    position = {tile: p for p, tile in enumerate(order(tiles))}
     for h in range(halves):
         lanes = slice(h * LANES, (h + 1) * LANES)
         start = halves * rows + h // 2 * SUB
-        place = h % 2 * SPILL
+        inset = h % 2 * SPILL
 
         def spill(s, above):
-            block = incoming_ref[s, start : start + SUB, :]
-            if place:
-                block = pltpu.roll(block, SUB - place if above else place, 0)
+            block = incoming_ref[position[s], start : start + SUB, :]
+            if inset:
+                block = pltpu.roll(block, SUB - inset if above else inset, 0)
             keep = half_row < SPILL if above else half_row >= SUB - SPILL
             return jnp.where(keep, block, 0.0)
 
         for s in range(tiles):
-            piece = incoming_ref[s, h * rows : (h + 1) * rows, :]
+            piece = incoming_ref[position[s], h * rows : (h + 1) * rows, :]
             parts = [piece[t * SUB : (t + 1) * SUB] for t in range(rows // SUB)]
             if s > 0:
                 parts[0] = parts[0] + spill(s - 1, True)
@@ -282,6 +290,12 @@
     forward = [(i, i + 1) for i in range(tiles - 1)]
     backward = [(target, source) for source, target in forward]
 
+    def swapped(pieces):
+        return lax.all_to_all(
+            pieces, "tile", split_axis=0, concat_axis=0, tiled=True,
+            axis_index_groups=[order(tiles)],
+        )
+
     def array(*shape):
         return jax.ShapeDtypeStruct(shape, jnp.float32)
 
@@ -293,7 +307,7 @@
         out_specs=vmem(1)[0],
         name="member_sum",
     )(loc_lat, loc_lon, ens_perts, ens_control)
-    received = lax.all_to_all(pieces, "tile", split_axis=0, concat_axis=0, tiled=True)
+    received = swapped(pieces)
 
     packed = array(levels // GROUP, PACKED, nlon)
     up, down = pl.pallas_call(
@@ -322,7 +336,7 @@
         compiler_params=params(8),
         name="window",
     )(level_map, received, low, high, static_control, static_scale, coefs, obs_weight, innovation)
-    incoming = lax.all_to_all(send, "tile", split_axis=0, concat_axis=0, tiled=True)
+    incoming = swapped(send)
     low = lax.ppermute(up, "tile", forward)
     high = lax.ppermute(down, "tile", backward)
 

time: 43 us -> 38.8 us (0.902)
  waiting for transfers between devices: 11.5 us -> 9.25 us
  starting transfers between devices: 23.6 us -> 22.3 us
    all_to_all x2, waiting for transfers between devices: 3.35 us -> 0.29 us  [swapped(): lax.all_to_all(pieces, 'tile', split_axis=0, concat_axis=0, tiled=True, a...]
    ppermute x2, starting transfers between devices: 7.07 us -> 4.92 us  [whole_local(): low = lax.ppermute(up, 'tile', forward)]
    ppermute x2, waiting for transfers between devices: 6.71 us -> 7.89 us  [whole_local(): high = lax.ppermute(down, 'tile', backward)]
    all_to_all x2, starting transfers between devices: 12.7 us -> 13.5 us  [swapped(): lax.all_to_all(pieces, 'tile', split_axis=0, concat_axis=0, tiled=True, a...]
  transfers between devices with their start and end apart: 6 -> 6, of which waited for: 5 -> 4; matrix products, arithmetic and copies ran while one was open for 0% -> 0% of each run, Pallas kernels for 0% -> 0%
where the time goes in v4:
time: 38.8 us; the launch traced here: 38.3 us
  starting transfers between devices  22.3 us (57%)
  waiting for transfers between devices  9.25 us (24%)
  Pallas kernels  5.99 us (15%)
  between operations  0.76 us (2%)
    all_to_all x2, starting transfers between devices, swapped(): lax.all_to_all(pieces, 'tile', split_axis=0, concat_axis=0, tiled=True, a...  13.5 us
    ppermute x2, waiting for transfers between devices, whole_local(): high = lax.ppermute(down, 'tile', backward)  7.89 us
    ppermute x2, starting transfers between devices, whole_local(): low = lax.ppermute(up, 'tile', forward)  4.92 us
    ppermute x2, starting transfers between devices, whole_local(): high = lax.ppermute(down, 'tile', backward)  3.84 us
    pallas_call x1, Pallas kernels, whole_local(): pl.pallas_call(window_kernel, out_shape=(array(tiles, halves * rows + -(-...  2.52 us
    pallas_call x1, Pallas kernels, whole_local(): pl.pallas_call(lambda *refs: member_sum_kernel(tiles, *refs), out_shape=a...  2.29 us
    pallas_call x1, Pallas kernels, whole_local(): pl.pallas_call(member_update_kernel, out_shape=(array(*ens_control.shape)...  1.08 us
    ppermute x2, waiting for transfers between devices, whole_local(): low = lax.ppermute(up, 'tile', forward)  1.07 us
  transfers between devices with their start and end apart: 6, of which 4 were waited for; matrix products, arithmetic and copies ran while one was open for 0% of the time, Pallas kernels for 0%

profile of v4, /device:TPU:1, one launch (start us, length us, event | category | flops | bytes accessed | tf_op | source)
XLA Modules:
  0.0 38.3 jit_solution(17974536965363166915)
XLA Ops:
  0.6 0.0 copy-start.1
  0.6 0.0 copy-start.2
  0.6 2.3 %member_sum.1 = f32[16,48,128]{2,1,0:T(8,128)} custom-call(bf16[256,256]{1,0:T(8,128)(2,1)} %lat_ref.1, bf16[256,256]{1,0:T(8,128)(2,1)} %lon_ref.1, bf16[1,256,256]{2,1,0:T(8,128)(2,1)} %perts_ref.1, f32[1,256,256]{2,1,0:T(8,128)} %control_ref.5), custom_call_target="tpu_custom_call" | custom-call | tf_op jit(solution)/shard_map/member_sum/pallas_call | solution.py:303
  2.9 0.0 copy-start
  2.9 0.0 copy-start.3
  2.9 0.0 copy-start.4
  3.0 7.6 %all-to-all-start = ((f32[16,48,128]{2,1,0:T(8,128)}), f32[16,48,128]{2,1,0:T(8,128)S(1)}, u32[]{:S(2)}, u32[]{:S(2)}) async-start(f32[16,48,128]{2,1,0:T(8,128)} %member_sum.1), calls=%async_computation | async-start | bytes 786432 | tf_op jit(solution)/shard_map/all_to_all | solution.py:294
  10.5 0.0 copy-done.1
  10.5 0.0 copy-done.2
  10.6 0.0 copy-done
  10.6 0.0 copy-done.3
  10.6 0.0 copy-done.4
  10.6 0.1 pack.1
  10.7 0.0 copy-start.9
  10.7 2.5 %collective-permute-start = (f32[2,72,256]{2,1,0:T(8,128)S(1)}, f32[2,72,256]{2,1,0:T(8,128)S(1)}, u32[]{:S(2)}, u32[]{:S(2)}) collective-permute-start(f32[2,72,256]{2,1,0:T(8,128)S(1)} %get-tuple-element.8), channel_id=1, source_target_pairs={{0,1},{1,2},{2,3},{3,4},{4,5},{5,6},{6,7},{7,8},{8,9},{9,10},{10,1... | collective-permute-start | bytes 442376 | tf_op jit(solution)/shard_map/ppermute | solution.py:321
  13.2 1.9 %collective-permute-start.1 = (f32[2,72,256]{2,1,0:T(8,128)S(1)}, f32[2,72,256]{2,1,0:T(8,128)S(1)}, u32[]{:S(2)}, u32[]{:S(2)}) collective-permute-start(f32[2,72,256]{2,1,0:T(8,128)S(1)} %get-tuple-element.9), channel_id=1, source_target_pairs={{1,0},{2,1},{3,2},{4,3},{5,4},{6,5},{7,6},{8,7},{9,8},{10,9},{11,1... | collective-permute-start | bytes 442376 | tf_op jit(solution)/shard_map/ppermute | solution.py:322
  15.1 1.1 %collective-permute-done.low_ref = f32[2,72,256]{2,1,0:T(8,128)S(1)} collective-permute-done((f32[2,72,256]{2,1,0:T(8,128)S(1)}, f32[2,72,256]{2,1,0:T(8,128)S(1)}, u32[]{:S(2)}, u32[]{:S(2)}) %collective-permute-start) | collective-permute-done | bytes 147488 | tf_op jit(solution)/shard_map/ppermute | solution.py:321
  16.2 4.4 %collective-permute-done.1.high_ref = f32[2,72,256]{2,1,0:T(8,128)S(1)} collective-permute-done((f32[2,72,256]{2,1,0:T(8,128)S(1)}, f32[2,72,256]{2,1,0:T(8,128)S(1)}, u32[]{:S(2)}, u32[]{:S(2)}) %collective-permute-start.1) | collective-permute-done | bytes 147488 | tf_op jit(solution)/shard_map/ppermute | solution.py:322
  20.5 0.0 all-to-all-done.received_ref
  20.5 0.0 copy-done.9
  20.5 2.5 %window.1 = (f32[16,40,128]{2,1,0:T(8,128)}, f32[8,24,256]{2,1,0:T(8,128)S(1)}, f32[2,8,256]{2,1,0:T(8,128)S(1)}, f32[2,8,256]{2,1,0:T(8,128)S(1)}) custom-call(s32[16]{0:T(128)S(1)} %copy-done.9, f32[16,48,128]{2,1,0:T(8,128)S(1)} %all-to-all-done.received_ref, f32[2,72,256]{2,1,0:T(8,128)S(1)} %collective-permute-done.low_ref, ...), custom_call_target="tpu_custom_call" | custom-call | tf_op jit(solution)/shard_map/window/pallas_call | solution.py:325
  23.1 0.0 copy-start.5
  23.1 0.0 copy-start.6
  23.1 0.0 copy-start.7
  23.1 0.0 copy-start.8
  23.1 5.9 %all-to-all-start.1 = ((f32[16,40,128]{2,1,0:T(8,128)}), f32[16,40,128]{2,1,0:T(8,128)S(1)}, u32[]{:S(2)}, u32[]{:S(2)}) async-start(f32[16,40,128]{2,1,0:T(8,128)} %get-tuple-element.10), calls=%async_computation.1 | async-start | bytes 655360 | tf_op jit(solution)/shard_map/all_to_all | solution.py:294
  29.0 2.5 %collective-permute-start.2 = (f32[2,8,256]{2,1,0:T(8,128)S(1)}, f32[2,8,256]{2,1,0:T(8,128)S(1)}, u32[]{:S(2)}, u32[]{:S(2)}) collective-permute-start(f32[2,8,256]{2,1,0:T(8,128)S(1)} %get-tuple-element.11), channel_id=1, source_target_pairs={{0,1},{1,2},{2,3},{3,4},{4,5},{5,6},{6,7},{7,8},{8,9},{9,10},{10,1... | collective-permute-start | bytes 49160 | tf_op jit(solution)/shard_map/ppermute | solution.py:340
  31.5 1.9 %collective-permute-start.3 = (f32[2,8,256]{2,1,0:T(8,128)S(1)}, f32[2,8,256]{2,1,0:T(8,128)S(1)}, u32[]{:S(2)}, u32[]{:S(2)}) collective-permute-start(f32[2,8,256]{2,1,0:T(8,128)S(1)} %get-tuple-element.12), channel_id=1, source_target_pairs={{1,0},{2,1},{3,2},{4,3},{5,4},{6,5},{7,6},{8,7},{9,8},{10,9},{11,1... | collective-permute-start | bytes 49160 | tf_op jit(solution)/shard_map/ppermute | solution.py:341
  33.4 0.0 collective-permute-done.2.low_ref
  33.4 3.5 %collective-permute-done.3.high_ref = f32[2,8,256]{2,1,0:T(8,128)S(1)} collective-permute-done((f32[2,8,256]{2,1,0:T(8,128)S(1)}, f32[2,8,256]{2,1,0:T(8,128)S(1)}, u32[]{:S(2)}, u32[]{:S(2)}) %collective-permute-start.3) | collective-permute-done | bytes 16416 | tf_op jit(solution)/shard_map/ppermute | solution.py:341
  36.9 0.3 all-to-all-done.1.incoming_ref
  37.2 0.0 copy-done.5
  37.2 0.0 copy-done.6
  37.2 0.0 copy-done.7
  37.2 0.0 copy-done.8
  37.3 1.1 %member_update.1 = (f32[1,256,256]{2,1,0:T(8,128)}, f32[8,16,256]{2,1,0:T(8,128)}) custom-call(bf16[256,256]{1,0:T(8,128)(2,1)S(1)} %copy-done.6, bf16[256,256]{1,0:T(8,128)(2,1)S(1)} %copy-done.7, bf16[1,256,256]{2,1,0:T(8,128)(2,1)S(1)} %copy-done.8, f32[16,40,128]{2,1,0:T(8,128)S(1)} %all-to-all-done.1.incoming_ref, f32[1,256,256]{2,1,0:T(8,128)S(1)} %copy-done.5, ...), custom_call_target="tpu_custom_call" | custom-call | tf_op jit(solution)/shard_map/member_update/pallas_call | solution.py:343
Async XLA Ops:
  0.6 9.9 %copy-start.1 = (f32[3,8,16,256]{3,2,1,0:T(8,128)S(1)}, f32[3,8,16,256]{3,2,1,0:T(8,128)}, u32[]{:S(2)}) copy-start(f32[3,8,16,256]{3,2,1,0:T(8,128)} %weight_ref.3) | copy-start | bytes 1179652
  0.6 9.9 %copy-start.2 = (f32[3,8,16,256]{3,2,1,0:T(8,128)S(1)}, f32[3,8,16,256]{3,2,1,0:T(8,128)}, u32[]{:S(2)}) copy-start(f32[3,8,16,256]{3,2,1,0:T(8,128)} %innov_ref.3) | copy-start | bytes 1179652
  2.9 7.6 %copy-start = (f32[4,8,16,256]{3,2,1,0:T(8,128)S(1)}, f32[4,8,16,256]{3,2,1,0:T(8,128)}, u32[]{:S(2)}) copy-start(f32[4,8,16,256]{3,2,1,0:T(8,128)} %coefs_ref.3) | copy-start | bytes 1572868
  2.9 7.6 %copy-start.3 = (f32[8,16,256]{2,1,0:T(8,128)S(1)}, f32[8,16,256]{2,1,0:T(8,128)}, u32[]{:S(2)}) copy-start(f32[8,16,256]{2,1,0:T(8,128)} %static_ref.1) | copy-start | bytes 393220
  2.9 7.6 %copy-start.4 = (f32[8,16,256]{2,1,0:T(8,128)S(1)}, f32[8,16,256]{2,1,0:T(8,128)}, u32[]{:S(2)}) copy-start(f32[8,16,256]{2,1,0:T(8,128)} %scale_ref.5) | copy-start | bytes 393220
  3.0 17.6 %all-to-all-start = ((f32[16,48,128]{2,1,0:T(8,128)}), f32[16,48,128]{2,1,0:T(8,128)S(1)}, u32[]{:S(2)}, u32[]{:S(2)}) async-start(f32[16,48,128]{2,1,0:T(8,128)} %member_sum.1), calls=%async_computation | async-start | bytes 786432 | tf_op jit(solution)/shard_map/all_to_all | solution.py:294
  10.7 9.8 %copy-start.9 = (s32[16]{0:T(128)S(1)}, s32[16]{0:T(128)}, u32[]{:S(2)}) copy-start(s32[16]{0:T(128)} %level_ref.1) | copy-start | bytes 196
  10.7 5.5 %collective-permute-start = (f32[2,72,256]{2,1,0:T(8,128)S(1)}, f32[2,72,256]{2,1,0:T(8,128)S(1)}, u32[]{:S(2)}, u32[]{:S(2)}) collective-permute-start(f32[2,72,256]{2,1,0:T(8,128)S(1)} %get-tuple-element.8), channel_id=1, source_target_pairs={{0,1},{1,2},{2,3},{3,4},{4,5},{5,6},{6,7},{7,8},{8,9},{9,10},{10,1... | collective-permute-start | bytes 442376 | tf_op jit(solution)/shard_map/ppermute | solution.py:321
  13.2 7.4 %collective-permute-start.1 = (f32[2,72,256]{2,1,0:T(8,128)S(1)}, f32[2,72,256]{2,1,0:T(8,128)S(1)}, u32[]{:S(2)}, u32[]{:S(2)}) collective-permute-start(f32[2,72,256]{2,1,0:T(8,128)S(1)} %get-tuple-element.9), channel_id=1, source_target_pairs={{1,0},{2,1},{3,2},{4,3},{5,4},{6,5},{7,6},{8,7},{9,8},{10,9},{11,1... | collective-permute-start | bytes 442376 | tf_op jit(solution)/shard_map/ppermute | solution.py:322
  23.1 14.2 %copy-start.5 = (f32[1,256,256]{2,1,0:T(8,128)S(1)}, f32[1,256,256]{2,1,0:T(8,128)}, u32[]{:S(2)}) copy-start(f32[1,256,256]{2,1,0:T(8,128)} %control_ref.5) | copy-start | bytes 786436
  23.1 14.2 %copy-start.6 = (bf16[256,256]{1,0:T(8,128)(2,1)S(1)}, bf16[256,256]{1,0:T(8,128)(2,1)}, u32[]{:S(2)}) copy-start(bf16[256,256]{1,0:T(8,128)(2,1)} %lat_ref.1) | copy-start | bytes 393220
  23.1 14.2 %copy-start.7 = (bf16[256,256]{1,0:T(8,128)(2,1)S(1)}, bf16[256,256]{1,0:T(8,128)(2,1)}, u32[]{:S(2)}) copy-start(bf16[256,256]{1,0:T(8,128)(2,1)} %lon_ref.1) | copy-start | bytes 393220
  23.1 14.2 %copy-start.8 = (bf16[1,256,256]{2,1,0:T(8,128)(2,1)S(1)}, bf16[1,256,256]{2,1,0:T(8,128)(2,1)}, u32[]{:S(2)}) copy-start(bf16[1,256,256]{2,1,0:T(8,128)(2,1)} %perts_ref.1) | copy-start | bytes 393220
  23.1 14.2 %all-to-all-start.1 = ((f32[16,40,128]{2,1,0:T(8,128)}), f32[16,40,128]{2,1,0:T(8,128)S(1)}, u32[]{:S(2)}, u32[]{:S(2)}) async-start(f32[16,40,128]{2,1,0:T(8,128)} %get-tuple-element.10), calls=%async_computation.1 | async-start | bytes 655360 | tf_op jit(solution)/shard_map/all_to_all | solution.py:294
  29.0 4.4 %collective-permute-start.2 = (f32[2,8,256]{2,1,0:T(8,128)S(1)}, f32[2,8,256]{2,1,0:T(8,128)S(1)}, u32[]{:S(2)}, u32[]{:S(2)}) collective-permute-start(f32[2,8,256]{2,1,0:T(8,128)S(1)} %get-tuple-element.11), channel_id=1, source_target_pairs={{0,1},{1,2},{2,3},{3,4},{4,5},{5,6},{6,7},{7,8},{8,9},{9,10},{10,1... | collective-permute-start | bytes 49160 | tf_op jit(solution)/shard_map/ppermute | solution.py:340
  31.5 5.5 %collective-permute-start.3 = (f32[2,8,256]{2,1,0:T(8,128)S(1)}, f32[2,8,256]{2,1,0:T(8,128)S(1)}, u32[]{:S(2)}, u32[]{:S(2)}) collective-permute-start(f32[2,8,256]{2,1,0:T(8,128)S(1)} %get-tuple-element.12), channel_id=1, source_target_pairs={{1,0},{2,1},{3,2},{4,3},{5,4},{6,5},{7,6},{8,7},{9,8},{10,9},{11,1... | collective-permute-start | bytes 49160 | tf_op jit(solution)/shard_map/ppermute | solution.py:341

commit v5 on v4

--- a/solution.py
+++ b/solution.py
@@ -71,7 +71,19 @@
             out_ref[e, at : at + SUB, :] = jnp.where(first, above, below)
 
 
-def pack_kernel(control_ref, scale_ref, coefs_ref, weight_ref, innov_ref, up_ref, down_ref):
+def pack_kernel(control_ref, scale_ref, coefs_ref, weight_ref, innov_ref, inner_ref, outer_ref):
+    even = lax.axis_index("tile") % 2 == 0
+
+    @pl.when(even)
+    def _():
+        pack(control_ref, scale_ref, coefs_ref, weight_ref, innov_ref, inner_ref, outer_ref)
+
+    @pl.when(jnp.logical_not(even))
+    def _():
+        pack(control_ref, scale_ref, coefs_ref, weight_ref, innov_ref, outer_ref, inner_ref)
+
+
+def pack(control_ref, scale_ref, coefs_ref, weight_ref, innov_ref, up_ref, down_ref):
     refs = {"coefs": coefs_ref, "obs_weight": weight_ref, "innovation": innov_ref}
     levels, rows, _ = control_ref.shape
     for l in range(levels):
@@ -91,8 +103,8 @@
 def window_kernel(
     level_ref,
     received_ref,
-    low_ref,
-    high_ref,
+    inner_ref,
+    outer_ref,
     control_ref,
     scale_ref,
     coefs_ref,
@@ -100,15 +112,28 @@
     innov_ref,
     send_ref,
     grad_ref,
-    up_ref,
-    down_ref,
+    inner_out_ref,
+    outer_out_ref,
     sums_ref,
+    low_ref,
+    high_ref,
 ):
     tiles = received_ref.shape[0]
     levels, rows, nlon = control_ref.shape
     ring = rows + SUB
     halves = nlon // LANES
     refs = {"coefs": coefs_ref, "obs_weight": weight_ref, "innovation": innov_ref}
+    even = lax.axis_index("tile") % 2 == 0
+
+    @pl.when(even)
+    def _():
+        low_ref[...] = outer_ref[...]
+        high_ref[...] = inner_ref[...]
+
+    @pl.when(jnp.logical_not(even))
+    def _():
+        low_ref[...] = inner_ref[...]
+        high_ref[...] = outer_ref[...]
 
     sums_ref[...] = jnp.zeros_like(sums_ref)
     for d, tile in enumerate(order(tiles)):
@@ -184,15 +209,13 @@
                     [adjoint[:rows] + weighted[left - 1], adjoint[rows:]], axis=0
                 )
         grad_ref[l] = adjoint
-        up_ref[g, i * SPILL : (i + 1) * SPILL, :] = adjoint[rows : rows + SPILL]
-        down_ref[g, i * SPILL : (i + 1) * SPILL, :] = adjoint[ring - SPILL :]
-
-    def group(g, carry):
-        for i in range(GROUP):
-            level(g, i)
-        return carry
-
-    lax.fori_loop(0, levels // GROUP, group, 0)
+        above_rows, below_rows = adjoint[rows : rows + SPILL], adjoint[ring - SPILL :]
+        spot = slice(i * SPILL, (i + 1) * SPILL)
+        inner_out_ref[g, spot, :] = jnp.where(even, above_rows, below_rows)
+        outer_out_ref[g, spot, :] = jnp.where(even, below_rows, above_rows)
+
+    for l in range(levels):
+        level(l // GROUP, l % GROUP)
     row = sublane((SUB, LANES))
     for e, tile in enumerate(order(tiles)):
         at = level_ref[tile]
@@ -218,8 +241,8 @@
     perts_ref,
     incoming_ref,
     control_ref,
-    low_ref,
-    high_ref,
+    inner_ref,
+    outer_ref,
     tile_grad_ref,
     static_ref,
     scale_ref,
@@ -263,11 +286,13 @@
         out_ref[b] = control - STEP_SIZE * (control + member_grad)
 
     row = sublane((SUB, nlon))
+    even = lax.axis_index("tile") % 2 == 0
     for l in range(static_ref.shape[0]):
         at = l % GROUP * SPILL
-        block = low_ref[l // GROUP, 0:SUB, :]
+        inner, outer = inner_ref[l // GROUP, 0:SUB, :], outer_ref[l // GROUP, 0:SUB, :]
+        block = jnp.where(even, outer, inner)
         above = jnp.where(row < SPILL, pltpu.roll(block, SUB - at, 0) if at else block, 0.0)
-        block = high_ref[l // GROUP, 0:SUB, :]
+        block = jnp.where(even, inner, outer)
         shift = (SUB - SPILL - at) % SUB
         below = jnp.where(
             row >= SUB - SPILL, pltpu.roll(block, shift, 0) if shift else block, 0.0
@@ -287,8 +312,11 @@
     tiles = lax.axis_size("tile")
     levels, rows, nlon = static_control.shape
     halves = nlon // LANES
-    forward = [(i, i + 1) for i in range(tiles - 1)]
-    backward = [(target, source) for source, target in forward]
+
+    def exchanged_pairs(inner, outer):
+        pairs = [[(i, i + 1) for i in range(first, tiles - 1, 2)] for first in (0, 1)]
+        both = [pair + [(b, a) for a, b in pair] for pair in pairs]
+        return lax.ppermute(inner, "tile", both[0]), lax.ppermute(outer, "tile", both[1])
 
     def swapped(pieces):
         return lax.all_to_all(
@@ -310,7 +338,7 @@
     received = swapped(pieces)
 
     packed = array(levels // GROUP, PACKED, nlon)
-    up, down = pl.pallas_call(
+    inner, outer = pl.pallas_call(
         pack_kernel,
         out_shape=(packed, packed),
         in_specs=vmem(5),
@@ -318,11 +346,10 @@
         compiler_params=params(8),
         name="pack",
     )(static_control, static_scale, coefs, obs_weight, innovation)
-    low = lax.ppermute(up, "tile", forward)
-    high = lax.ppermute(down, "tile", backward)
+    inner, outer = exchanged_pairs(inner, outer)
 
     spilled = array(levels // GROUP, GROUP * SPILL, nlon)
-    send, tile_grad, up, down = pl.pallas_call(
+    send, tile_grad, inner, outer = pl.pallas_call(
         window_kernel,
         out_shape=(
             array(tiles, halves * rows + -(-halves // 2) * SUB, LANES),
@@ -332,13 +359,16 @@
         ),
         in_specs=[pl.BlockSpec(memory_space=pltpu.SMEM)] + vmem(8),
         out_specs=tuple(vmem(4)),
-        scratch_shapes=[pltpu.VMEM((levels,) + first_shape[1:], jnp.float32)],
+        scratch_shapes=[
+            pltpu.VMEM((levels,) + first_shape[1:], jnp.float32),
+            pltpu.VMEM(packed.shape, jnp.float32),
+            pltpu.VMEM(packed.shape, jnp.float32),
+        ],
         compiler_params=params(8),
         name="window",
-    )(level_map, received, low, high, static_control, static_scale, coefs, obs_weight, innovation)
+    )(level_map, received, inner, outer, static_control, static_scale, coefs, obs_weight, innovation)
     incoming = swapped(send)
-    low = lax.ppermute(up, "tile", forward)
-    high = lax.ppermute(down, "tile", backward)
+    inner, outer = exchanged_pairs(inner, outer)
 
     return pl.pallas_call(
         member_update_kernel,
@@ -350,7 +380,7 @@
         name="member_update",
     )(
         loc_lat, loc_lon, ens_perts, incoming, ens_control,
-        low, high, tile_grad, static_control, static_scale,
+        inner, outer, tile_grad, static_control, static_scale,
     )
 
 

time: 38.8 us -> 38.4 us (0.990)
  starting transfers between devices: 22.3 us -> 18.9 us
  waiting for transfers between devices: 9.25 us -> 12.4 us
    ppermute x4, starting transfers between devices: 8.76 us -> 5.2 us  [the longest x2 4.34 us: exchanged_pairs(): lax.ppermute(outer, 'tile', both[1])]
    all_to_all x2, waiting for transfers between devices: 0.29 us -> 3.81 us  [swapped(): lax.all_to_all(pieces, 'tile', split_axis=0, concat_axis=0, tiled=True, a...]
where the time goes in v5:
time: 38.4 us; the launch traced here: 38 us
  starting transfers between devices  18.9 us (49%)
  waiting for transfers between devices  12.4 us (32%)
  Pallas kernels  5.83 us (15%)
  between operations  0.75 us (2%)
    all_to_all x2, starting transfers between devices, swapped(): lax.all_to_all(pieces, 'tile', split_axis=0, concat_axis=0, tiled=True, a...  13.7 us
    ppermute x2, waiting for transfers between devices, exchanged_pairs(): lax.ppermute(outer, 'tile', both[1])  8.62 us
    ppermute x2, starting transfers between devices, exchanged_pairs(): lax.ppermute(outer, 'tile', both[1])  4.34 us
    all_to_all x2, waiting for transfers between devices, swapped(): lax.all_to_all(pieces, 'tile', split_axis=0, concat_axis=0, tiled=True, a...  3.81 us
    pallas_call x1, Pallas kernels, whole_local(): pl.pallas_call(window_kernel, out_shape=(array(tiles, halves * rows + -(-...  2.34 us
    pallas_call x1, Pallas kernels, whole_local(): pl.pallas_call(lambda *refs: member_sum_kernel(tiles, *refs), out_shape=a...  2.29 us
    pallas_call x1, Pallas kernels, whole_local(): pl.pallas_call(member_update_kernel, out_shape=(array(*ens_control.shape)...  1.08 us
    ppermute x2, starting transfers between devices, exchanged_pairs(): lax.ppermute(inner, 'tile', both[0])  0.86 us
  transfers between devices with their start and end apart: 6, of which 4 were waited for; matrix products, arithmetic and copies ran while one was open for 0% of the time, Pallas kernels for 0%

profile of v5, /device:TPU:1, one launch (start us, length us, event | category | flops | bytes accessed | tf_op | source)
XLA Modules:
  0.0 38.0 jit_solution(10620638756419287410)
XLA Ops:
  0.6 0.0 copy-start.1
  0.6 0.0 copy-start.2
  0.6 2.3 %member_sum.1 = f32[16,48,128]{2,1,0:T(8,128)} custom-call(bf16[256,256]{1,0:T(8,128)(2,1)} %lat_ref.1, bf16[256,256]{1,0:T(8,128)(2,1)} %lon_ref.1, bf16[1,256,256]{2,1,0:T(8,128)(2,1)} %perts_ref.1, f32[1,256,256]{2,1,0:T(8,128)} %control_ref.5), custom_call_target="tpu_custom_call" | custom-call | tf_op jit(solution)/shard_map/member_sum/pallas_call | solution.py:331
  2.9 0.0 copy-start
  2.9 0.0 copy-start.3
  2.9 0.0 copy-start.4
  3.0 7.6 %all-to-all-start = ((f32[16,48,128]{2,1,0:T(8,128)}), f32[16,48,128]{2,1,0:T(8,128)S(1)}, u32[]{:S(2)}, u32[]{:S(2)}) async-start(f32[16,48,128]{2,1,0:T(8,128)} %member_sum.1), calls=%async_computation | async-start | bytes 786432 | tf_op jit(solution)/shard_map/all_to_all | solution.py:322
  10.5 0.0 copy-done.1
  10.5 0.0 copy-done.2
  10.6 0.0 copy-done
  10.6 0.0 copy-done.3
  10.6 0.0 copy-done.4
  10.6 0.1 pack.1
  10.7 0.0 copy-start.9
  10.7 0.5 %collective-permute-start = (f32[2,72,256]{2,1,0:T(8,128)S(1)}, f32[2,72,256]{2,1,0:T(8,128)S(1)}, u32[]{:S(2)}, u32[]{:S(2)}) collective-permute-start(f32[2,72,256]{2,1,0:T(8,128)S(1)} %get-tuple-element.8), channel_id=1, source_target_pairs={{0,1},{2,3},{4,5},{6,7},{8,9},{10,11},{12,13},{14,15},{1,0},{3,2},... | collective-permute-start | bytes 442376 | tf_op jit(solution)/shard_map/ppermute | solution.py:319
  11.2 2.2 %collective-permute-start.1 = (f32[2,72,256]{2,1,0:T(8,128)S(1)}, f32[2,72,256]{2,1,0:T(8,128)S(1)}, u32[]{:S(2)}, u32[]{:S(2)}) collective-permute-start(f32[2,72,256]{2,1,0:T(8,128)S(1)} %get-tuple-element.9), channel_id=1, source_target_pairs={{1,2},{3,4},{5,6},{7,8},{9,10},{11,12},{13,14},{2,1},{4,3},{6,5},{... | collective-permute-start | bytes 442376 | tf_op jit(solution)/shard_map/ppermute | solution.py:319
  13.4 0.0 collective-permute-done.inner_ref
  13.4 5.3 %collective-permute-done.1.outer_ref = f32[2,72,256]{2,1,0:T(8,128)S(1)} collective-permute-done((f32[2,72,256]{2,1,0:T(8,128)S(1)}, f32[2,72,256]{2,1,0:T(8,128)S(1)}, u32[]{:S(2)}, u32[]{:S(2)}) %collective-permute-start.1) | collective-permute-done | bytes 147488 | tf_op jit(solution)/shard_map/ppermute | solution.py:319
  18.7 1.5 %all-to-all-done.received_ref = f32[16,48,128]{2,1,0:T(8,128)S(1)} async-done(((f32[16,48,128]{2,1,0:T(8,128)}), f32[16,48,128]{2,1,0:T(8,128)S(1)}, u32[]{:S(2)}, u32[]{:S(2)}) %all-to-all-start) | async-done | bytes 393248 | tf_op jit(solution)/shard_map/all_to_all | solution.py:322
  20.2 0.0 copy-done.9
  20.2 2.3 %window.1 = (f32[16,40,128]{2,1,0:T(8,128)}, f32[8,24,256]{2,1,0:T(8,128)S(1)}, f32[2,8,256]{2,1,0:T(8,128)S(1)}, f32[2,8,256]{2,1,0:T(8,128)S(1)}) custom-call(s32[16]{0:T(128)S(1)} %copy-done.9, f32[16,48,128]{2,1,0:T(8,128)S(1)} %all-to-all-done.received_ref, f32[2,72,256]{2,1,0:T(8,128)S(1)} %collective-permute-done.inner_ref, ...), custom_call_target="tpu_custom_call" | custom-call | tf_op jit(solution)/shard_map/window/pallas_call | solution.py:352
  22.5 0.0 copy-start.5
  22.5 0.0 copy-start.6
  22.5 0.0 copy-start.7
  22.5 0.0 copy-start.8
  22.5 6.2 %all-to-all-start.1 = ((f32[16,40,128]{2,1,0:T(8,128)}), f32[16,40,128]{2,1,0:T(8,128)S(1)}, u32[]{:S(2)}, u32[]{:S(2)}) async-start(f32[16,40,128]{2,1,0:T(8,128)} %get-tuple-element.10), calls=%async_computation.1 | async-start | bytes 655360 | tf_op jit(solution)/shard_map/all_to_all | solution.py:322
  28.7 0.4 %collective-permute-start.2 = (f32[2,8,256]{2,1,0:T(8,128)S(1)}, f32[2,8,256]{2,1,0:T(8,128)S(1)}, u32[]{:S(2)}, u32[]{:S(2)}) collective-permute-start(f32[2,8,256]{2,1,0:T(8,128)S(1)} %get-tuple-element.11), channel_id=1, source_target_pairs={{0,1},{2,3},{4,5},{6,7},{8,9},{10,11},{12,13},{14,15},{1,0},{3,2},... | collective-permute-start | bytes 49160 | tf_op jit(solution)/shard_map/ppermute | solution.py:319
  29.1 2.2 %collective-permute-start.3 = (f32[2,8,256]{2,1,0:T(8,128)S(1)}, f32[2,8,256]{2,1,0:T(8,128)S(1)}, u32[]{:S(2)}, u32[]{:S(2)}) collective-permute-start(f32[2,8,256]{2,1,0:T(8,128)S(1)} %get-tuple-element.12), channel_id=1, source_target_pairs={{1,2},{3,4},{5,6},{7,8},{9,10},{11,12},{13,14},{2,1},{4,3},{6,5},{... | collective-permute-start | bytes 49160 | tf_op jit(solution)/shard_map/ppermute | solution.py:319
  31.3 0.0 collective-permute-done.2.inner_ref
  31.3 3.3 %collective-permute-done.3.outer_ref = f32[2,8,256]{2,1,0:T(8,128)S(1)} collective-permute-done((f32[2,8,256]{2,1,0:T(8,128)S(1)}, f32[2,8,256]{2,1,0:T(8,128)S(1)}, u32[]{:S(2)}, u32[]{:S(2)}) %collective-permute-start.3) | collective-permute-done | bytes 16416 | tf_op jit(solution)/shard_map/ppermute | solution.py:319
  34.6 2.3 %all-to-all-done.1.incoming_ref = f32[16,40,128]{2,1,0:T(8,128)S(1)} async-done(((f32[16,40,128]{2,1,0:T(8,128)}), f32[16,40,128]{2,1,0:T(8,128)S(1)}, u32[]{:S(2)}, u32[]{:S(2)}) %all-to-all-start.1) | async-done | bytes 327712 | tf_op jit(solution)/shard_map/all_to_all | solution.py:322
  36.9 0.0 copy-done.5
  36.9 0.0 copy-done.6
  36.9 0.0 copy-done.7
  36.9 0.0 copy-done.8
  36.9 1.1 %member_update.1 = (f32[1,256,256]{2,1,0:T(8,128)}, f32[8,16,256]{2,1,0:T(8,128)}) custom-call(bf16[256,256]{1,0:T(8,128)(2,1)S(1)} %copy-done.6, bf16[256,256]{1,0:T(8,128)(2,1)S(1)} %copy-done.7, bf16[1,256,256]{2,1,0:T(8,128)(2,1)S(1)} %copy-done.8, f32[16,40,128]{2,1,0:T(8,128)S(1)} %all-to-all-done.1.incoming_ref, f32[1,256,256]{2,1,0:T(8,128)S(1)} %copy-done.5, ...), custom_call_target="tpu_custom_call" | custom-call | tf_op jit(solution)/shard_map/member_update/pallas_call | solution.py:373
Async XLA Ops:
  0.6 9.9 %copy-start.1 = (f32[3,8,16,256]{3,2,1,0:T(8,128)S(1)}, f32[3,8,16,256]{3,2,1,0:T(8,128)}, u32[]{:S(2)}) copy-start(f32[3,8,16,256]{3,2,1,0:T(8,128)} %weight_ref.3) | copy-start | bytes 1179652
  0.6 9.9 %copy-start.2 = (f32[3,8,16,256]{3,2,1,0:T(8,128)S(1)}, f32[3,8,16,256]{3,2,1,0:T(8,128)}, u32[]{:S(2)}) copy-start(f32[3,8,16,256]{3,2,1,0:T(8,128)} %innov_ref.3) | copy-start | bytes 1179652
  2.9 7.6 %copy-start = (f32[4,8,16,256]{3,2,1,0:T(8,128)S(1)}, f32[4,8,16,256]{3,2,1,0:T(8,128)}, u32[]{:S(2)}) copy-start(f32[4,8,16,256]{3,2,1,0:T(8,128)} %coefs_ref.3) | copy-start | bytes 1572868
  2.9 7.6 %copy-start.3 = (f32[8,16,256]{2,1,0:T(8,128)S(1)}, f32[8,16,256]{2,1,0:T(8,128)}, u32[]{:S(2)}) copy-start(f32[8,16,256]{2,1,0:T(8,128)} %static_ref.1) | copy-start | bytes 393220
  2.9 7.6 %copy-start.4 = (f32[8,16,256]{2,1,0:T(8,128)S(1)}, f32[8,16,256]{2,1,0:T(8,128)}, u32[]{:S(2)}) copy-start(f32[8,16,256]{2,1,0:T(8,128)} %scale_ref.5) | copy-start | bytes 393220
  3.0 17.2 %all-to-all-start = ((f32[16,48,128]{2,1,0:T(8,128)}), f32[16,48,128]{2,1,0:T(8,128)S(1)}, u32[]{:S(2)}, u32[]{:S(2)}) async-start(f32[16,48,128]{2,1,0:T(8,128)} %member_sum.1), calls=%async_computation | async-start | bytes 786432 | tf_op jit(solution)/shard_map/all_to_all | solution.py:322
  10.7 9.5 %copy-start.9 = (s32[16]{0:T(128)S(1)}, s32[16]{0:T(128)}, u32[]{:S(2)}) copy-start(s32[16]{0:T(128)} %level_ref.1) | copy-start | bytes 196
  10.7 2.6 %collective-permute-start = (f32[2,72,256]{2,1,0:T(8,128)S(1)}, f32[2,72,256]{2,1,0:T(8,128)S(1)}, u32[]{:S(2)}, u32[]{:S(2)}) collective-permute-start(f32[2,72,256]{2,1,0:T(8,128)S(1)} %get-tuple-element.8), channel_id=1, source_target_pairs={{0,1},{2,3},{4,5},{6,7},{8,9},{10,11},{12,13},{14,15},{1,0},{3,2},... | collective-permute-start | bytes 442376 | tf_op jit(solution)/shard_map/ppermute | solution.py:319
  11.2 7.5 %collective-permute-start.1 = (f32[2,72,256]{2,1,0:T(8,128)S(1)}, f32[2,72,256]{2,1,0:T(8,128)S(1)}, u32[]{:S(2)}, u32[]{:S(2)}) collective-permute-start(f32[2,72,256]{2,1,0:T(8,128)S(1)} %get-tuple-element.9), channel_id=1, source_target_pairs={{1,2},{3,4},{5,6},{7,8},{9,10},{11,12},{13,14},{2,1},{4,3},{6,5},{... | collective-permute-start | bytes 442376 | tf_op jit(solution)/shard_map/ppermute | solution.py:319
  22.5 14.4 %copy-start.5 = (f32[1,256,256]{2,1,0:T(8,128)S(1)}, f32[1,256,256]{2,1,0:T(8,128)}, u32[]{:S(2)}) copy-start(f32[1,256,256]{2,1,0:T(8,128)} %control_ref.5) | copy-start | bytes 786436
  22.5 14.4 %copy-start.6 = (bf16[256,256]{1,0:T(8,128)(2,1)S(1)}, bf16[256,256]{1,0:T(8,128)(2,1)}, u32[]{:S(2)}) copy-start(bf16[256,256]{1,0:T(8,128)(2,1)} %lat_ref.1) | copy-start | bytes 393220
  22.5 14.4 %copy-start.7 = (bf16[256,256]{1,0:T(8,128)(2,1)S(1)}, bf16[256,256]{1,0:T(8,128)(2,1)}, u32[]{:S(2)}) copy-start(bf16[256,256]{1,0:T(8,128)(2,1)} %lon_ref.1) | copy-start | bytes 393220
  22.5 14.4 %copy-start.8 = (bf16[1,256,256]{2,1,0:T(8,128)(2,1)S(1)}, bf16[1,256,256]{2,1,0:T(8,128)(2,1)}, u32[]{:S(2)}) copy-start(bf16[1,256,256]{2,1,0:T(8,128)(2,1)} %perts_ref.1) | copy-start | bytes 393220
  22.5 14.4 %all-to-all-start.1 = ((f32[16,40,128]{2,1,0:T(8,128)}), f32[16,40,128]{2,1,0:T(8,128)S(1)}, u32[]{:S(2)}, u32[]{:S(2)}) async-start(f32[16,40,128]{2,1,0:T(8,128)} %get-tuple-element.10), calls=%async_computation.1 | async-start | bytes 655360 | tf_op jit(solution)/shard_map/all_to_all | solution.py:322
  28.7 2.6 %collective-permute-start.2 = (f32[2,8,256]{2,1,0:T(8,128)S(1)}, f32[2,8,256]{2,1,0:T(8,128)S(1)}, u32[]{:S(2)}, u32[]{:S(2)}) collective-permute-start(f32[2,8,256]{2,1,0:T(8,128)S(1)} %get-tuple-element.11), channel_id=1, source_target_pairs={{0,1},{2,3},{4,5},{6,7},{8,9},{10,11},{12,13},{14,15},{1,0},{3,2},... | collective-permute-start | bytes 49160 | tf_op jit(solution)/shard_map/ppermute | solution.py:319
  29.1 5.5 %collective-permute-start.3 = (f32[2,8,256]{2,1,0:T(8,128)S(1)}, f32[2,8,256]{2,1,0:T(8,128)S(1)}, u32[]{:S(2)}, u32[]{:S(2)}) collective-permute-start(f32[2,8,256]{2,1,0:T(8,128)S(1)} %get-tuple-element.12), channel_id=1, source_target_pairs={{1,2},{3,4},{5,6},{7,8},{9,10},{11,12},{13,14},{2,1},{4,3},{6,5},{... | collective-permute-start | bytes 49160 | tf_op jit(solution)/shard_map/ppermute | solution.py:319

commit v6 on v5

--- a/solution.py
+++ b/solution.py
@@ -36,7 +36,8 @@
 
 
 def order(tiles):
-    return [(2 * tiles // 3 + 1 - position) % tiles for position in range(tiles)]
+    quarters = [list(range(q * tiles // 4, (q + 1) * tiles // 4))[::-1] for q in (2, 0, 1, 3)]
+    return sum(quarters, [])
 
 
 def sublane(shape):

time: 38.4 us -> 38 us (0.990)
  waiting for transfers between devices: 12.4 us -> 11.5 us
  starting transfers between devices: 18.9 us -> 19.5 us
    ppermute x2, waiting for transfers between devices: 8.62 us -> 8.04 us  [exchanged_pairs(): lax.ppermute(outer, 'tile', both[1])]
    all_to_all x2, starting transfers between devices: 13.7 us -> 14.3 us  [swapped(): lax.all_to_all(pieces, 'tile', split_axis=0, concat_axis=0, tiled=True, a...]
where the time goes in v6:
time: 38 us; the launch traced here: 37.6 us
  starting transfers between devices  19.5 us (51%)
  waiting for transfers between devices  11.5 us (30%)
  Pallas kernels  5.83 us (15%)
  between operations  0.75 us (2%)
    all_to_all x2, starting transfers between devices, swapped(): lax.all_to_all(pieces, 'tile', split_axis=0, concat_axis=0, tiled=True, a...  14.3 us
    ppermute x2, waiting for transfers between devices, exchanged_pairs(): lax.ppermute(outer, 'tile', both[1])  8.04 us
    ppermute x2, starting transfers between devices, exchanged_pairs(): lax.ppermute(outer, 'tile', both[1])  4.34 us
    all_to_all x2, waiting for transfers between devices, swapped(): lax.all_to_all(pieces, 'tile', split_axis=0, concat_axis=0, tiled=True, a...  3.46 us
    pallas_call x1, Pallas kernels, whole_local(): pl.pallas_call(window_kernel, out_shape=(array(tiles, halves * rows + -(-...  2.34 us
    pallas_call x1, Pallas kernels, whole_local(): pl.pallas_call(lambda *refs: member_sum_kernel(tiles, *refs), out_shape=a...  2.29 us
    pallas_call x1, Pallas kernels, whole_local(): pl.pallas_call(member_update_kernel, out_shape=(array(*ens_control.shape)...  1.08 us
    ppermute x2, starting transfers between devices, exchanged_pairs(): lax.ppermute(inner, 'tile', both[0])  0.86 us
  transfers between devices with their start and end apart: 6, of which 4 were waited for; matrix products, arithmetic and copies ran while one was open for 0% of the time, Pallas kernels for 0%

profile of v6, /device:TPU:1, one launch (start us, length us, event | category | flops | bytes accessed | tf_op | source)
XLA Modules:
  0.0 37.6 jit_solution(17747592667847206805)
XLA Ops:
  0.6 0.0 copy-start.1
  0.6 0.0 copy-start.2
  0.6 2.3 %member_sum.1 = f32[16,48,128]{2,1,0:T(8,128)} custom-call(bf16[256,256]{1,0:T(8,128)(2,1)} %lat_ref.1, bf16[256,256]{1,0:T(8,128)(2,1)} %lon_ref.1, bf16[1,256,256]{2,1,0:T(8,128)(2,1)} %perts_ref.1, f32[1,256,256]{2,1,0:T(8,128)} %control_ref.5), custom_call_target="tpu_custom_call" | custom-call | tf_op jit(solution)/shard_map/member_sum/pallas_call | solution.py:332
  2.9 0.0 copy-start
  2.9 0.0 copy-start.3
  2.9 0.0 copy-start.4
  3.0 7.6 %all-to-all-start = ((f32[16,48,128]{2,1,0:T(8,128)}), f32[16,48,128]{2,1,0:T(8,128)S(1)}, u32[]{:S(2)}, u32[]{:S(2)}) async-start(f32[16,48,128]{2,1,0:T(8,128)} %member_sum.1), calls=%async_computation | async-start | bytes 786432 | tf_op jit(solution)/shard_map/all_to_all | solution.py:323
  10.5 0.0 copy-done.1
  10.5 0.0 copy-done.2
  10.5 0.0 copy-done
  10.5 0.0 copy-done.3
  10.6 0.0 copy-done.4
  10.6 0.1 pack.1
  10.7 0.0 copy-start.9
  10.7 0.5 %collective-permute-start = (f32[2,72,256]{2,1,0:T(8,128)S(1)}, f32[2,72,256]{2,1,0:T(8,128)S(1)}, u32[]{:S(2)}, u32[]{:S(2)}) collective-permute-start(f32[2,72,256]{2,1,0:T(8,128)S(1)} %get-tuple-element.8), channel_id=1, source_target_pairs={{0,1},{2,3},{4,5},{6,7},{8,9},{10,11},{12,13},{14,15},{1,0},{3,2},... | collective-permute-start | bytes 442376 | tf_op jit(solution)/shard_map/ppermute | solution.py:320
  11.2 2.2 %collective-permute-start.1 = (f32[2,72,256]{2,1,0:T(8,128)S(1)}, f32[2,72,256]{2,1,0:T(8,128)S(1)}, u32[]{:S(2)}, u32[]{:S(2)}) collective-permute-start(f32[2,72,256]{2,1,0:T(8,128)S(1)} %get-tuple-element.9), channel_id=1, source_target_pairs={{1,2},{3,4},{5,6},{7,8},{9,10},{11,12},{13,14},{2,1},{4,3},{6,5},{... | collective-permute-start | bytes 442376 | tf_op jit(solution)/shard_map/ppermute | solution.py:320
  13.3 0.0 collective-permute-done.inner_ref
  13.3 4.9 %collective-permute-done.1.outer_ref = f32[2,72,256]{2,1,0:T(8,128)S(1)} collective-permute-done((f32[2,72,256]{2,1,0:T(8,128)S(1)}, f32[2,72,256]{2,1,0:T(8,128)S(1)}, u32[]{:S(2)}, u32[]{:S(2)}) %collective-permute-start.1) | collective-permute-done | bytes 147488 | tf_op jit(solution)/shard_map/ppermute | solution.py:320
  18.2 1.4 %all-to-all-done.received_ref = f32[16,48,128]{2,1,0:T(8,128)S(1)} async-done(((f32[16,48,128]{2,1,0:T(8,128)}), f32[16,48,128]{2,1,0:T(8,128)S(1)}, u32[]{:S(2)}, u32[]{:S(2)}) %all-to-all-start) | async-done | bytes 393248 | tf_op jit(solution)/shard_map/all_to_all | solution.py:323
  19.6 0.0 copy-done.9
  19.6 2.3 %window.1 = (f32[16,40,128]{2,1,0:T(8,128)}, f32[8,24,256]{2,1,0:T(8,128)S(1)}, f32[2,8,256]{2,1,0:T(8,128)S(1)}, f32[2,8,256]{2,1,0:T(8,128)S(1)}) custom-call(s32[16]{0:T(128)S(1)} %copy-done.9, f32[16,48,128]{2,1,0:T(8,128)S(1)} %all-to-all-done.received_ref, f32[2,72,256]{2,1,0:T(8,128)S(1)} %collective-permute-done.inner_ref, ...), custom_call_target="tpu_custom_call" | custom-call | tf_op jit(solution)/shard_map/window/pallas_call | solution.py:353
  22.0 0.0 copy-start.5
  22.0 0.0 copy-start.6
  22.0 0.0 copy-start.7
  22.0 0.0 copy-start.8
  22.0 6.7 %all-to-all-start.1 = ((f32[16,40,128]{2,1,0:T(8,128)}), f32[16,40,128]{2,1,0:T(8,128)S(1)}, u32[]{:S(2)}, u32[]{:S(2)}) async-start(f32[16,40,128]{2,1,0:T(8,128)} %get-tuple-element.10), calls=%async_computation.1 | async-start | bytes 655360 | tf_op jit(solution)/shard_map/all_to_all | solution.py:323
  28.7 0.4 %collective-permute-start.2 = (f32[2,8,256]{2,1,0:T(8,128)S(1)}, f32[2,8,256]{2,1,0:T(8,128)S(1)}, u32[]{:S(2)}, u32[]{:S(2)}) collective-permute-start(f32[2,8,256]{2,1,0:T(8,128)S(1)} %get-tuple-element.11), channel_id=1, source_target_pairs={{0,1},{2,3},{4,5},{6,7},{8,9},{10,11},{12,13},{14,15},{1,0},{3,2},... | collective-permute-start | bytes 49160 | tf_op jit(solution)/shard_map/ppermute | solution.py:320
  29.1 2.2 %collective-permute-start.3 = (f32[2,8,256]{2,1,0:T(8,128)S(1)}, f32[2,8,256]{2,1,0:T(8,128)S(1)}, u32[]{:S(2)}, u32[]{:S(2)}) collective-permute-start(f32[2,8,256]{2,1,0:T(8,128)S(1)} %get-tuple-element.12), channel_id=1, source_target_pairs={{1,2},{3,4},{5,6},{7,8},{9,10},{11,12},{13,14},{2,1},{4,3},{6,5},{... | collective-permute-start | bytes 49160 | tf_op jit(solution)/shard_map/ppermute | solution.py:320
  31.3 0.0 collective-permute-done.2.inner_ref
  31.3 3.1 %collective-permute-done.3.outer_ref = f32[2,8,256]{2,1,0:T(8,128)S(1)} collective-permute-done((f32[2,8,256]{2,1,0:T(8,128)S(1)}, f32[2,8,256]{2,1,0:T(8,128)S(1)}, u32[]{:S(2)}, u32[]{:S(2)}) %collective-permute-start.3) | collective-permute-done | bytes 16416 | tf_op jit(solution)/shard_map/ppermute | solution.py:320
  34.4 2.1 %all-to-all-done.1.incoming_ref = f32[16,40,128]{2,1,0:T(8,128)S(1)} async-done(((f32[16,40,128]{2,1,0:T(8,128)}), f32[16,40,128]{2,1,0:T(8,128)S(1)}, u32[]{:S(2)}, u32[]{:S(2)}) %all-to-all-start.1) | async-done | bytes 327712 | tf_op jit(solution)/shard_map/all_to_all | solution.py:323
  36.5 0.0 copy-done.5
  36.5 0.0 copy-done.6
  36.5 0.0 copy-done.7
  36.5 0.0 copy-done.8
  36.5 1.1 %member_update.1 = (f32[1,256,256]{2,1,0:T(8,128)}, f32[8,16,256]{2,1,0:T(8,128)}) custom-call(bf16[256,256]{1,0:T(8,128)(2,1)S(1)} %copy-done.6, bf16[256,256]{1,0:T(8,128)(2,1)S(1)} %copy-done.7, bf16[1,256,256]{2,1,0:T(8,128)(2,1)S(1)} %copy-done.8, f32[16,40,128]{2,1,0:T(8,128)S(1)} %all-to-all-done.1.incoming_ref, f32[1,256,256]{2,1,0:T(8,128)S(1)} %copy-done.5, ...), custom_call_target="tpu_custom_call" | custom-call | tf_op jit(solution)/shard_map/member_update/pallas_call | solution.py:374
Async XLA Ops:
  0.6 9.9 %copy-start.1 = (f32[3,8,16,256]{3,2,1,0:T(8,128)S(1)}, f32[3,8,16,256]{3,2,1,0:T(8,128)}, u32[]{:S(2)}) copy-start(f32[3,8,16,256]{3,2,1,0:T(8,128)} %weight_ref.3) | copy-start | bytes 1179652
  0.6 9.9 %copy-start.2 = (f32[3,8,16,256]{3,2,1,0:T(8,128)S(1)}, f32[3,8,16,256]{3,2,1,0:T(8,128)}, u32[]{:S(2)}) copy-start(f32[3,8,16,256]{3,2,1,0:T(8,128)} %innov_ref.3) | copy-start | bytes 1179652
  2.9 7.6 %copy-start = (f32[4,8,16,256]{3,2,1,0:T(8,128)S(1)}, f32[4,8,16,256]{3,2,1,0:T(8,128)}, u32[]{:S(2)}) copy-start(f32[4,8,16,256]{3,2,1,0:T(8,128)} %coefs_ref.3) | copy-start | bytes 1572868
  2.9 7.6 %copy-start.3 = (f32[8,16,256]{2,1,0:T(8,128)S(1)}, f32[8,16,256]{2,1,0:T(8,128)}, u32[]{:S(2)}) copy-start(f32[8,16,256]{2,1,0:T(8,128)} %static_ref.1) | copy-start | bytes 393220
  2.9 7.6 %copy-start.4 = (f32[8,16,256]{2,1,0:T(8,128)S(1)}, f32[8,16,256]{2,1,0:T(8,128)}, u32[]{:S(2)}) copy-start(f32[8,16,256]{2,1,0:T(8,128)} %scale_ref.5) | copy-start | bytes 393220
  3.0 16.7 %all-to-all-start = ((f32[16,48,128]{2,1,0:T(8,128)}), f32[16,48,128]{2,1,0:T(8,128)S(1)}, u32[]{:S(2)}, u32[]{:S(2)}) async-start(f32[16,48,128]{2,1,0:T(8,128)} %member_sum.1), calls=%async_computation | async-start | bytes 786432 | tf_op jit(solution)/shard_map/all_to_all | solution.py:323
  10.7 9.0 %copy-start.9 = (s32[16]{0:T(128)S(1)}, s32[16]{0:T(128)}, u32[]{:S(2)}) copy-start(s32[16]{0:T(128)} %level_ref.1) | copy-start | bytes 196
  10.7 2.6 %collective-permute-start = (f32[2,72,256]{2,1,0:T(8,128)S(1)}, f32[2,72,256]{2,1,0:T(8,128)S(1)}, u32[]{:S(2)}, u32[]{:S(2)}) collective-permute-start(f32[2,72,256]{2,1,0:T(8,128)S(1)} %get-tuple-element.8), channel_id=1, source_target_pairs={{0,1},{2,3},{4,5},{6,7},{8,9},{10,11},{12,13},{14,15},{1,0},{3,2},... | collective-permute-start | bytes 442376 | tf_op jit(solution)/shard_map/ppermute | solution.py:320
  11.2 7.1 %collective-permute-start.1 = (f32[2,72,256]{2,1,0:T(8,128)S(1)}, f32[2,72,256]{2,1,0:T(8,128)S(1)}, u32[]{:S(2)}, u32[]{:S(2)}) collective-permute-start(f32[2,72,256]{2,1,0:T(8,128)S(1)} %get-tuple-element.9), channel_id=1, source_target_pairs={{1,2},{3,4},{5,6},{7,8},{9,10},{11,12},{13,14},{2,1},{4,3},{6,5},{... | collective-permute-start | bytes 442376 | tf_op jit(solution)/shard_map/ppermute | solution.py:320
  22.0 14.5 %copy-start.5 = (f32[1,256,256]{2,1,0:T(8,128)S(1)}, f32[1,256,256]{2,1,0:T(8,128)}, u32[]{:S(2)}) copy-start(f32[1,256,256]{2,1,0:T(8,128)} %control_ref.5) | copy-start | bytes 786436
  22.0 14.5 %copy-start.6 = (bf16[256,256]{1,0:T(8,128)(2,1)S(1)}, bf16[256,256]{1,0:T(8,128)(2,1)}, u32[]{:S(2)}) copy-start(bf16[256,256]{1,0:T(8,128)(2,1)} %lat_ref.1) | copy-start | bytes 393220
  22.0 14.5 %copy-start.7 = (bf16[256,256]{1,0:T(8,128)(2,1)S(1)}, bf16[256,256]{1,0:T(8,128)(2,1)}, u32[]{:S(2)}) copy-start(bf16[256,256]{1,0:T(8,128)(2,1)} %lon_ref.1) | copy-start | bytes 393220
  22.0 14.5 %copy-start.8 = (bf16[1,256,256]{2,1,0:T(8,128)(2,1)S(1)}, bf16[1,256,256]{2,1,0:T(8,128)(2,1)}, u32[]{:S(2)}) copy-start(bf16[1,256,256]{2,1,0:T(8,128)(2,1)} %perts_ref.1) | copy-start | bytes 393220
  22.0 14.5 %all-to-all-start.1 = ((f32[16,40,128]{2,1,0:T(8,128)}), f32[16,40,128]{2,1,0:T(8,128)S(1)}, u32[]{:S(2)}, u32[]{:S(2)}) async-start(f32[16,40,128]{2,1,0:T(8,128)} %get-tuple-element.10), calls=%async_computation.1 | async-start | bytes 655360 | tf_op jit(solution)/shard_map/all_to_all | solution.py:323
  28.7 2.6 %collective-permute-start.2 = (f32[2,8,256]{2,1,0:T(8,128)S(1)}, f32[2,8,256]{2,1,0:T(8,128)S(1)}, u32[]{:S(2)}, u32[]{:S(2)}) collective-permute-start(f32[2,8,256]{2,1,0:T(8,128)S(1)} %get-tuple-element.11), channel_id=1, source_target_pairs={{0,1},{2,3},{4,5},{6,7},{8,9},{10,11},{12,13},{14,15},{1,0},{3,2},... | collective-permute-start | bytes 49160 | tf_op jit(solution)/shard_map/ppermute | solution.py:320
  29.1 5.3 %collective-permute-start.3 = (f32[2,8,256]{2,1,0:T(8,128)S(1)}, f32[2,8,256]{2,1,0:T(8,128)S(1)}, u32[]{:S(2)}, u32[]{:S(2)}) collective-permute-start(f32[2,8,256]{2,1,0:T(8,128)S(1)} %get-tuple-element.12), channel_id=1, source_target_pairs={{1,2},{3,4},{5,6},{7,8},{9,10},{11,12},{13,14},{2,1},{4,3},{6,5},{... | collective-permute-start | bytes 49160 | tf_op jit(solution)/shard_map/ppermute | solution.py:320

commit v7 on v6

--- a/solution.py
+++ b/solution.py
@@ -118,12 +118,16 @@
     sums_ref,
     low_ref,
     high_ref,
+    levels_ref,
+    levels_sem,
 ):
     tiles = received_ref.shape[0]
     levels, rows, nlon = control_ref.shape
     ring = rows + SUB
     halves = nlon // LANES
     refs = {"coefs": coefs_ref, "obs_weight": weight_ref, "innovation": innov_ref}
+    copy = pltpu.make_async_copy(level_ref, levels_ref, levels_sem)
+    copy.start()
     even = lax.axis_index("tile") % 2 == 0
 
     @pl.when(even)
@@ -137,8 +141,9 @@
         high_ref[...] = outer_ref[...]
 
     sums_ref[...] = jnp.zeros_like(sums_ref)
+    copy.wait()
     for d, tile in enumerate(order(tiles)):
-        sums_ref[level_ref[tile]] += received_ref[d]
+        sums_ref[levels_ref[tile]] += received_ref[d]
 
     above = sublane((SUB, nlon)) < HALO
 
@@ -219,7 +224,7 @@
         level(l // GROUP, l % GROUP)
     row = sublane((SUB, LANES))
     for e, tile in enumerate(order(tiles)):
-        at = level_ref[tile]
+        at = levels_ref[tile]
         for h in range(0, halves, 2):
             spilled = grad_ref[at, rows:ring, h * LANES : (h + 1) * LANES]
             if h + 1 < halves:
@@ -358,12 +363,14 @@
             spilled,
             spilled,
         ),
-        in_specs=[pl.BlockSpec(memory_space=pltpu.SMEM)] + vmem(8),
+        in_specs=vmem(9),
         out_specs=tuple(vmem(4)),
         scratch_shapes=[
             pltpu.VMEM((levels,) + first_shape[1:], jnp.float32),
             pltpu.VMEM(packed.shape, jnp.float32),
             pltpu.VMEM(packed.shape, jnp.float32),
+            pltpu.SMEM(level_map.shape, jnp.int32),
+            pltpu.SemaphoreType.DMA(()),
         ],
         compiler_params=params(8),
         name="window",

time: 38 us -> 38 us (level)
  no operation moved by 1% of the time
where the time goes in v7:
time: 38 us; the launch traced here: 37.6 us
  starting transfers between devices  19.5 us (51%)
  waiting for transfers between devices  11.5 us (30%)
  Pallas kernels  5.78 us (15%)
  between operations  0.79 us (2%)
    all_to_all x2, starting transfers between devices, swapped(): lax.all_to_all(pieces, 'tile', split_axis=0, concat_axis=0, tiled=True, a...  14.3 us
    ppermute x2, waiting for transfers between devices, exchanged_pairs(): lax.ppermute(outer, 'tile', both[1])  8.04 us
    ppermute x2, starting transfers between devices, exchanged_pairs(): lax.ppermute(outer, 'tile', both[1])  4.34 us
    all_to_all x2, waiting for transfers between devices, swapped(): lax.all_to_all(pieces, 'tile', split_axis=0, concat_axis=0, tiled=True, a...  3.46 us
    pallas_call x1, Pallas kernels, whole_local(): pl.pallas_call(lambda *refs: member_sum_kernel(tiles, *refs), out_shape=a...  2.29 us
    pallas_call x1, Pallas kernels, whole_local(): pl.pallas_call(window_kernel, out_shape=(array(tiles, halves * rows + -(-...  2.29 us
    pallas_call x1, Pallas kernels, whole_local(): pl.pallas_call(member_update_kernel, out_shape=(array(*ens_control.shape)...  1.08 us
    ppermute x2, starting transfers between devices, exchanged_pairs(): lax.ppermute(inner, 'tile', both[0])  0.86 us
  transfers between devices with their start and end apart: 6, of which 4 were waited for; matrix products, arithmetic and copies ran while one was open for 0% of the time, Pallas kernels for 0%

profile of v7, /device:TPU:1, one launch (start us, length us, event | category | flops | bytes accessed | tf_op | source)
XLA Modules:
  0.0 37.6 jit_solution(3393511337933732427)
XLA Ops:
  0.6 0.0 copy-start.1
  0.6 0.0 copy-start.2
  0.6 2.3 %member_sum.1 = f32[16,48,128]{2,1,0:T(8,128)} custom-call(bf16[256,256]{1,0:T(8,128)(2,1)} %lat_ref.1, bf16[256,256]{1,0:T(8,128)(2,1)} %lon_ref.1, bf16[1,256,256]{2,1,0:T(8,128)(2,1)} %perts_ref.1, f32[1,256,256]{2,1,0:T(8,128)} %control_ref.5), custom_call_target="tpu_custom_call" | custom-call | tf_op jit(solution)/shard_map/member_sum/pallas_call | solution.py:337
  2.9 0.0 copy-start
  2.9 0.0 copy-start.3
  2.9 0.0 copy-start.4
  3.0 7.6 %all-to-all-start = ((f32[16,48,128]{2,1,0:T(8,128)}), f32[16,48,128]{2,1,0:T(8,128)S(1)}, u32[]{:S(2)}, u32[]{:S(2)}) async-start(f32[16,48,128]{2,1,0:T(8,128)} %member_sum.1), calls=%async_computation | async-start | bytes 786432 | tf_op jit(solution)/shard_map/all_to_all | solution.py:328
  10.5 0.0 copy-done.1
  10.5 0.0 copy-done.2
  10.5 0.0 copy-done
  10.5 0.0 copy-done.3
  10.6 0.0 copy-done.4
  10.6 0.1 pack.1
  10.7 0.0 copy-start.9
  10.7 0.5 %collective-permute-start = (f32[2,72,256]{2,1,0:T(8,128)S(1)}, f32[2,72,256]{2,1,0:T(8,128)S(1)}, u32[]{:S(2)}, u32[]{:S(2)}) collective-permute-start(f32[2,72,256]{2,1,0:T(8,128)S(1)} %get-tuple-element.8), channel_id=1, source_target_pairs={{0,1},{2,3},{4,5},{6,7},{8,9},{10,11},{12,13},{14,15},{1,0},{3,2},... | collective-permute-start | bytes 442376 | tf_op jit(solution)/shard_map/ppermute | solution.py:325
  11.2 2.2 %collective-permute-start.1 = (f32[2,72,256]{2,1,0:T(8,128)S(1)}, f32[2,72,256]{2,1,0:T(8,128)S(1)}, u32[]{:S(2)}, u32[]{:S(2)}) collective-permute-start(f32[2,72,256]{2,1,0:T(8,128)S(1)} %get-tuple-element.9), channel_id=1, source_target_pairs={{1,2},{3,4},{5,6},{7,8},{9,10},{11,12},{13,14},{2,1},{4,3},{6,5},{... | collective-permute-start | bytes 442376 | tf_op jit(solution)/shard_map/ppermute | solution.py:325
  13.3 0.0 collective-permute-done.inner_ref
  13.3 4.9 %collective-permute-done.1.outer_ref = f32[2,72,256]{2,1,0:T(8,128)S(1)} collective-permute-done((f32[2,72,256]{2,1,0:T(8,128)S(1)}, f32[2,72,256]{2,1,0:T(8,128)S(1)}, u32[]{:S(2)}, u32[]{:S(2)}) %collective-permute-start.1) | collective-permute-done | bytes 147488 | tf_op jit(solution)/shard_map/ppermute | solution.py:325
  18.2 1.4 %all-to-all-done.received_ref = f32[16,48,128]{2,1,0:T(8,128)S(1)} async-done(((f32[16,48,128]{2,1,0:T(8,128)}), f32[16,48,128]{2,1,0:T(8,128)S(1)}, u32[]{:S(2)}, u32[]{:S(2)}) %all-to-all-start) | async-done | bytes 393248 | tf_op jit(solution)/shard_map/all_to_all | solution.py:328
  19.6 0.0 copy-done.9
  19.6 2.3 %window.1 = (f32[16,40,128]{2,1,0:T(8,128)}, f32[8,24,256]{2,1,0:T(8,128)S(1)}, f32[2,8,256]{2,1,0:T(8,128)S(1)}, f32[2,8,256]{2,1,0:T(8,128)S(1)}) custom-call(s32[16]{0:T(128)S(1)} %copy-done.9, f32[16,48,128]{2,1,0:T(8,128)S(1)} %all-to-all-done.received_ref, f32[2,72,256]{2,1,0:T(8,128)S(1)} %collective-permute-done.inner_ref, ...), custom_call_target="tpu_custom_call" | custom-call | tf_op jit(solution)/shard_map/window/pallas_call | solution.py:358
  21.9 0.0 copy-start.5
  22.0 0.0 copy-start.6
  22.0 0.0 copy-start.7
  22.0 0.0 copy-start.8
  22.0 6.7 %all-to-all-start.1 = ((f32[16,40,128]{2,1,0:T(8,128)}), f32[16,40,128]{2,1,0:T(8,128)S(1)}, u32[]{:S(2)}, u32[]{:S(2)}) async-start(f32[16,40,128]{2,1,0:T(8,128)} %get-tuple-element.10), calls=%async_computation.1 | async-start | bytes 655360 | tf_op jit(solution)/shard_map/all_to_all | solution.py:328
  28.7 0.4 %collective-permute-start.2 = (f32[2,8,256]{2,1,0:T(8,128)S(1)}, f32[2,8,256]{2,1,0:T(8,128)S(1)}, u32[]{:S(2)}, u32[]{:S(2)}) collective-permute-start(f32[2,8,256]{2,1,0:T(8,128)S(1)} %get-tuple-element.11), channel_id=1, source_target_pairs={{0,1},{2,3},{4,5},{6,7},{8,9},{10,11},{12,13},{14,15},{1,0},{3,2},... | collective-permute-start | bytes 49160 | tf_op jit(solution)/shard_map/ppermute | solution.py:325
  29.1 2.2 %collective-permute-start.3 = (f32[2,8,256]{2,1,0:T(8,128)S(1)}, f32[2,8,256]{2,1,0:T(8,128)S(1)}, u32[]{:S(2)}, u32[]{:S(2)}) collective-permute-start(f32[2,8,256]{2,1,0:T(8,128)S(1)} %get-tuple-element.12), channel_id=1, source_target_pairs={{1,2},{3,4},{5,6},{7,8},{9,10},{11,12},{13,14},{2,1},{4,3},{6,5},{... | collective-permute-start | bytes 49160 | tf_op jit(solution)/shard_map/ppermute | solution.py:325
  31.3 0.0 collective-permute-done.2.inner_ref
  31.3 3.1 %collective-permute-done.3.outer_ref = f32[2,8,256]{2,1,0:T(8,128)S(1)} collective-permute-done((f32[2,8,256]{2,1,0:T(8,128)S(1)}, f32[2,8,256]{2,1,0:T(8,128)S(1)}, u32[]{:S(2)}, u32[]{:S(2)}) %collective-permute-start.3) | collective-permute-done | bytes 16416 | tf_op jit(solution)/shard_map/ppermute | solution.py:325
  34.4 2.1 %all-to-all-done.1.incoming_ref = f32[16,40,128]{2,1,0:T(8,128)S(1)} async-done(((f32[16,40,128]{2,1,0:T(8,128)}), f32[16,40,128]{2,1,0:T(8,128)S(1)}, u32[]{:S(2)}, u32[]{:S(2)}) %all-to-all-start.1) | async-done | bytes 327712 | tf_op jit(solution)/shard_map/all_to_all | solution.py:328
  36.5 0.0 copy-done.5
  36.5 0.0 copy-done.6
  36.5 0.0 copy-done.7
  36.5 0.0 copy-done.8
  36.5 1.1 %member_update.1 = (f32[1,256,256]{2,1,0:T(8,128)}, f32[8,16,256]{2,1,0:T(8,128)}) custom-call(bf16[256,256]{1,0:T(8,128)(2,1)S(1)} %copy-done.6, bf16[256,256]{1,0:T(8,128)(2,1)S(1)} %copy-done.7, bf16[1,256,256]{2,1,0:T(8,128)(2,1)S(1)} %copy-done.8, f32[16,40,128]{2,1,0:T(8,128)S(1)} %all-to-all-done.1.incoming_ref, f32[1,256,256]{2,1,0:T(8,128)S(1)} %copy-done.5, ...), custom_call_target="tpu_custom_call" | custom-call | tf_op jit(solution)/shard_map/member_update/pallas_call | solution.py:381
Async XLA Ops:
  0.6 9.9 %copy-start.1 = (f32[3,8,16,256]{3,2,1,0:T(8,128)S(1)}, f32[3,8,16,256]{3,2,1,0:T(8,128)}, u32[]{:S(2)}) copy-start(f32[3,8,16,256]{3,2,1,0:T(8,128)} %weight_ref.3) | copy-start | bytes 1179652
  0.6 9.9 %copy-start.2 = (f32[3,8,16,256]{3,2,1,0:T(8,128)S(1)}, f32[3,8,16,256]{3,2,1,0:T(8,128)}, u32[]{:S(2)}) copy-start(f32[3,8,16,256]{3,2,1,0:T(8,128)} %innov_ref.3) | copy-start | bytes 1179652
  2.9 7.6 %copy-start = (f32[4,8,16,256]{3,2,1,0:T(8,128)S(1)}, f32[4,8,16,256]{3,2,1,0:T(8,128)}, u32[]{:S(2)}) copy-start(f32[4,8,16,256]{3,2,1,0:T(8,128)} %coefs_ref.3) | copy-start | bytes 1572868
  2.9 7.6 %copy-start.3 = (f32[8,16,256]{2,1,0:T(8,128)S(1)}, f32[8,16,256]{2,1,0:T(8,128)}, u32[]{:S(2)}) copy-start(f32[8,16,256]{2,1,0:T(8,128)} %static_ref.1) | copy-start | bytes 393220
  2.9 7.6 %copy-start.4 = (f32[8,16,256]{2,1,0:T(8,128)S(1)}, f32[8,16,256]{2,1,0:T(8,128)}, u32[]{:S(2)}) copy-start(f32[8,16,256]{2,1,0:T(8,128)} %scale_ref.5) | copy-start | bytes 393220
  3.0 16.7 %all-to-all-start = ((f32[16,48,128]{2,1,0:T(8,128)}), f32[16,48,128]{2,1,0:T(8,128)S(1)}, u32[]{:S(2)}, u32[]{:S(2)}) async-start(f32[16,48,128]{2,1,0:T(8,128)} %member_sum.1), calls=%async_computation | async-start | bytes 786432 | tf_op jit(solution)/shard_map/all_to_all | solution.py:328
  10.7 9.0 %copy-start.9 = (s32[16]{0:T(128)S(1)}, s32[16]{0:T(128)}, u32[]{:S(2)}) copy-start(s32[16]{0:T(128)} %level_ref.1) | copy-start | bytes 196
  10.7 2.6 %collective-permute-start = (f32[2,72,256]{2,1,0:T(8,128)S(1)}, f32[2,72,256]{2,1,0:T(8,128)S(1)}, u32[]{:S(2)}, u32[]{:S(2)}) collective-permute-start(f32[2,72,256]{2,1,0:T(8,128)S(1)} %get-tuple-element.8), channel_id=1, source_target_pairs={{0,1},{2,3},{4,5},{6,7},{8,9},{10,11},{12,13},{14,15},{1,0},{3,2},... | collective-permute-start | bytes 442376 | tf_op jit(solution)/shard_map/ppermute | solution.py:325
  11.2 7.1 %collective-permute-start.1 = (f32[2,72,256]{2,1,0:T(8,128)S(1)}, f32[2,72,256]{2,1,0:T(8,128)S(1)}, u32[]{:S(2)}, u32[]{:S(2)}) collective-permute-start(f32[2,72,256]{2,1,0:T(8,128)S(1)} %get-tuple-element.9), channel_id=1, source_target_pairs={{1,2},{3,4},{5,6},{7,8},{9,10},{11,12},{13,14},{2,1},{4,3},{6,5},{... | collective-permute-start | bytes 442376 | tf_op jit(solution)/shard_map/ppermute | solution.py:325
  21.9 14.6 %copy-start.5 = (f32[1,256,256]{2,1,0:T(8,128)S(1)}, f32[1,256,256]{2,1,0:T(8,128)}, u32[]{:S(2)}) copy-start(f32[1,256,256]{2,1,0:T(8,128)} %control_ref.5) | copy-start | bytes 786436
  22.0 14.5 %copy-start.6 = (bf16[256,256]{1,0:T(8,128)(2,1)S(1)}, bf16[256,256]{1,0:T(8,128)(2,1)}, u32[]{:S(2)}) copy-start(bf16[256,256]{1,0:T(8,128)(2,1)} %lat_ref.1) | copy-start | bytes 393220
  22.0 14.5 %copy-start.7 = (bf16[256,256]{1,0:T(8,128)(2,1)S(1)}, bf16[256,256]{1,0:T(8,128)(2,1)}, u32[]{:S(2)}) copy-start(bf16[256,256]{1,0:T(8,128)(2,1)} %lon_ref.1) | copy-start | bytes 393220
  22.0 14.5 %copy-start.8 = (bf16[1,256,256]{2,1,0:T(8,128)(2,1)S(1)}, bf16[1,256,256]{2,1,0:T(8,128)(2,1)}, u32[]{:S(2)}) copy-start(bf16[1,256,256]{2,1,0:T(8,128)(2,1)} %perts_ref.1) | copy-start | bytes 393220
  22.0 14.5 %all-to-all-start.1 = ((f32[16,40,128]{2,1,0:T(8,128)}), f32[16,40,128]{2,1,0:T(8,128)S(1)}, u32[]{:S(2)}, u32[]{:S(2)}) async-start(f32[16,40,128]{2,1,0:T(8,128)} %get-tuple-element.10), calls=%async_computation.1 | async-start | bytes 655360 | tf_op jit(solution)/shard_map/all_to_all | solution.py:328
  28.7 2.6 %collective-permute-start.2 = (f32[2,8,256]{2,1,0:T(8,128)S(1)}, f32[2,8,256]{2,1,0:T(8,128)S(1)}, u32[]{:S(2)}, u32[]{:S(2)}) collective-permute-start(f32[2,8,256]{2,1,0:T(8,128)S(1)} %get-tuple-element.11), channel_id=1, source_target_pairs={{0,1},{2,3},{4,5},{6,7},{8,9},{10,11},{12,13},{14,15},{1,0},{3,2},... | collective-permute-start | bytes 49160 | tf_op jit(solution)/shard_map/ppermute | solution.py:325
  29.1 5.3 %collective-permute-start.3 = (f32[2,8,256]{2,1,0:T(8,128)S(1)}, f32[2,8,256]{2,1,0:T(8,128)S(1)}, u32[]{:S(2)}, u32[]{:S(2)}) collective-permute-start(f32[2,8,256]{2,1,0:T(8,128)S(1)} %get-tuple-element.12), channel_id=1, source_target_pairs={{1,2},{3,4},{5,6},{7,8},{9,10},{11,12},{13,14},{2,1},{4,3},{6,5},{... | collective-permute-start | bytes 49160 | tf_op jit(solution)/shard_map/ppermute | solution.py:325

commit v8 on v6

--- a/solution.py
+++ b/solution.py
@@ -242,13 +242,7 @@
     perts_ref,
     incoming_ref,
     control_ref,
-    inner_ref,
-    outer_ref,
-    tile_grad_ref,
-    static_ref,
-    scale_ref,
     out_ref,
-    static_out_ref,
     field_ref,
 ):
     tiles = incoming_ref.shape[0]
@@ -286,6 +280,11 @@
         control = control_ref[b]
         out_ref[b] = control - STEP_SIZE * (control + member_grad)
 
+
+def static_update_kernel(
+    inner_ref, outer_ref, tile_grad_ref, static_ref, scale_ref, static_out_ref
+):
+    rows, nlon = static_ref.shape[1:]
     row = sublane((SUB, nlon))
     even = lax.axis_index("tile") % 2 == 0
     for l in range(static_ref.shape[0]):
@@ -371,18 +370,24 @@
     incoming = swapped(send)
     inner, outer = exchanged_pairs(inner, outer)
 
-    return pl.pallas_call(
+    static_final = pl.pallas_call(
+        static_update_kernel,
+        out_shape=array(*static_control.shape),
+        in_specs=vmem(5),
+        out_specs=vmem(1)[0],
+        compiler_params=params(8),
+        name="static_update",
+    )(inner, outer, tile_grad, static_control, static_scale)
+    ens_final = pl.pallas_call(
         member_update_kernel,
-        out_shape=(array(*ens_control.shape), array(*static_control.shape)),
-        in_specs=vmem(10),
-        out_specs=tuple(vmem(2)),
+        out_shape=array(*ens_control.shape),
+        in_specs=vmem(5),
+        out_specs=vmem(1)[0],
         scratch_shapes=[pltpu.VMEM(ens_control.shape[1:], jnp.float32)],
         compiler_params=params(8),
         name="member_update",
-    )(
-        loc_lat, loc_lon, ens_perts, incoming, ens_control,
-        inner, outer, tile_grad, static_control, static_scale,
-    )
+    )(loc_lat, loc_lon, ens_perts, incoming, ens_control)
+    return ens_final, static_final
 
 
 def exchanged(block, axis):

time: 38 us -> 38 us (level)
  waiting for transfers between devices: 11.5 us -> 10.8 us
  Pallas kernels: 5.83 us -> 6.51 us
    all_to_all x2, waiting for transfers between devices: 3.46 us -> 2.75 us  [swapped(): lax.all_to_all(pieces, 'tile', split_axis=0, concat_axis=0, tiled=True, a...]
    pallas_call x1 -> x2, Pallas kernels: 1.08 us -> 1.76 us  [the longest x1 1.06 us: whole_local(): pl.pallas_call(member_update_kernel, out_shape=array(*ens_control.shape),...]
  transfers between devices with their start and end apart: 6 -> 6, of which waited for: 4 -> 4; matrix products, arithmetic and copies ran while one was open for 0% -> 0% of each run, Pallas kernels for 0% -> 2%
where the time goes in v8:
time: 38 us; the launch traced here: 37.6 us
  starting transfers between devices  19.5 us (51%)
  waiting for transfers between devices  10.8 us (28%)
  Pallas kernels  6.51 us (17%)
  between operations  0.75 us (2%)
    all_to_all x2, starting transfers between devices, swapped(): lax.all_to_all(pieces, 'tile', split_axis=0, concat_axis=0, tiled=True, a...  14.3 us
    ppermute x2, waiting for transfers between devices, exchanged_pairs(): lax.ppermute(outer, 'tile', both[1])  8.04 us
    ppermute x2, starting transfers between devices, exchanged_pairs(): lax.ppermute(outer, 'tile', both[1])  4.34 us
    all_to_all x2, waiting for transfers between devices, swapped(): lax.all_to_all(pieces, 'tile', split_axis=0, concat_axis=0, tiled=True, a...  2.75 us
    pallas_call x1, Pallas kernels, whole_local(): pl.pallas_call(window_kernel, out_shape=(array(tiles, halves * rows + -(-...  2.34 us
    pallas_call x1, Pallas kernels, whole_local(): pl.pallas_call(lambda *refs: member_sum_kernel(tiles, *refs), out_shape=a...  2.29 us
    pallas_call x1, Pallas kernels, whole_local(): pl.pallas_call(member_update_kernel, out_shape=array(*ens_control.shape),...  1.06 us
    ppermute x2, starting transfers between devices, exchanged_pairs(): lax.ppermute(inner, 'tile', both[0])  0.86 us
  transfers between devices with their start and end apart: 6, of which 4 were waited for; matrix products, arithmetic and copies ran while one was open for 0% of the time, Pallas kernels for 2%

profile of v8, /device:TPU:1, one launch (start us, length us, event | category | flops | bytes accessed | tf_op | source)
XLA Modules:
  0.0 37.6 jit_solution(2413218133159752931)
XLA Ops:
  0.6 0.0 copy-start.1
  0.6 0.0 copy-start.2
  0.6 2.3 %member_sum.1 = f32[16,48,128]{2,1,0:T(8,128)} custom-call(bf16[256,256]{1,0:T(8,128)(2,1)} %lat_ref.1, bf16[256,256]{1,0:T(8,128)(2,1)} %lon_ref.1, bf16[1,256,256]{2,1,0:T(8,128)(2,1)} %perts_ref.1, f32[1,256,256]{2,1,0:T(8,128)} %control_ref.5), custom_call_target="tpu_custom_call" | custom-call | tf_op jit(solution)/shard_map/member_sum/pallas_call | solution.py:331
  2.9 0.0 copy-start
  2.9 0.0 copy-start.3
  2.9 0.0 copy-start.4
  3.0 7.6 %all-to-all-start = ((f32[16,48,128]{2,1,0:T(8,128)}), f32[16,48,128]{2,1,0:T(8,128)S(1)}, u32[]{:S(2)}, u32[]{:S(2)}) async-start(f32[16,48,128]{2,1,0:T(8,128)} %member_sum.1), calls=%async_computation | async-start | bytes 786432 | tf_op jit(solution)/shard_map/all_to_all | solution.py:322
  10.5 0.0 copy-done.1
  10.5 0.0 copy-done.2
  10.5 0.0 copy-done
  10.5 0.0 copy-done.3
  10.6 0.0 copy-done.4
  10.6 0.1 pack.1
  10.7 0.0 copy-start.9
  10.7 0.5 %collective-permute-start = (f32[2,72,256]{2,1,0:T(8,128)S(1)}, f32[2,72,256]{2,1,0:T(8,128)S(1)}, u32[]{:S(2)}, u32[]{:S(2)}) collective-permute-start(f32[2,72,256]{2,1,0:T(8,128)S(1)} %get-tuple-element.8), channel_id=1, source_target_pairs={{0,1},{2,3},{4,5},{6,7},{8,9},{10,11},{12,13},{14,15},{1,0},{3,2},... | collective-permute-start | bytes 442376 | tf_op jit(solution)/shard_map/ppermute | solution.py:319
  11.2 2.2 %collective-permute-start.1 = (f32[2,72,256]{2,1,0:T(8,128)S(1)}, f32[2,72,256]{2,1,0:T(8,128)S(1)}, u32[]{:S(2)}, u32[]{:S(2)}) collective-permute-start(f32[2,72,256]{2,1,0:T(8,128)S(1)} %get-tuple-element.9), channel_id=1, source_target_pairs={{1,2},{3,4},{5,6},{7,8},{9,10},{11,12},{13,14},{2,1},{4,3},{6,5},{... | collective-permute-start | bytes 442376 | tf_op jit(solution)/shard_map/ppermute | solution.py:319
  13.3 0.0 collective-permute-done.inner_ref
  13.3 4.9 %collective-permute-done.1.outer_ref = f32[2,72,256]{2,1,0:T(8,128)S(1)} collective-permute-done((f32[2,72,256]{2,1,0:T(8,128)S(1)}, f32[2,72,256]{2,1,0:T(8,128)S(1)}, u32[]{:S(2)}, u32[]{:S(2)}) %collective-permute-start.1) | collective-permute-done | bytes 147488 | tf_op jit(solution)/shard_map/ppermute | solution.py:319
  18.2 1.4 %all-to-all-done.received_ref = f32[16,48,128]{2,1,0:T(8,128)S(1)} async-done(((f32[16,48,128]{2,1,0:T(8,128)}), f32[16,48,128]{2,1,0:T(8,128)S(1)}, u32[]{:S(2)}, u32[]{:S(2)}) %all-to-all-start) | async-done | bytes 393248 | tf_op jit(solution)/shard_map/all_to_all | solution.py:322
  19.6 0.0 copy-done.9
  19.6 2.3 %window.1 = (f32[16,40,128]{2,1,0:T(8,128)}, f32[8,24,256]{2,1,0:T(8,128)S(1)}, f32[2,8,256]{2,1,0:T(8,128)S(1)}, f32[2,8,256]{2,1,0:T(8,128)S(1)}) custom-call(s32[16]{0:T(128)S(1)} %copy-done.9, f32[16,48,128]{2,1,0:T(8,128)S(1)} %all-to-all-done.received_ref, f32[2,72,256]{2,1,0:T(8,128)S(1)} %collective-permute-done.inner_ref, ...), custom_call_target="tpu_custom_call" | custom-call | tf_op jit(solution)/shard_map/window/pallas_call | solution.py:352
  22.0 0.0 copy-start.8
  22.0 6.7 %all-to-all-start.1 = ((f32[16,40,128]{2,1,0:T(8,128)}), f32[16,40,128]{2,1,0:T(8,128)S(1)}, u32[]{:S(2)}, u32[]{:S(2)}) async-start(f32[16,40,128]{2,1,0:T(8,128)} %get-tuple-element.10), calls=%async_computation.1 | async-start | bytes 655360 | tf_op jit(solution)/shard_map/all_to_all | solution.py:322
  28.7 0.4 %collective-permute-start.2 = (f32[2,8,256]{2,1,0:T(8,128)S(1)}, f32[2,8,256]{2,1,0:T(8,128)S(1)}, u32[]{:S(2)}, u32[]{:S(2)}) collective-permute-start(f32[2,8,256]{2,1,0:T(8,128)S(1)} %get-tuple-element.11), channel_id=1, source_target_pairs={{0,1},{2,3},{4,5},{6,7},{8,9},{10,11},{12,13},{14,15},{1,0},{3,2},... | collective-permute-start | bytes 49160 | tf_op jit(solution)/shard_map/ppermute | solution.py:319
  29.1 2.2 %collective-permute-start.3 = (f32[2,8,256]{2,1,0:T(8,128)S(1)}, f32[2,8,256]{2,1,0:T(8,128)S(1)}, u32[]{:S(2)}, u32[]{:S(2)}) collective-permute-start(f32[2,8,256]{2,1,0:T(8,128)S(1)} %get-tuple-element.12), channel_id=1, source_target_pairs={{1,2},{3,4},{5,6},{7,8},{9,10},{11,12},{13,14},{2,1},{4,3},{6,5},{... | collective-permute-start | bytes 49160 | tf_op jit(solution)/shard_map/ppermute | solution.py:319
  31.3 0.0 collective-permute-done.2.inner_ref
  31.3 3.1 %collective-permute-done.3.outer_ref = f32[2,8,256]{2,1,0:T(8,128)S(1)} collective-permute-done((f32[2,8,256]{2,1,0:T(8,128)S(1)}, f32[2,8,256]{2,1,0:T(8,128)S(1)}, u32[]{:S(2)}, u32[]{:S(2)}) %collective-permute-start.3) | collective-permute-done | bytes 16416 | tf_op jit(solution)/shard_map/ppermute | solution.py:319
  34.4 0.0 copy-start.5
  34.4 0.0 copy-start.6
  34.4 0.0 copy-start.7
  34.4 0.7 %static_update.1 = f32[8,16,256]{2,1,0:T(8,128)} custom-call(f32[2,8,256]{2,1,0:T(8,128)S(1)} %collective-permute-done.2.inner_ref, f32[2,8,256]{2,1,0:T(8,128)S(1)} %collective-permute-done.3.outer_ref, f32[8,24,256]{2,1,0:T(8,128)S(1)} %get-tuple-element.13.tile_grad_ref, f32[8,16,256]{2,1,0:T(8,128)S(1)} %copy-done.3, f32[8,16,256]{2,1,0:T(8,128)S(1)} %copy-done.4), custom_call_target="tpu_custom_call" | custom-call | tf_op jit(solution)/shard_map/static_update/pallas_call | solution.py:373
  35.1 1.4 %all-to-all-done.1.incoming_ref = f32[16,40,128]{2,1,0:T(8,128)S(1)} async-done(((f32[16,40,128]{2,1,0:T(8,128)}), f32[16,40,128]{2,1,0:T(8,128)S(1)}, u32[]{:S(2)}, u32[]{:S(2)}) %all-to-all-start.1) | async-done | bytes 327712 | tf_op jit(solution)/shard_map/all_to_all | solution.py:322
  36.5 0.0 copy-done.8
  36.5 0.0 copy-done.5
  36.5 0.0 copy-done.6
  36.5 0.0 copy-done.7
  36.5 1.1 %member_update.1 = f32[1,256,256]{2,1,0:T(8,128)} custom-call(bf16[256,256]{1,0:T(8,128)(2,1)S(1)} %copy-done.6, bf16[256,256]{1,0:T(8,128)(2,1)S(1)} %copy-done.7, bf16[1,256,256]{2,1,0:T(8,128)(2,1)S(1)} %copy-done.8, f32[16,40,128]{2,1,0:T(8,128)S(1)} %all-to-all-done.1.incoming_ref, f32[1,256,256]{2,1,0:T(8,128)S(1)} %copy-done.5), custom_call_target="tpu_custom_call" | custom-call | tf_op jit(solution)/shard_map/member_update/pallas_call | solution.py:381
Async XLA Ops:
  0.6 9.9 %copy-start.1 = (f32[3,8,16,256]{3,2,1,0:T(8,128)S(1)}, f32[3,8,16,256]{3,2,1,0:T(8,128)}, u32[]{:S(2)}) copy-start(f32[3,8,16,256]{3,2,1,0:T(8,128)} %weight_ref.3) | copy-start | bytes 1179652
  0.6 9.9 %copy-start.2 = (f32[3,8,16,256]{3,2,1,0:T(8,128)S(1)}, f32[3,8,16,256]{3,2,1,0:T(8,128)}, u32[]{:S(2)}) copy-start(f32[3,8,16,256]{3,2,1,0:T(8,128)} %innov_ref.3) | copy-start | bytes 1179652
  2.9 7.6 %copy-start = (f32[4,8,16,256]{3,2,1,0:T(8,128)S(1)}, f32[4,8,16,256]{3,2,1,0:T(8,128)}, u32[]{:S(2)}) copy-start(f32[4,8,16,256]{3,2,1,0:T(8,128)} %coefs_ref.3) | copy-start | bytes 1572868
  2.9 7.6 %copy-start.3 = (f32[8,16,256]{2,1,0:T(8,128)S(1)}, f32[8,16,256]{2,1,0:T(8,128)}, u32[]{:S(2)}) copy-start(f32[8,16,256]{2,1,0:T(8,128)} %static_ref.1) | copy-start | bytes 393220
  2.9 7.6 %copy-start.4 = (f32[8,16,256]{2,1,0:T(8,128)S(1)}, f32[8,16,256]{2,1,0:T(8,128)}, u32[]{:S(2)}) copy-start(f32[8,16,256]{2,1,0:T(8,128)} %scale_ref.5) | copy-start | bytes 393220
  3.0 16.7 %all-to-all-start = ((f32[16,48,128]{2,1,0:T(8,128)}), f32[16,48,128]{2,1,0:T(8,128)S(1)}, u32[]{:S(2)}, u32[]{:S(2)}) async-start(f32[16,48,128]{2,1,0:T(8,128)} %member_sum.1), calls=%async_computation | async-start | bytes 786432 | tf_op jit(solution)/shard_map/all_to_all | solution.py:322
  10.7 9.0 %copy-start.9 = (s32[16]{0:T(128)S(1)}, s32[16]{0:T(128)}, u32[]{:S(2)}) copy-start(s32[16]{0:T(128)} %level_ref.1) | copy-start | bytes 196
  10.7 2.6 %collective-permute-start = (f32[2,72,256]{2,1,0:T(8,128)S(1)}, f32[2,72,256]{2,1,0:T(8,128)S(1)}, u32[]{:S(2)}, u32[]{:S(2)}) collective-permute-start(f32[2,72,256]{2,1,0:T(8,128)S(1)} %get-tuple-element.8), channel_id=1, source_target_pairs={{0,1},{2,3},{4,5},{6,7},{8,9},{10,11},{12,13},{14,15},{1,0},{3,2},... | collective-permute-start | bytes 442376 | tf_op jit(solution)/shard_map/ppermute | solution.py:319
  11.2 7.1 %collective-permute-start.1 = (f32[2,72,256]{2,1,0:T(8,128)S(1)}, f32[2,72,256]{2,1,0:T(8,128)S(1)}, u32[]{:S(2)}, u32[]{:S(2)}) collective-permute-start(f32[2,72,256]{2,1,0:T(8,128)S(1)} %get-tuple-element.9), channel_id=1, source_target_pairs={{1,2},{3,4},{5,6},{7,8},{9,10},{11,12},{13,14},{2,1},{4,3},{6,5},{... | collective-permute-start | bytes 442376 | tf_op jit(solution)/shard_map/ppermute | solution.py:319
  22.0 14.5 %copy-start.8 = (bf16[1,256,256]{2,1,0:T(8,128)(2,1)S(1)}, bf16[1,256,256]{2,1,0:T(8,128)(2,1)}, u32[]{:S(2)}) copy-start(bf16[1,256,256]{2,1,0:T(8,128)(2,1)} %perts_ref.1) | copy-start | bytes 393220
  22.0 14.5 %all-to-all-start.1 = ((f32[16,40,128]{2,1,0:T(8,128)}), f32[16,40,128]{2,1,0:T(8,128)S(1)}, u32[]{:S(2)}, u32[]{:S(2)}) async-start(f32[16,40,128]{2,1,0:T(8,128)} %get-tuple-element.10), calls=%async_computation.1 | async-start | bytes 655360 | tf_op jit(solution)/shard_map/all_to_all | solution.py:322
  28.7 2.6 %collective-permute-start.2 = (f32[2,8,256]{2,1,0:T(8,128)S(1)}, f32[2,8,256]{2,1,0:T(8,128)S(1)}, u32[]{:S(2)}, u32[]{:S(2)}) collective-permute-start(f32[2,8,256]{2,1,0:T(8,128)S(1)} %get-tuple-element.11), channel_id=1, source_target_pairs={{0,1},{2,3},{4,5},{6,7},{8,9},{10,11},{12,13},{14,15},{1,0},{3,2},... | collective-permute-start | bytes 49160 | tf_op jit(solution)/shard_map/ppermute | solution.py:319
  29.1 5.3 %collective-permute-start.3 = (f32[2,8,256]{2,1,0:T(8,128)S(1)}, f32[2,8,256]{2,1,0:T(8,128)S(1)}, u32[]{:S(2)}, u32[]{:S(2)}) collective-permute-start(f32[2,8,256]{2,1,0:T(8,128)S(1)} %get-tuple-element.12), channel_id=1, source_target_pairs={{1,2},{3,4},{5,6},{7,8},{9,10},{11,12},{13,14},{2,1},{4,3},{6,5},{... | collective-permute-start | bytes 49160 | tf_op jit(solution)/shard_map/ppermute | solution.py:319
  34.4 2.1 %copy-start.5 = (f32[1,256,256]{2,1,0:T(8,128)S(1)}, f32[1,256,256]{2,1,0:T(8,128)}, u32[]{:S(2)}) copy-start(f32[1,256,256]{2,1,0:T(8,128)} %control_ref.5) | copy-start | bytes 786436
  34.4 2.1 %copy-start.6 = (bf16[256,256]{1,0:T(8,128)(2,1)S(1)}, bf16[256,256]{1,0:T(8,128)(2,1)}, u32[]{:S(2)}) copy-start(bf16[256,256]{1,0:T(8,128)(2,1)} %lat_ref.1) | copy-start | bytes 393220
  34.4 2.1 %copy-start.7 = (bf16[256,256]{1,0:T(8,128)(2,1)S(1)}, bf16[256,256]{1,0:T(8,128)(2,1)}, u32[]{:S(2)}) copy-start(bf16[256,256]{1,0:T(8,128)(2,1)} %lon_ref.1) | copy-start | bytes 393220

commit v9 on v6

--- a/solution.py
+++ b/solution.py
@@ -44,7 +44,7 @@
     return lax.broadcasted_iota(jnp.int32, shape, 0)
 
 
-def member_sum_kernel(tiles, lat_ref, lon_ref, perts_ref, control_ref, out_ref):
+def member_sum_kernel(tiles, control_ref, lat_ref, lon_ref, perts_ref, out_ref):
     blocks, nlat, nlon = control_ref.shape
     rows = nlat // tiles
     halves = nlon // LANES
@@ -335,7 +335,7 @@
         in_specs=vmem(4),
         out_specs=vmem(1)[0],
         name="member_sum",
-    )(loc_lat, loc_lon, ens_perts, ens_control)
+    )(ens_control, loc_lat, loc_lon, ens_perts)
     received = swapped(pieces)
 
     packed = array(levels // GROUP, PACKED, nlon)

time: 38 us -> 37.9 us (level)
  no operation moved by 1% of the time
where the time goes in v9:
time: 37.9 us; the launch traced here: 37.6 us
  starting transfers between devices  19.5 us (51%)
  waiting for transfers between devices  11.5 us (30%)
  Pallas kernels  5.79 us (15%)
  between operations  0.75 us (2%)
    all_to_all x2, starting transfers between devices, swapped(): lax.all_to_all(pieces, 'tile', split_axis=0, concat_axis=0, tiled=True, a...  14.3 us
    ppermute x2, waiting for transfers between devices, exchanged_pairs(): lax.ppermute(outer, 'tile', both[1])  8.04 us
    ppermute x2, starting transfers between devices, exchanged_pairs(): lax.ppermute(outer, 'tile', both[1])  4.34 us
    all_to_all x2, waiting for transfers between devices, swapped(): lax.all_to_all(pieces, 'tile', split_axis=0, concat_axis=0, tiled=True, a...  3.46 us
    pallas_call x1, Pallas kernels, whole_local(): pl.pallas_call(window_kernel, out_shape=(array(tiles, halves * rows + -(-...  2.34 us
    pallas_call x1, Pallas kernels, whole_local(): pl.pallas_call(lambda *refs: member_sum_kernel(tiles, *refs), out_shape=a...  2.26 us
    pallas_call x1, Pallas kernels, whole_local(): pl.pallas_call(member_update_kernel, out_shape=(array(*ens_control.shape)...  1.08 us
    ppermute x2, starting transfers between devices, exchanged_pairs(): lax.ppermute(inner, 'tile', both[0])  0.86 us
  transfers between devices with their start and end apart: 6, of which 4 were waited for; matrix products, arithmetic and copies ran while one was open for 0% of the time, Pallas kernels for 0%

profile of v9, /device:TPU:1, one launch (start us, length us, event | category | flops | bytes accessed | tf_op | source)
XLA Modules:
  0.0 37.6 jit_solution(2284680445821988042)
XLA Ops:
  0.6 0.0 copy-start.1
  0.6 0.0 copy-start.2
  0.6 2.3 %member_sum.1 = f32[16,48,128]{2,1,0:T(8,128)} custom-call(f32[1,256,256]{2,1,0:T(8,128)} %control_ref.5, bf16[256,256]{1,0:T(8,128)(2,1)} %lat_ref.1, bf16[256,256]{1,0:T(8,128)(2,1)} %lon_ref.1, bf16[1,256,256]{2,1,0:T(8,128)(2,1)} %perts_ref.1), custom_call_target="tpu_custom_call" | custom-call | tf_op jit(solution)/shard_map/member_sum/pallas_call | solution.py:332
  2.9 0.0 copy-start
  2.9 0.0 copy-start.3
  2.9 0.0 copy-start.4
  2.9 7.6 %all-to-all-start = ((f32[16,48,128]{2,1,0:T(8,128)}), f32[16,48,128]{2,1,0:T(8,128)S(1)}, u32[]{:S(2)}, u32[]{:S(2)}) async-start(f32[16,48,128]{2,1,0:T(8,128)} %member_sum.1), calls=%async_computation | async-start | bytes 786432 | tf_op jit(solution)/shard_map/all_to_all | solution.py:323
  10.5 0.0 copy-done.1
  10.5 0.0 copy-done.2
  10.5 0.0 copy-done
  10.5 0.0 copy-done.3
  10.5 0.0 copy-done.4
  10.5 0.1 pack.1
  10.7 0.0 copy-start.9
  10.7 0.5 %collective-permute-start = (f32[2,72,256]{2,1,0:T(8,128)S(1)}, f32[2,72,256]{2,1,0:T(8,128)S(1)}, u32[]{:S(2)}, u32[]{:S(2)}) collective-permute-start(f32[2,72,256]{2,1,0:T(8,128)S(1)} %get-tuple-element.8), channel_id=1, source_target_pairs={{0,1},{2,3},{4,5},{6,7},{8,9},{10,11},{12,13},{14,15},{1,0},{3,2},... | collective-permute-start | bytes 442376 | tf_op jit(solution)/shard_map/ppermute | solution.py:320
  11.1 2.2 %collective-permute-start.1 = (f32[2,72,256]{2,1,0:T(8,128)S(1)}, f32[2,72,256]{2,1,0:T(8,128)S(1)}, u32[]{:S(2)}, u32[]{:S(2)}) collective-permute-start(f32[2,72,256]{2,1,0:T(8,128)S(1)} %get-tuple-element.9), channel_id=1, source_target_pairs={{1,2},{3,4},{5,6},{7,8},{9,10},{11,12},{13,14},{2,1},{4,3},{6,5},{... | collective-permute-start | bytes 442376 | tf_op jit(solution)/shard_map/ppermute | solution.py:320
  13.3 0.0 collective-permute-done.inner_ref
  13.3 4.9 %collective-permute-done.1.outer_ref = f32[2,72,256]{2,1,0:T(8,128)S(1)} collective-permute-done((f32[2,72,256]{2,1,0:T(8,128)S(1)}, f32[2,72,256]{2,1,0:T(8,128)S(1)}, u32[]{:S(2)}, u32[]{:S(2)}) %collective-permute-start.1) | collective-permute-done | bytes 147488 | tf_op jit(solution)/shard_map/ppermute | solution.py:320
  18.2 1.4 %all-to-all-done.received_ref = f32[16,48,128]{2,1,0:T(8,128)S(1)} async-done(((f32[16,48,128]{2,1,0:T(8,128)}), f32[16,48,128]{2,1,0:T(8,128)S(1)}, u32[]{:S(2)}, u32[]{:S(2)}) %all-to-all-start) | async-done | bytes 393248 | tf_op jit(solution)/shard_map/all_to_all | solution.py:323
  19.6 0.0 copy-done.9
  19.6 2.3 %window.1 = (f32[16,40,128]{2,1,0:T(8,128)}, f32[8,24,256]{2,1,0:T(8,128)S(1)}, f32[2,8,256]{2,1,0:T(8,128)S(1)}, f32[2,8,256]{2,1,0:T(8,128)S(1)}) custom-call(s32[16]{0:T(128)S(1)} %copy-done.9, f32[16,48,128]{2,1,0:T(8,128)S(1)} %all-to-all-done.received_ref, f32[2,72,256]{2,1,0:T(8,128)S(1)} %collective-permute-done.inner_ref, ...), custom_call_target="tpu_custom_call" | custom-call | tf_op jit(solution)/shard_map/window/pallas_call | solution.py:353
  22.0 0.0 copy-start.5
  22.0 0.0 copy-start.6
  22.0 0.0 copy-start.7
  22.0 0.0 copy-start.8
  22.0 6.7 %all-to-all-start.1 = ((f32[16,40,128]{2,1,0:T(8,128)}), f32[16,40,128]{2,1,0:T(8,128)S(1)}, u32[]{:S(2)}, u32[]{:S(2)}) async-start(f32[16,40,128]{2,1,0:T(8,128)} %get-tuple-element.10), calls=%async_computation.1 | async-start | bytes 655360 | tf_op jit(solution)/shard_map/all_to_all | solution.py:323
  28.7 0.4 %collective-permute-start.2 = (f32[2,8,256]{2,1,0:T(8,128)S(1)}, f32[2,8,256]{2,1,0:T(8,128)S(1)}, u32[]{:S(2)}, u32[]{:S(2)}) collective-permute-start(f32[2,8,256]{2,1,0:T(8,128)S(1)} %get-tuple-element.11), channel_id=1, source_target_pairs={{0,1},{2,3},{4,5},{6,7},{8,9},{10,11},{12,13},{14,15},{1,0},{3,2},... | collective-permute-start | bytes 49160 | tf_op jit(solution)/shard_map/ppermute | solution.py:320
  29.1 2.2 %collective-permute-start.3 = (f32[2,8,256]{2,1,0:T(8,128)S(1)}, f32[2,8,256]{2,1,0:T(8,128)S(1)}, u32[]{:S(2)}, u32[]{:S(2)}) collective-permute-start(f32[2,8,256]{2,1,0:T(8,128)S(1)} %get-tuple-element.12), channel_id=1, source_target_pairs={{1,2},{3,4},{5,6},{7,8},{9,10},{11,12},{13,14},{2,1},{4,3},{6,5},{... | collective-permute-start | bytes 49160 | tf_op jit(solution)/shard_map/ppermute | solution.py:320
  31.3 0.0 collective-permute-done.2.inner_ref
  31.3 3.1 %collective-permute-done.3.outer_ref = f32[2,8,256]{2,1,0:T(8,128)S(1)} collective-permute-done((f32[2,8,256]{2,1,0:T(8,128)S(1)}, f32[2,8,256]{2,1,0:T(8,128)S(1)}, u32[]{:S(2)}, u32[]{:S(2)}) %collective-permute-start.3) | collective-permute-done | bytes 16416 | tf_op jit(solution)/shard_map/ppermute | solution.py:320
  34.4 2.1 %all-to-all-done.1.incoming_ref = f32[16,40,128]{2,1,0:T(8,128)S(1)} async-done(((f32[16,40,128]{2,1,0:T(8,128)}), f32[16,40,128]{2,1,0:T(8,128)S(1)}, u32[]{:S(2)}, u32[]{:S(2)}) %all-to-all-start.1) | async-done | bytes 327712 | tf_op jit(solution)/shard_map/all_to_all | solution.py:323
  36.5 0.0 copy-done.5
  36.5 0.0 copy-done.6
  36.5 0.0 copy-done.7
  36.5 0.0 copy-done.8
  36.5 1.1 %member_update.1 = (f32[1,256,256]{2,1,0:T(8,128)}, f32[8,16,256]{2,1,0:T(8,128)}) custom-call(bf16[256,256]{1,0:T(8,128)(2,1)S(1)} %copy-done.6, bf16[256,256]{1,0:T(8,128)(2,1)S(1)} %copy-done.7, bf16[1,256,256]{2,1,0:T(8,128)(2,1)S(1)} %copy-done.8, f32[16,40,128]{2,1,0:T(8,128)S(1)} %all-to-all-done.1.incoming_ref, f32[1,256,256]{2,1,0:T(8,128)S(1)} %copy-done.5, ...), custom_call_target="tpu_custom_call" | custom-call | tf_op jit(solution)/shard_map/member_update/pallas_call | solution.py:374
Async XLA Ops:
  0.6 9.9 %copy-start.1 = (f32[3,8,16,256]{3,2,1,0:T(8,128)S(1)}, f32[3,8,16,256]{3,2,1,0:T(8,128)}, u32[]{:S(2)}) copy-start(f32[3,8,16,256]{3,2,1,0:T(8,128)} %weight_ref.3) | copy-start | bytes 1179652
  0.6 9.9 %copy-start.2 = (f32[3,8,16,256]{3,2,1,0:T(8,128)S(1)}, f32[3,8,16,256]{3,2,1,0:T(8,128)}, u32[]{:S(2)}) copy-start(f32[3,8,16,256]{3,2,1,0:T(8,128)} %innov_ref.3) | copy-start | bytes 1179652
  2.9 7.6 %copy-start = (f32[4,8,16,256]{3,2,1,0:T(8,128)S(1)}, f32[4,8,16,256]{3,2,1,0:T(8,128)}, u32[]{:S(2)}) copy-start(f32[4,8,16,256]{3,2,1,0:T(8,128)} %coefs_ref.3) | copy-start | bytes 1572868
  2.9 7.6 %copy-start.3 = (f32[8,16,256]{2,1,0:T(8,128)S(1)}, f32[8,16,256]{2,1,0:T(8,128)}, u32[]{:S(2)}) copy-start(f32[8,16,256]{2,1,0:T(8,128)} %static_ref.1) | copy-start | bytes 393220
  2.9 7.6 %copy-start.4 = (f32[8,16,256]{2,1,0:T(8,128)S(1)}, f32[8,16,256]{2,1,0:T(8,128)}, u32[]{:S(2)}) copy-start(f32[8,16,256]{2,1,0:T(8,128)} %scale_ref.5) | copy-start | bytes 393220
  2.9 16.7 %all-to-all-start = ((f32[16,48,128]{2,1,0:T(8,128)}), f32[16,48,128]{2,1,0:T(8,128)S(1)}, u32[]{:S(2)}, u32[]{:S(2)}) async-start(f32[16,48,128]{2,1,0:T(8,128)} %member_sum.1), calls=%async_computation | async-start | bytes 786432 | tf_op jit(solution)/shard_map/all_to_all | solution.py:323
  10.7 9.0 %copy-start.9 = (s32[16]{0:T(128)S(1)}, s32[16]{0:T(128)}, u32[]{:S(2)}) copy-start(s32[16]{0:T(128)} %level_ref.1) | copy-start | bytes 196
  10.7 2.6 %collective-permute-start = (f32[2,72,256]{2,1,0:T(8,128)S(1)}, f32[2,72,256]{2,1,0:T(8,128)S(1)}, u32[]{:S(2)}, u32[]{:S(2)}) collective-permute-start(f32[2,72,256]{2,1,0:T(8,128)S(1)} %get-tuple-element.8), channel_id=1, source_target_pairs={{0,1},{2,3},{4,5},{6,7},{8,9},{10,11},{12,13},{14,15},{1,0},{3,2},... | collective-permute-start | bytes 442376 | tf_op jit(solution)/shard_map/ppermute | solution.py:320
  11.1 7.1 %collective-permute-start.1 = (f32[2,72,256]{2,1,0:T(8,128)S(1)}, f32[2,72,256]{2,1,0:T(8,128)S(1)}, u32[]{:S(2)}, u32[]{:S(2)}) collective-permute-start(f32[2,72,256]{2,1,0:T(8,128)S(1)} %get-tuple-element.9), channel_id=1, source_target_pairs={{1,2},{3,4},{5,6},{7,8},{9,10},{11,12},{13,14},{2,1},{4,3},{6,5},{... | collective-permute-start | bytes 442376 | tf_op jit(solution)/shard_map/ppermute | solution.py:320
  22.0 14.5 %copy-start.5 = (f32[1,256,256]{2,1,0:T(8,128)S(1)}, f32[1,256,256]{2,1,0:T(8,128)}, u32[]{:S(2)}) copy-start(f32[1,256,256]{2,1,0:T(8,128)} %control_ref.5) | copy-start | bytes 786436
  22.0 14.5 %copy-start.6 = (bf16[256,256]{1,0:T(8,128)(2,1)S(1)}, bf16[256,256]{1,0:T(8,128)(2,1)}, u32[]{:S(2)}) copy-start(bf16[256,256]{1,0:T(8,128)(2,1)} %lat_ref.1) | copy-start | bytes 393220
  22.0 14.5 %copy-start.7 = (bf16[256,256]{1,0:T(8,128)(2,1)S(1)}, bf16[256,256]{1,0:T(8,128)(2,1)}, u32[]{:S(2)}) copy-start(bf16[256,256]{1,0:T(8,128)(2,1)} %lon_ref.1) | copy-start | bytes 393220
  22.0 14.5 %copy-start.8 = (bf16[1,256,256]{2,1,0:T(8,128)(2,1)S(1)}, bf16[1,256,256]{2,1,0:T(8,128)(2,1)}, u32[]{:S(2)}) copy-start(bf16[1,256,256]{2,1,0:T(8,128)(2,1)} %perts_ref.1) | copy-start | bytes 393220
  22.0 14.5 %all-to-all-start.1 = ((f32[16,40,128]{2,1,0:T(8,128)}), f32[16,40,128]{2,1,0:T(8,128)S(1)}, u32[]{:S(2)}, u32[]{:S(2)}) async-start(f32[16,40,128]{2,1,0:T(8,128)} %get-tuple-element.10), calls=%async_computation.1 | async-start | bytes 655360 | tf_op jit(solution)/shard_map/all_to_all | solution.py:323
  28.7 2.6 %collective-permute-start.2 = (f32[2,8,256]{2,1,0:T(8,128)S(1)}, f32[2,8,256]{2,1,0:T(8,128)S(1)}, u32[]{:S(2)}, u32[]{:S(2)}) collective-permute-start(f32[2,8,256]{2,1,0:T(8,128)S(1)} %get-tuple-element.11), channel_id=1, source_target_pairs={{0,1},{2,3},{4,5},{6,7},{8,9},{10,11},{12,13},{14,15},{1,0},{3,2},... | collective-permute-start | bytes 49160 | tf_op jit(solution)/shard_map/ppermute | solution.py:320
  29.1 5.3 %collective-permute-start.3 = (f32[2,8,256]{2,1,0:T(8,128)S(1)}, f32[2,8,256]{2,1,0:T(8,128)S(1)}, u32[]{:S(2)}, u32[]{:S(2)}) collective-permute-start(f32[2,8,256]{2,1,0:T(8,128)S(1)} %get-tuple-element.12), channel_id=1, source_target_pairs={{1,2},{3,4},{5,6},{7,8},{9,10},{11,12},{13,14},{2,1},{4,3},{6,5},{... | collective-permute-start | bytes 49160 | tf_op jit(solution)/shard_map/ppermute | solution.py:320
